TPU v7x, 32 devices: a whole 2x2x4 slice. The times are simulated.
32 devices in a mesh: fsdp: 2 (over y), ctx: 4 (over x, core), tp: 4 (over z).
Axes of the slice: x: 2, y: 2, z: 4, core: 2. Of those that a mesh axis runs over, the one named last changes fastest.
Arguments:
- tokens: bfloat16 [8, 2048, 1024], P('fsdp', 'ctx'), may hold values from -6 to 6
- segments: int32 [8, 2048], P('fsdp'), may hold values from 0 to 10, as said below
- w_qkv: bfloat16 [3, 1024, 1024], P(None, 'fsdp', 'tp'), may hold values from -0.1875 to 0.1875
- b_qv: bfloat16 [2, 16, 64], P(None, 'tp', 'fsdp'), may hold values from -3 to 3
- w_o: bfloat16 [1024, 1024], P('tp', 'fsdp'), may hold values from -3 to 3
- b_o: bfloat16 [1024], P('fsdp'), may hold values from -3 to 3
- ln1_gain: bfloat16 [1024], P('fsdp'), may hold values from 0.5 to 1.5
- ln1_bias: bfloat16 [1024], P('fsdp'), may hold values from -2 to 2
- w_in: bfloat16 [1024, 4096], P('fsdp', 'tp'), may hold values from -0.1875 to 0.1875
- b_in: bfloat16 [64, 64], P('tp', 'fsdp'), may hold values from -3 to 3
- w_out: bfloat16 [4096, 1024], P('tp', 'fsdp'), may hold values from -0.09375 to 0.09375
- b_out: bfloat16 [1024], P('fsdp'), may hold values from -3 to 3
- ln2_gain: bfloat16 [1024], P('fsdp'), may hold values from 0.5 to 1.5
- ln2_bias: bfloat16 [1024], P('fsdp'), may hold values from -2 to 2
- cotangent: bfloat16 [8, 2048, 1024], P('fsdp', 'ctx'), may hold values from -6 to 6
Outputs:
- output: bfloat16 [8, 2048, 1024], P('fsdp', 'ctx')
- grad_tokens: bfloat16 [8, 2048, 1024], P('fsdp', 'ctx')
- grad_w_qkv: float32 [3, 1024, 1024], P(None, 'fsdp', 'tp')
- grad_b_qv: float32 [2, 16, 64], P(None, 'tp', 'fsdp')
- grad_w_o: float32 [1024, 1024], P('tp', 'fsdp')
- grad_b_o: float32 [1024], P('fsdp')
- grad_ln1_gain: float32 [1024], P('fsdp')
- grad_ln1_bias: float32 [1024], P('fsdp')
- grad_w_in: float32 [1024, 4096], P('fsdp', 'tp')
- grad_b_in: float32 [64, 64], P('tp', 'fsdp')
- grad_w_out: float32 [4096, 1024], P('tp', 'fsdp')
- grad_b_out: float32 [1024], P('fsdp')
- grad_ln2_gain: float32 [1024], P('fsdp')
- grad_ln2_bias: float32 [1024], P('fsdp')
Inputs may be any that keep to these rules, and one draw needn't show every extreme that they name: `segments`: in each sequence the ids start at 0 and rise by one at each document boundary; every document has 200 to 2000 tokens except a sequence's last, which ends with the sequence and may be shorter; one document of the batch has exactly 2000 tokens, and one sequence is made of documents of exactly 200 tokens except its last.
All inputs are finite; a program needn't handle non-finite values.
Results may differ from a plain program's by a relative error of at most 0.02.
Values may be sent and summed in bfloat16 or wider, within the bound.
No kernel may reach another device: no remote copies, remote signals or barrier semaphores. Data moves between devices by JAX's collectives and lax.ppermute only.
A program may use at most 192 MiB of HBM per device.

v0:
```python
import jax
import jax.numpy as jnp
from jax import lax
from jax.sharding import PartitionSpec as P

EPSILON = 1e-12
NEG_LARGE = -1e30
SCALE_QK = 0.125


def layer_norm(values, gain_vec, offset):
    center = values - jnp.mean(values, -1, keepdims=True)
    spread = jnp.mean(center * center, -1, keepdims=True)
    return center * lax.rsqrt(spread + EPSILON) * gain_vec + offset


def gelu_exact(values):
    return 0.5 * values * (1.0 + jax.scipy.special.erf(values * 0.7071067811865476))


def to_heads(blocks, head_size):
    seq_count, row_len, col_count = blocks.shape
    return blocks.reshape(seq_count, row_len, col_count // head_size, head_size).transpose(
        2, 0, 1, 3
    )


def from_heads(blocks):
    head_count, seq_count, row_len, head_size = blocks.shape
    return blocks.transpose(1, 2, 0, 3).reshape(seq_count, row_len, head_count * head_size)


def masked_scores(query_head, key_head, same_doc):
    scores = (
        jnp.einsum("sqd,skd->sqk", query_head, key_head, preferred_element_type=jnp.float32)
        * SCALE_QK
    )
    return jnp.where(same_doc, scores, NEG_LARGE)


def local(
    tokens,
    segments,
    w_qkv,
    b_qv,
    w_o,
    b_o,
    ln1_gain,
    ln1_bias,
    w_in,
    b_in,
    w_out,
    b_out,
    ln2_gain,
    ln2_bias,
    cotangent,
):
    seq_count, local_len, model_width = tokens.shape
    (
        proj_qkv,
        bias_qv,
        proj_attn,
        bias_attn,
        gain_first,
        shift_first,
        proj_in,
        bias_in,
        proj_out,
        bias_out,
        gain_second,
        shift_second,
    ) = (
        lax.all_gather(w_qkv, "fsdp", axis=1, tiled=True),
        lax.all_gather(b_qv, "fsdp", axis=2, tiled=True),
        lax.all_gather(w_o, "fsdp", axis=1, tiled=True),
        lax.all_gather(b_o, "fsdp", axis=0, tiled=True),
        lax.all_gather(ln1_gain, "fsdp", axis=0, tiled=True),
        lax.all_gather(ln1_bias, "fsdp", axis=0, tiled=True),
        lax.all_gather(w_in, "fsdp", axis=0, tiled=True),
        lax.all_gather(b_in, "fsdp", axis=1, tiled=True),
        lax.all_gather(w_out, "fsdp", axis=1, tiled=True),
        lax.all_gather(b_out, "fsdp", axis=0, tiled=True),
        lax.all_gather(ln2_gain, "fsdp", axis=0, tiled=True),
        lax.all_gather(ln2_bias, "fsdp", axis=0, tiled=True),
    )
    local_width = proj_qkv.shape[2]
    head_size = bias_qv.shape[2]
    local_heads = local_width // head_size
    row_count = seq_count * local_len
    inputs = tokens.reshape(row_count, model_width)
    gain_one = gain_first.astype(jnp.float32)
    shift_one = shift_first.astype(jnp.float32)
    gain_two = gain_second.astype(jnp.float32)
    shift_two = shift_second.astype(jnp.float32)

    def finish_sum(partial_rows):
        return lax.psum(partial_rows.astype(jnp.bfloat16), "tp").astype(jnp.float32)

    projected = jnp.einsum("rd,kdc->krc", inputs, proj_qkv, preferred_element_type=jnp.float32)
    query_rows = (projected[0] + bias_qv[0].reshape(-1).astype(jnp.float32)).astype(jnp.bfloat16)
    key_blocks = projected[1].astype(jnp.bfloat16).reshape(seq_count, local_len, local_width)
    value_blocks = (
        (projected[2] + bias_qv[1].reshape(-1).astype(jnp.float32))
        .astype(jnp.bfloat16)
        .reshape(seq_count, local_len, local_width)
    )
    key_all, value_all = (
        lax.all_gather(key_blocks, "ctx", axis=1, tiled=True),
        lax.all_gather(value_blocks, "ctx", axis=1, tiled=True),
    )
    block_start = lax.axis_index("ctx") * local_len
    query_segments = lax.dynamic_slice_in_dim(segments, block_start, local_len, 1)
    same_doc = query_segments[:, :, None] == segments[:, None, :]
    query_heads = to_heads(query_rows.reshape(seq_count, local_len, local_width), head_size)
    key_heads = to_heads(key_all, head_size)
    value_heads = to_heads(value_all, head_size)

    def attend_head(operands):
        query_head, key_head, value_head = operands
        scores = masked_scores(query_head, key_head, same_doc)
        row_max = jnp.max(scores, -1, keepdims=True)
        exp_scores = jnp.exp(scores - row_max)
        denominator = jnp.sum(exp_scores, -1, keepdims=True)
        probs_low = (exp_scores / denominator).astype(jnp.bfloat16)
        mixed_rows = jnp.einsum(
            "sqk,skd->sqd", probs_low, value_head, preferred_element_type=jnp.float32
        )
        return (mixed_rows.astype(jnp.bfloat16), row_max, denominator)

    attended_heads, row_maxes, denominators = lax.map(
        attend_head, (query_heads, key_heads, value_heads)
    )
    attended_rows = from_heads(attended_heads).reshape(row_count, local_width)
    attn_part = jnp.dot(attended_rows, proj_attn, preferred_element_type=jnp.float32)
    attn_rows = finish_sum(attn_part) + bias_attn.astype(jnp.float32)
    first_in = inputs.astype(jnp.float32) + attn_rows
    normed = layer_norm(first_in, gain_one, shift_one)
    normed_low = normed.astype(jnp.bfloat16)
    pre_act = jnp.dot(normed_low, proj_in, preferred_element_type=jnp.float32) + bias_in.reshape(
        -1
    ).astype(jnp.float32)
    act_low = gelu_exact(pre_act).astype(jnp.bfloat16)
    mlp_part = jnp.dot(act_low, proj_out, preferred_element_type=jnp.float32)
    mlp_rows = finish_sum(mlp_part) + bias_out.astype(jnp.float32)
    second_in = normed + mlp_rows
    final_rows = layer_norm(second_in, gain_two, shift_two)
    output = final_rows.astype(jnp.bfloat16).reshape(seq_count, local_len, model_width)
    grad_final = cotangent.reshape(row_count, model_width).astype(jnp.float32)
    unused_second, pull_second = jax.vjp(layer_norm, second_in, gain_two, shift_two)
    grad_second, grad_gain_second, grad_shift_second = pull_second(grad_final)
    grad_mlp = grad_second.astype(jnp.bfloat16)
    grad_bias_out = jnp.sum(grad_mlp, 0, dtype=jnp.float32)
    grad_proj_out = jnp.einsum("rf,rd->fd", act_low, grad_mlp, preferred_element_type=jnp.float32)
    grad_act = jnp.einsum("rd,fd->rf", grad_mlp, proj_out, preferred_element_type=jnp.float32)
    unused_gelu, pull_gelu = jax.vjp(gelu_exact, pre_act)
    grad_pre = pull_gelu(grad_act)[0].astype(jnp.bfloat16)
    grad_bias_in = jnp.sum(grad_pre, 0, dtype=jnp.float32).reshape(bias_in.shape)
    grad_proj_in = jnp.einsum("rd,rf->df", normed_low, grad_pre, preferred_element_type=jnp.float32)
    back_part = jnp.einsum("rf,df->rd", grad_pre, proj_in, preferred_element_type=jnp.float32)
    grad_normed = grad_second + finish_sum(back_part)
    unused_first, pull_first = jax.vjp(layer_norm, first_in, gain_one, shift_one)
    grad_first, grad_gain_first, grad_shift_first = pull_first(grad_normed)
    grad_attn = grad_first.astype(jnp.bfloat16)
    grad_bias_attn = jnp.sum(grad_attn, 0, dtype=jnp.float32)
    grad_proj_attn = jnp.einsum(
        "rc,rd->cd", attended_rows, grad_attn, preferred_element_type=jnp.float32
    )
    grad_attended = jnp.einsum(
        "rd,cd->rc", grad_attn, proj_attn, preferred_element_type=jnp.float32
    ).astype(jnp.bfloat16)
    grad_att_heads = to_heads(grad_attended.reshape(seq_count, local_len, local_width), head_size)
    key_again, value_again = (
        lax.all_gather(key_blocks, "ctx", axis=1, tiled=True),
        lax.all_gather(value_blocks, "ctx", axis=1, tiled=True),
    )
    key_back = to_heads(key_again, head_size)
    value_back = to_heads(value_again, head_size)

    def head_grads(operands):
        query_head, key_head, value_head, grad_head, row_max, denominator = operands
        scores = masked_scores(query_head, key_head, same_doc)
        attn_probs = jnp.exp(scores - row_max) / denominator
        probs_low = attn_probs.astype(jnp.bfloat16)
        grad_probs = jnp.einsum(
            "sqd,skd->sqk", grad_head, value_head, preferred_element_type=jnp.float32
        )
        row_delta = jnp.sum(attn_probs * grad_probs, -1, keepdims=True)
        grad_scores = (attn_probs * (grad_probs - row_delta)).astype(jnp.bfloat16)
        grad_query = (
            jnp.einsum("sqk,skd->sqd", grad_scores, key_head, preferred_element_type=jnp.float32)
            * SCALE_QK
        )
        grad_key = (
            jnp.einsum("sqk,sqd->skd", grad_scores, query_head, preferred_element_type=jnp.float32)
            * SCALE_QK
        )
        grad_value = jnp.einsum(
            "sqk,sqd->skd", probs_low, grad_head, preferred_element_type=jnp.float32
        )
        return (grad_query.astype(jnp.bfloat16), grad_key, grad_value)

    grad_query_heads, grad_key_heads, grad_value_heads = lax.map(
        head_grads, (query_heads, key_back, value_back, grad_att_heads, row_maxes, denominators)
    )
    grad_key_full = from_heads(grad_key_heads)
    grad_value_full = from_heads(grad_value_heads)
    grad_key_part, grad_value_part = (
        lax.psum_scatter(
            grad_key_full.astype(jnp.bfloat16), "ctx", scatter_dimension=1, tiled=True
        ).astype(jnp.float32),
        lax.psum_scatter(
            grad_value_full.astype(jnp.bfloat16), "ctx", scatter_dimension=1, tiled=True
        ).astype(jnp.float32),
    )
    grad_query_rows = from_heads(grad_query_heads).reshape(row_count, local_width)
    grad_key_rows = grad_key_part.astype(jnp.bfloat16).reshape(row_count, local_width)
    grad_value_rows = grad_value_part.astype(jnp.bfloat16).reshape(row_count, local_width)
    grad_stack = jnp.stack([grad_query_rows, grad_key_rows, grad_value_rows])
    grad_proj_qkv = jnp.einsum(
        "rd,krc->kdc", inputs, grad_stack, preferred_element_type=jnp.float32
    )
    grad_bias_qv = jnp.stack(
        [
            jnp.sum(grad_query_rows, 0, dtype=jnp.float32),
            jnp.sum(grad_value_rows, 0, dtype=jnp.float32),
        ]
    ).reshape(2, local_heads, head_size)
    input_part = jnp.einsum("krc,kdc->rd", grad_stack, proj_qkv, preferred_element_type=jnp.float32)
    grad_inputs = grad_first + finish_sum(input_part)
    grad_tokens = grad_inputs.astype(jnp.bfloat16).reshape(seq_count, local_len, model_width)
    (
        share_qkv,
        share_bqv,
        share_attn,
        share_battn,
        share_gone,
        share_sone,
        share_in,
        share_bin,
        share_out,
        share_bout,
        share_gtwo,
        share_stwo,
    ) = (
        lax.psum_scatter(grad_proj_qkv, ("fsdp", "ctx"), scatter_dimension=1, tiled=True),
        lax.psum_scatter(grad_bias_qv, ("fsdp", "ctx"), scatter_dimension=2, tiled=True),
        lax.psum_scatter(grad_proj_attn, ("fsdp", "ctx"), scatter_dimension=1, tiled=True),
        lax.psum_scatter(grad_bias_attn, ("fsdp", "ctx"), scatter_dimension=0, tiled=True),
        lax.psum_scatter(grad_gain_first, ("fsdp", "ctx"), scatter_dimension=0, tiled=True),
        lax.psum_scatter(grad_shift_first, ("fsdp", "ctx"), scatter_dimension=0, tiled=True),
        lax.psum_scatter(grad_proj_in, ("fsdp", "ctx"), scatter_dimension=0, tiled=True),
        lax.psum_scatter(grad_bias_in, ("fsdp", "ctx"), scatter_dimension=1, tiled=True),
        lax.psum_scatter(grad_proj_out, ("fsdp", "ctx"), scatter_dimension=1, tiled=True),
        lax.psum_scatter(grad_bias_out, ("fsdp", "ctx"), scatter_dimension=0, tiled=True),
        lax.psum_scatter(grad_gain_second, ("fsdp", "ctx"), scatter_dimension=0, tiled=True),
        lax.psum_scatter(grad_shift_second, ("fsdp", "ctx"), scatter_dimension=0, tiled=True),
    )
    reduced = (
        lax.all_gather(share_qkv.astype(jnp.bfloat16), "ctx", axis=1, tiled=True).astype(
            share_qkv.dtype
        ),
        lax.all_gather(share_bqv.astype(jnp.bfloat16), "ctx", axis=2, tiled=True).astype(
            share_bqv.dtype
        ),
        lax.all_gather(share_attn.astype(jnp.bfloat16), "ctx", axis=1, tiled=True).astype(
            share_attn.dtype
        ),
        lax.all_gather(share_battn.astype(jnp.bfloat16), "ctx", axis=0, tiled=True).astype(
            share_battn.dtype
        ),
        lax.all_gather(share_gone.astype(jnp.bfloat16), "ctx", axis=0, tiled=True).astype(
            share_gone.dtype
        ),
        lax.all_gather(share_sone.astype(jnp.bfloat16), "ctx", axis=0, tiled=True).astype(
            share_sone.dtype
        ),
        lax.all_gather(share_in.astype(jnp.bfloat16), "ctx", axis=0, tiled=True).astype(
            share_in.dtype
        ),
        lax.all_gather(share_bin.astype(jnp.bfloat16), "ctx", axis=1, tiled=True).astype(
            share_bin.dtype
        ),
        lax.all_gather(share_out.astype(jnp.bfloat16), "ctx", axis=1, tiled=True).astype(
            share_out.dtype
        ),
        lax.all_gather(share_bout.astype(jnp.bfloat16), "ctx", axis=0, tiled=True).astype(
            share_bout.dtype
        ),
        lax.all_gather(share_gtwo.astype(jnp.bfloat16), "ctx", axis=0, tiled=True).astype(
            share_gtwo.dtype
        ),
        lax.all_gather(share_stwo.astype(jnp.bfloat16), "ctx", axis=0, tiled=True).astype(
            share_stwo.dtype
        ),
    )
    return (
        output,
        grad_tokens,
        reduced[0],
        reduced[1],
        reduced[2],
        reduced[3],
        reduced[4],
        reduced[5],
        reduced[6],
        reduced[7],
        reduced[8],
        reduced[9],
        reduced[10],
        reduced[11],
    )


def solution(mesh):
    in_specs = (
        P("fsdp", "ctx", None),
        P("fsdp", None),
        P(None, "fsdp", "tp"),
        P(None, "tp", "fsdp"),
        P("tp", "fsdp"),
        P("fsdp"),
        P("fsdp"),
        P("fsdp"),
        P("fsdp", "tp"),
        P("tp", "fsdp"),
        P("tp", "fsdp"),
        P("fsdp"),
        P("fsdp"),
        P("fsdp"),
        P("fsdp", "ctx", None),
    )
    out_specs = (
        P("fsdp", "ctx", None),
        P("fsdp", "ctx", None),
        P(None, "fsdp", "tp"),
        P(None, "tp", "fsdp"),
        P("tp", "fsdp"),
        P("fsdp"),
        P("fsdp"),
        P("fsdp"),
        P("fsdp", "tp"),
        P("tp", "fsdp"),
        P("tp", "fsdp"),
        P("fsdp"),
        P("fsdp"),
        P("fsdp"),
    )
    return jax.shard_map(local, mesh=mesh, in_specs=in_specs, out_specs=out_specs, check_vma=False)
```

profile of v0, /device:TPU:0, one launch (start us, length us, event | category | flops | bytes accessed | tf_op | source)
XLA Modules:
  0.0 1384.4 jit_solution(14793995309170661180)
XLA Ops:
  16.0 24.1 %all-gather.21.cloned.1.call-done = bf16[3,1024,256]{1,2,0:T(8,128)(2,1)} async-done(((bf16[3,512,256]{1,2,0:T(8,128)(2,1)}), bf16[3,1024,256]{1,2,0:T(8,128)(2,1)}) %all-gather.21.cloned.1.call-update) | async-done | bytes 1572880 | tf_op jit(solution)/shard_map/all_gather | solution.py:73
  71.3 17.5 %all-gather.25.cloned.1.call-done = bf16[4,2048,256]{1,2,0:T(8,128)(2,1)} async-done(((bf16[4,512,256]{1,2,0:T(8,128)(2,1)}), bf16[4,2048,256]{1,2,0:T(8,128)(2,1)}) %all-gather.25.cloned.1.call-update) | async-done | bytes 4194320 | tf_op jit(solution)/shard_map/all_gather | solution.py:109
  93.5 31.9 %all-gather.23.cloned.1.call-done = bf16[4,2048,256]{1,2,0:T(8,128)(2,1)} async-done(((bf16[4,512,256]{1,2,0:T(8,128)(2,1)}), bf16[4,2048,256]{1,2,0:T(8,128)(2,1)}) %all-gather.23.cloned.1.call-update) | async-done | bytes 4194320 | tf_op jit(solution)/shard_map/all_gather | solution.py:108
  130.3 62.6 %while.30 = (s32[]{:T(128)}, bf16[4,4,512,64]{2,3,1,0:T(8,128)(2,1)S(1)}, f32[4,4,512,1]{2,1,3,0:T(4,128)}, f32[4,4,512,1]{2,1,3,0:T(4,128)}, bf16[4,4,512,64]{2...) while((s32[]{:T(128)}, ...), condition=%wide.region_3.4_spmd.clone, body=%wide.region_0.3_spmd.clone.sunk | while | flops 1136783360 | bytes 53152356 | solution.py:130
  217.5 136.0 %all-reduce.14.cloned.1.call-done = bf16[2048,1024]{1,0:T(8,128)(2,1)} async-done(((bf16[2048,1024]{1,0:T(8,128)(2,1)}), bf16[2048,1024]{1,0:T(8,128)(2,1)}) %all-reduce.14.cloned.1.call-update) | async-done | bytes 4194320 | tf_op jit(solution)/shard_map/psum | solution.py:97
  364.1 22.9 %all-gather.27.cloned.1.call-done = bf16[1024,1024]{1,0:T(8,128)(2,1)} async-done(((bf16[512,1024]{1,0:T(8,128)(2,1)}), bf16[1024,1024]{1,0:T(8,128)(2,1)}) %all-gather.27.cloned.1.call-update) | async-done | bytes 2097168 | tf_op jit(solution)/shard_map/all_gather | solution.py:79
  387.0 11.0 multiply_convert_fusion.1
  398.0 23.6 %all-gather.29.cloned.1.call-done = bf16[1024,1024]{1,0:T(8,128)(2,1)} async-done(((bf16[1024,512]{1,0:T(8,128)(2,1)}), bf16[1024,1024]{1,0:T(8,128)(2,1)}) %all-gather.29.cloned.1.call-update) | async-done | bytes 2097168 | tf_op jit(solution)/shard_map/all_gather | solution.py:81
  421.5 9.4 convolution_convert_fusion.2
  444.7 141.4 %all-reduce.16.cloned.1.call-done = bf16[2048,1024]{1,0:T(8,128)(2,1)} async-done(((bf16[2048,1024]{1,0:T(8,128)(2,1)}), bf16[2048,1024]{1,0:T(8,128)(2,1)}) %all-reduce.16.cloned.1.call-update) | async-done | bytes 4194320 | tf_op jit(solution)/shard_map/psum | solution.py:97
  606.5 12.3 convert_reduce_fusion.2
  627.3 10.0 fusion.81
  637.4 11.4 fusion.69
  648.9 132.4 %all-reduce.18.cloned.1.call-done = bf16[2048,1024]{1,0:T(8,128)(2,1)} async-done(((bf16[2048,1024]{1,0:T(8,128)(2,1)}), bf16[2048,1024]{1,0:T(8,128)(2,1)}) %all-reduce.18.cloned.1.call-update) | async-done | bytes 4194320 | tf_op jit(solution)/shard_map/psum | solution.py:97
  781.2 9.4 multiply_reduce_fusion.1
  810.9 182.2 %while.31 = (s32[]{:T(128)}, bf16[4,4,512,64]{2,3,1,0:T(8,128)(2,1)}, bf16[4,4,2048,64]{2,3,0,1:T(8,128)(2,1)}, bf16[4,4,2048,64]{2,3,0,1:T(8,128)(2,1)}, bf16[4...) while((s32[]{:T(128)}, ...), condition=%wide.region_17.18_spmd.clone, body=%wide.region_15.17_spmd.clone.sunk | while | flops 2731276288 | bytes 202223824 | solution.py:202
  812.2 9.4 fusion.128
  822.3 9.8 multiply_reduce_fusion.6
  858.3 9.4 fusion.128
  868.4 9.8 multiply_reduce_fusion.6
  903.9 9.4 fusion.128
  914.0 9.7 multiply_reduce_fusion.6
  949.0 9.4 fusion.128
  959.1 9.7 multiply_reduce_fusion.6
  1007.2 29.6 %reduce-scatter.9.cloned.1.call-done = bf16[4,512,256]{1,2,0:T(8,128)(2,1)} async-done(((bf16[4,2048,256]{1,2,0:T(8,128)(2,1)}), bf16[4,512,256]{1,2,0:T(8,128)(2,1)}) %reduce-scatter.9.cloned.1.call-update) | async-done | bytes 1048592 | tf_op jit(solution)/shard_map/reduce_scatter | solution.py:208
  1038.3 45.3 %reduce-scatter.11.cloned.1.call-done = bf16[4,512,256]{1,2,0:T(8,128)(2,1)} async-done(((bf16[4,2048,256]{1,2,0:T(8,128)(2,1)}), bf16[4,512,256]{1,2,0:T(8,128)(2,1)}) %reduce-scatter.11.cloned.1.call-update) | async-done | bytes 1048592 | tf_op jit(solution)/shard_map/reduce_scatter | solution.py:211
  1105.4 18.0 %reduce-scatter.15.cloned.1.call-done = f32[256,128]{1,0:T(8,128)} async-done(((f32[256,1024]{1,0:T(8,128)}), f32[256,128]{1,0:T(8,128)}) %reduce-scatter.15.cloned.1.call-update) | async-done | bytes 131088 | tf_op jit(solution)/shard_map/reduce_scatter | solution.py:247
  1130.9 10.7 all-gather.33.cloned.1.call-done
  1144.5 15.9 %all-gather.31.cloned.1.call-done = bf16[512,1024]{1,0:T(8,128)(2,1)} async-done(((bf16[128,1024]{1,0:T(8,128)(2,1)}), bf16[512,1024]{1,0:T(8,128)(2,1)}) %all-gather.31.cloned.1.call-update) | async-done | bytes 1048592 | tf_op jit(solution)/shard_map/all_gather | solution.py:277
  1163.5 25.0 %all-reduce.8 = (bf16[2,4,64]{2,1,0:T(4,128)(2,1)S(1)}, bf16[16,64]{1,0:T(8,128)(2,1)S(1)}, bf16[1024]{0:T(1024)(128)(2,1)S(1)}, bf16[1024]{0:T(1024)(128)(2,1)S...) all-reduce(f32[2,4,64]{2,1,0:T(4,128)S(1)} %pad_maximum_fusion.3, ...), channel_id=5, replica_groups=mesh['fsdp'=2,'ctx'=4,'tp'=4] {'fsdp','ctx'}, use_global_device_ids=true, to_apply=%region_24.25.clone | all-reduce | flops 7680 | bytes 46080
  1234.7 83.4 %all-reduce.20.cloned.1.call-done = bf16[2048,1024]{1,0:T(8,128)(2,1)} async-done(((bf16[2048,1024]{1,0:T(8,128)(2,1)}), bf16[2048,1024]{1,0:T(8,128)(2,1)}) %all-reduce.20.cloned.1.call-update) | async-done | bytes 4194320 | tf_op jit(solution)/shard_map/psum | solution.py:97
  1325.3 41.2 %reduce-scatter.13.cloned.1.call-done = f32[3,128,256]{1,2,0:T(8,128)} async-done(((f32[3,1024,256]{1,2,0:T(8,128)}), f32[3,128,256]{1,2,0:T(8,128)}) %reduce-scatter.13.cloned.1.call-update) | async-done | bytes 393232 | tf_op jit(solution)/shard_map/reduce_scatter | solution.py:245
  (297 shorter events, 428.8 us)
Async XLA Ops:
  7.2 32.9 %all-gather.21.cloned.1.call-start = ((), (), s32[]{:S(2)}) async-start(), calls=%async_computation.6 | async-start | bytes 2359296 | tf_op jit(solution)/shard_map/all_gather | solution.py:73
  9.5 79.2 %all-gather.25.cloned.1.call-start = ((), (), s32[]{:S(2)}) async-start(), calls=%async_computation.8 | async-start | bytes 5242880 | tf_op jit(solution)/shard_map/all_gather | solution.py:109
  54.2 71.2 %all-gather.23.cloned.1.call-start = ((), (), s32[]{:S(2)}) async-start(), calls=%async_computation.7 | async-start | bytes 5242880 | tf_op jit(solution)/shard_map/all_gather | solution.py:108
  57.9 295.6 %all-reduce.14.cloned.1.call-start = ((), (), s32[]{:S(2)}) async-start(), calls=%async_computation.9 | async-start | bytes 8388608 | tf_op jit(solution)/shard_map/psum | solution.py:97
  130.3 64.7 %copy-start.15 = (bf16[256,1024]{1,0:T(8,128)(2,1)S(1)}, bf16[256,1024]{1,0:T(8,128)(2,1)}, u32[]{:S(2)}) copy-start(bf16[256,1024]{1,0:T(8,128)(2,1)} %all_gather.84) | copy-start | bytes 1572868
  193.8 14.6 %copy-start.32 = (bf16[512]{0:T(512)(128)(2,1)S(1)}, bf16[512]{0:T(512)(128)(2,1)}, u32[]{:S(2)}) copy-start(bf16[512]{0:T(512)(128)(2,1)} %param.26) | copy-start | bytes 3076
  193.8 19.0 %copy-start.28 = (bf16[16,32]{1,0:T(8,128)(2,1)S(1)}, bf16[16,32]{1,0:T(8,128)(2,1)}, u32[]{:S(2)}) copy-start(bf16[16,32]{1,0:T(8,128)(2,1)} %param.28) | copy-start | bytes 3076
  198.4 188.6 %all-gather.27.cloned.1.call-start = ((), (), s32[]{:S(2)}) async-start(), calls=%async_computation.10 | async-start | bytes 3145728 | tf_op jit(solution)/shard_map/all_gather | solution.py:79
  199.0 222.6 %all-gather.29.cloned.1.call-start = ((), (), s32[]{:S(2)}) async-start(), calls=%async_computation.11 | async-start | bytes 3145728 | tf_op jit(solution)/shard_map/all_gather | solution.py:81
  199.5 386.6 %all-reduce.16.cloned.1.call-start = ((), (), s32[]{:S(2)}) async-start(), calls=%async_computation.12 | async-start | bytes 8388608 | tf_op jit(solution)/shard_map/psum | solution.py:97
  421.5 13.9 %copy-start.34 = (bf16[512]{0:T(512)(128)(2,1)S(1)}, bf16[512]{0:T(512)(128)(2,1)}, u32[]{:S(2)}) copy-start(bf16[512]{0:T(512)(128)(2,1)} %param.31) | copy-start | bytes 3076
  421.5 18.3 %copy-start.35 = (bf16[512]{0:T(512)(128)(2,1)S(1)}, bf16[512]{0:T(512)(128)(2,1)}, u32[]{:S(2)}) copy-start(bf16[512]{0:T(512)(128)(2,1)} %param.32) | copy-start | bytes 3076
  431.0 350.2 %all-reduce.18.cloned.1.call-start = ((), (), s32[]{:S(2)}) async-start(), calls=%async_computation.13 | async-start | bytes 8388608 | tf_op jit(solution)/shard_map/psum | solution.py:97
  603.4 15.5 %copy-start.1 = (f32[2048,1024]{1,0:T(8,128)}, f32[2048,1024]{1,0:T(8,128)S(1)}, u32[]{:S(2)}) copy-start(f32[2048,1024]{1,0:T(8,128)S(1)} %get-tuple-element.391) | copy-start | bytes 25165828
  604.8 14.0 %copy-start.11 = (bf16[2048,1024]{1,0:T(8,128)(2,1)}, bf16[2048,1024]{1,0:T(8,128)(2,1)S(1)}, u32[]{:S(2)}) copy-start(bf16[2048,1024]{1,0:T(8,128)(2,1)S(1)} %get-tuple-element.383) | copy-start | bytes 12582916
  606.5 14.3 %copy-start.36 = (bf16[1024,1024]{1,0:T(8,128)(2,1)S(1)}, bf16[1024,1024]{1,0:T(8,128)(2,1)}, u32[]{:S(2)}) copy-start(bf16[1024,1024]{1,0:T(8,128)(2,1)} %all-gather.27.cloned.1.call-done) | copy-start | bytes 6291460
  627.1 371.7 %reduce-scatter.19.cloned.1.call-start = ((), (), s32[]{:S(2)}) async-start(), calls=%async_computation.21 | async-start | bytes 4718592 | tf_op jit(solution)/shard_map/reduce_scatter | solution.py:253
  637.3 363.4 %reduce-scatter.17.cloned.1.call-start = ((), (), s32[]{:S(2)}) async-start(), calls=%async_computation.19 | async-start | bytes 4718592 | tf_op jit(solution)/shard_map/reduce_scatter | solution.py:251
  648.8 388.0 %reduce-scatter.9.cloned.1.call-start = ((), (), s32[]{:S(2)}) async-start(), calls=%async_computation.14 | async-start | bytes 5242880 | tf_op jit(solution)/shard_map/reduce_scatter | solution.py:208
  993.1 90.5 %reduce-scatter.11.cloned.1.call-start = ((), (), s32[]{:S(2)}) async-start(), calls=%async_computation.15 | async-start | bytes 5242880 | tf_op jit(solution)/shard_map/reduce_scatter | solution.py:211
  993.7 129.6 %reduce-scatter.15.cloned.1.call-start = ((), (), s32[]{:S(2)}) async-start(), calls=%async_computation.18 | async-start | bytes 1179648 | tf_op jit(solution)/shard_map/reduce_scatter | solution.py:247
  998.8 142.8 %all-gather.33.cloned.1.call-start = ((), (), s32[]{:S(2)}) async-start(), calls=%async_computation.22 | async-start | bytes 1310720 | tf_op jit(solution)/shard_map/all_gather | solution.py:283
  1000.6 159.7 %all-gather.31.cloned.1.call-start = ((), (), s32[]{:S(2)}) async-start(), calls=%async_computation.20 | async-start | bytes 1310720 | tf_op jit(solution)/shard_map/all_gather | solution.py:277
  1002.6 315.5 %all-reduce.20.cloned.1.call-start = ((), (), s32[]{:S(2)}) async-start(), calls=%async_computation.16 | async-start | bytes 8388608 | tf_op jit(solution)/shard_map/psum | solution.py:97
  1091.5 274.9 %reduce-scatter.13.cloned.1.call-start = ((), (), s32[]{:S(2)}) async-start(), calls=%async_computation.17 | async-start | bytes 3538944 | tf_op jit(solution)/shard_map/reduce_scatter | solution.py:245
  1099.0 64.1 %copy-start.14 = (bf16[4,512,256]{1,2,0:T(8,128)(2,1)S(1)}, bf16[4,512,256]{1,2,0:T(8,128)(2,1)}, u32[]{:S(2)}) copy-start(bf16[4,512,256]{1,2,0:T(8,128)(2,1)} %reduce-scatter.11.cloned.1.call-done) | copy-start | bytes 3145732
  1099.0 64.4 %copy-start.23 = (f32[1024]{0:T(1024)S(1)}, f32[1024]{0:T(1024)}, u32[]{:S(2)}) copy-start(f32[1024]{0:T(1024)} %get-tuple-element.382) | copy-start | bytes 12292
  1099.0 64.4 %copy-start.24 = (f32[1024]{0:T(1024)S(1)}, f32[1024]{0:T(1024)}, u32[]{:S(2)}) copy-start(f32[1024]{0:T(1024)} %get-tuple-element.384) | copy-start | bytes 12292
  1099.0 64.4 %copy-start.25 = (f32[1024]{0:T(1024)S(1)}, f32[1024]{0:T(1024)}, u32[]{:S(2)}) copy-start(f32[1024]{0:T(1024)} %get-tuple-element.329) | copy-start | bytes 12292
  1099.0 64.4 %copy-start.26 = (f32[1024]{0:T(1024)S(1)}, f32[1024]{0:T(1024)}, u32[]{:S(2)}) copy-start(f32[1024]{0:T(1024)} %get-tuple-element.327) | copy-start | bytes 12292
  1099.0 64.4 %copy-start.27 = (f32[1024]{0:T(1024)S(1)}, f32[1024]{0:T(1024)}, u32[]{:S(2)}) copy-start(f32[1024]{0:T(1024)} %get-tuple-element.331) | copy-start | bytes 12292
  1099.1 219.1 %copy-start.22 = (f32[2048]{0:T(1024)S(1)}, f32[2048]{0:T(1024)}, u32[]{:S(2)}) copy-start(f32[2048]{0:T(1024)} %copy-done.21) | copy-start | bytes 24580
  (34 other events, 187.0 us)
Sparse Core Ops, SparseCore 0:
  10.1 29.8 all-gather.20
  54.3 34.4 all-gather.24
  90.9 34.4 all-gather.22
  198.5 154.9 all-reduce.13
  354.9 32.0 all-gather.26
  388.4 33.0 all-gather.28
  431.1 154.9 all-reduce.15
  627.2 153.9 all-reduce.17
  784.6 50.0 reduce-scatter.18
  837.9 51.1 reduce-scatter.16
  993.3 43.4 reduce-scatter.8
  1039.2 44.3 reduce-scatter.10
  1087.4 35.9 reduce-scatter.14
  1124.8 16.8 all-gather.32
  1143.6 16.6 all-gather.30
  1163.1 155.0 all-reduce.19
  1321.4 45.0 reduce-scatter.12
where the time goes:
time: 1390 us; the launch traced here: 1380 us
  waiting for transfers between devices  776 us (56%)
  matrix products  257 us (18%)
  blocking collectives  126 us (9%)
  other arithmetic  123 us (9%)
  local copies, waits for them, and re-layouts  85 us (6%)
  between operations  16.3 us (1%)
    psum x4, waiting for transfers between devices, finish_sum(): return lax.psum(partial_rows.astype(jnp.bfloat16), 'tp').astype(jnp.float32)  493 us
    dot_general x8, matrix products, masked_scores(): jnp.einsum('sqd,skd->sqk', query_head, key_head, preferred_element_type=j...  56.8 us
    reduce_scatter x1, waiting for transfers between devices, local(): lax.psum_scatter(grad_value_full.astype(jnp.bfloat16), 'ctx', scatter_dim...  45.3 us
    reduce_scatter x1, waiting for transfers between devices, local(): lax.psum_scatter(grad_proj_qkv, ('fsdp', 'ctx'), scatter_dimension=1, til...  41.2 us
    dot_general x4, matrix products, head_grads(): jnp.einsum('sqd,skd->sqk', grad_head, value_head, preferred_element_type=...  37.4 us
    all_gather x1, waiting for transfers between devices, local(): lax.all_gather(key_blocks, 'ctx', axis=1, tiled=True)  31.9 us
    unnamed x97, local copies, waits for them, and re-layouts  30.6 us
    reduce_scatter x1, waiting for transfers between devices, local(): lax.psum_scatter(grad_key_full.astype(jnp.bfloat16), 'ctx', scatter_dimen...  29.6 us
  transfers between devices with their start and end apart: 17, of which 15 were waited for; matrix products, arithmetic and copies ran while one was open for 21% of the time, Pallas kernels for 0%

commit v1 on v0

v1 whole, which is shorter than its diff:
```python
import functools

import jax
import jax.numpy as jnp
from jax import lax
from jax.experimental import pallas as pl
from jax.experimental.pallas import tpu as pltpu
from jax.sharding import PartitionSpec as P

EPSILON = 1e-12
NEG_LARGE = -1e30
SCALE_QK = 0.125
LOG2_E = 1.4426950408889634
SCALE_LOG2 = SCALE_QK * LOG2_E
LANES = 128
BF16 = jnp.bfloat16
F32 = jnp.float32
CONTRACT_LAST = (((1,), (1,)), ((), ()))
CONTRACT_FIRST = (((0,), (0,)), ((), ()))


def layer_norm(values, gain_vec, offset):
    center = values - jnp.mean(values, -1, keepdims=True)
    spread = jnp.mean(center * center, -1, keepdims=True)
    return center * lax.rsqrt(spread + EPSILON) * gain_vec + offset


def gelu_exact(values):
    return 0.5 * values * (1.0 + lax.erf(values * 0.7071067811865476))


def gelu_slope(values):
    normal_cdf = 0.5 * (1.0 + lax.erf(values * 0.7071067811865476))
    return normal_cdf + values * jnp.exp(-0.5 * values * values) * 0.3989422804014327


def dot_nt(left, right):
    return lax.dot_general(left, right, CONTRACT_LAST, preferred_element_type=F32)


def dot_tn(left, right):
    return lax.dot_general(left, right, CONTRACT_FIRST, preferred_element_type=F32)


def dot_nn(left, right):
    return jnp.dot(left, right, preferred_element_type=F32)


def attend_kernel(head_size, q_ref, k_ref, v_ref, sq_ref, sk_ref, o_ref, lse_ref):
    lane_head = lax.broadcasted_iota(jnp.int32, (1, LANES), 1) // head_size
    query, key, value = q_ref[0], k_ref[0], v_ref[0]
    same_doc = sq_ref[0] == sk_ref[0]
    heads = LANES // head_size
    mixed = jnp.zeros(query.shape, F32)
    lse = jnp.zeros(query.shape, F32)
    for head in range(heads):
        own = lane_head == head
        scores = dot_nt(jnp.where(own, query, jnp.zeros_like(query)), key)
        scores = jnp.where(same_doc, scores, NEG_LARGE)
        row_max = jnp.max(scores, -1, keepdims=True)
        exp_scores = jnp.exp2((scores - row_max) * SCALE_LOG2)
        denominator = jnp.sum(exp_scores, -1, keepdims=True)
        part = dot_nn(exp_scores.astype(BF16), value) / denominator
        mixed = jnp.where(own, part, mixed)
        lse = jnp.where(own, row_max * SCALE_LOG2 + jnp.log2(denominator), lse)
    o_ref[0] = mixed.astype(BF16)
    turned = lse.T
    for head in range(heads):
        lse_ref[0, 0, head : head + 1, :] = turned[head * head_size : head * head_size + 1, :]


def attend(query, key, value, segs, head_size):
    seq_count, length, cols = query.shape
    block = min(256, length)
    pairs = cols // LANES
    flops = 4 * seq_count * length * length * cols
    row_spec = pl.BlockSpec((1, block, LANES), lambda s, p, i: (s, i, p))
    full_spec = pl.BlockSpec((1, length, LANES), lambda s, p, i: (s, 0, p))
    return pl.pallas_call(
        functools.partial(attend_kernel, head_size),
        grid=(seq_count, pairs, length // block),
        in_specs=[
            row_spec,
            full_spec,
            full_spec,
            pl.BlockSpec((1, block, 1), lambda s, p, i: (s, i, 0)),
            pl.BlockSpec((1, 1, length), lambda s, p, i: (s, 0, 0)),
        ],
        out_specs=[row_spec, pl.BlockSpec((1, 1, 8, block), lambda s, p, i: (s, p, 0, i))],
        out_shape=[
            jax.ShapeDtypeStruct(query.shape, BF16),
            jax.ShapeDtypeStruct((seq_count, pairs, 8, length), F32),
        ],
        compiler_params=pltpu.CompilerParams(vmem_limit_bytes=48 << 20),
        cost_estimate=pl.CostEstimate(
            flops=flops,
            bytes_accessed=8 * seq_count * length * cols,
            transcendentals=seq_count * length * length * cols // head_size,
        ),
        name="attend",
    )(query, key, value, segs[:, :, None], segs[:, None, :])


def attend_grad_kernel(
    head_size,
    q_ref,
    do_ref,
    o_ref,
    k_ref,
    v_ref,
    sq_ref,
    sk_ref,
    lse_ref,
    dq_ref,
    dk_ref,
    dv_ref,
    kt_ref,
    dk_sum,
    dv_sum,
):
    step = pl.program_id(2)
    lane_head = lax.broadcasted_iota(jnp.int32, (1, LANES), 1) // head_size
    query, grad_out, key, value = q_ref[0], do_ref[0], k_ref[0], v_ref[0]

    @pl.when(step == 0)
    def _():
        kt_ref[...] = k_ref[0].T
        dk_sum[...] = jnp.zeros_like(dk_sum)
        dv_sum[...] = jnp.zeros_like(dv_sum)

    same_doc = sk_ref[0] == sq_ref[0]
    products = (grad_out.astype(F32) * o_ref[0].astype(F32)).T
    grad_query = []
    for head in range(LANES // head_size):
        own = lane_head == head
        rows = slice(head * head_size, (head + 1) * head_size)
        row_delta = jnp.sum(products[rows], 0, keepdims=True)
        query_own = jnp.where(own, query, jnp.zeros_like(query))
        grad_own = jnp.where(own, grad_out, jnp.zeros_like(grad_out))
        scores = dot_nt(key, query_own) * SCALE_LOG2 - lse_ref[0, 0, head : head + 1, :]
        probs = jnp.exp2(jnp.where(same_doc, scores, NEG_LARGE))
        grad_probs = dot_nt(value, grad_own)
        grad_scores = (probs * (grad_probs - row_delta)).astype(BF16)
        dv_sum[...] += dot_nn(probs.astype(BF16), grad_own)
        dk_sum[...] += dot_nn(grad_scores, query_own)
        grad_query.append(dot_nn(kt_ref[rows, :], grad_scores))
    dq_ref[0] = (jnp.concatenate(grad_query, 0).T * SCALE_QK).astype(BF16)

    @pl.when(step == pl.num_programs(2) - 1)
    def _():
        dk_ref[0] = (dk_sum[...] * SCALE_QK).astype(BF16)
        dv_ref[0] = dv_sum[...].astype(BF16)


def attend_grad(query, grad_out, mixed, key, value, segs, lse, head_size):
    seq_count, length, cols = query.shape
    block = min(256, length)
    pairs = cols // LANES
    row_spec = pl.BlockSpec((1, block, LANES), lambda s, p, i: (s, i, p))
    full_spec = pl.BlockSpec((1, length, LANES), lambda s, p, i: (s, 0, p))
    return pl.pallas_call(
        functools.partial(attend_grad_kernel, head_size),
        grid=(seq_count, pairs, length // block),
        in_specs=[
            row_spec,
            row_spec,
            row_spec,
            full_spec,
            full_spec,
            pl.BlockSpec((1, 1, block), lambda s, p, i: (s, 0, i)),
            pl.BlockSpec((1, length, 1), lambda s, p, i: (s, 0, 0)),
            pl.BlockSpec((1, 1, 8, block), lambda s, p, i: (s, p, 0, i)),
        ],
        out_specs=[row_spec, full_spec, full_spec],
        out_shape=[jax.ShapeDtypeStruct(query.shape, BF16)] * 3,
        scratch_shapes=[
            pltpu.VMEM((LANES, length), BF16),
            pltpu.VMEM((length, LANES), F32),
            pltpu.VMEM((length, LANES), F32),
        ],
        compiler_params=pltpu.CompilerParams(vmem_limit_bytes=56 << 20),
        cost_estimate=pl.CostEstimate(
            flops=10 * seq_count * length * length * cols,
            bytes_accessed=16 * seq_count * length * cols,
            transcendentals=seq_count * length * length * cols // head_size,
        ),
        name="attend_grad",
    )(query, grad_out, mixed, key, value, segs[:, None, :], segs[:, :, None], lse)


def local(
    sizes,
    tokens,
    segments,
    w_qkv,
    b_qv,
    w_o,
    b_o,
    ln1_gain,
    ln1_bias,
    w_in,
    b_in,
    w_out,
    b_out,
    ln2_gain,
    ln2_bias,
    cotangent,
):
    fsdp, ctx, tp = sizes
    at_fsdp, at_ctx, at_tp = (lax.axis_index(a) for a in ("fsdp", "ctx", "tp"))
    fsdp_bits, ctx_bits = fsdp.bit_length() - 1, ctx.bit_length() - 1
    low_ctx = ctx // 2
    seqs, block_len, width = tokens.shape
    own_seqs = seqs // tp
    rows = own_seqs * block_len
    length = segments.shape[1]
    head_size = b_qv.shape[2] * fsdp
    head_cols = w_qkv.shape[2] // ctx
    hidden = w_in.shape[1] // ctx
    width_part = width // fsdp

    def exchange(values, axis, size, j):
        return lax.ppermute(values, axis, [(i, i ^ j) for i in range(size)])

    def shift_tp(values):
        return lax.ppermute(values, "tp", [(i, (i + 1) % tp) for i in range(tp)])

    def reorder(blocks, place, bits, axis):
        size = blocks.shape[axis]
        for bit in range(bits):
            order = [i ^ (1 << bit) for i in range(size)]
            turned = jnp.stack([lax.index_in_dim(blocks, i, axis, False) for i in order], axis)
            blocks = jnp.where((place >> bit) & 1 == 1, turned, blocks)
        return blocks

    def reorder_width(values):
        if fsdp == 1:
            return values
        blocks = values.reshape(values.shape[0], fsdp, width_part)
        for bit in range(fsdp_bits):
            order = [i ^ (1 << bit) for i in range(fsdp)]
            parts = [values[:, i * width_part : (i + 1) * width_part] for i in order]
            values = jnp.where((at_fsdp >> bit) & 1 == 1, jnp.concatenate(parts, 1), values)
        del blocks
        return values

    def tp_pieces(piece):
        pieces = [piece]
        for _ in range(tp - 1):
            piece = shift_tp(piece)
            pieces.append(piece)
        return pieces

    def gather_width(values):
        for bit in range(fsdp_bits):
            values = jnp.concatenate([values, exchange(values, "fsdp", fsdp, 1 << bit)], 1)
        return values

    def rows_at(values, place, count):
        return lax.dynamic_slice_in_dim(values, place * count, count, 0)

    qkv_turned = jnp.swapaxes(w_qkv, 1, 2)
    qkv_piece = lax.dynamic_slice_in_dim(qkv_turned, at_ctx * head_cols, head_cols, 1).reshape(
        3 * head_cols, width_part
    )
    small_width = [v.reshape(1, -1) for v in (b_o, ln1_gain, ln1_bias, b_out, ln2_gain, ln2_bias)]
    small_tail = jnp.concatenate([b_qv.reshape(-1), b_in.reshape(-1)])
    tail_rows = -(-small_tail.shape[0] // width_part)
    small_tail = jnp.pad(small_tail, (0, tail_rows * width_part - small_tail.shape[0]))
    small = jnp.concatenate(small_width + [small_tail.reshape(tail_rows, width_part)], 0)
    small = jnp.pad(small, ((0, -small.shape[0] % 16), (0, 0)))
    small_rows = small.shape[0]
    first_pieces = tp_pieces(jnp.concatenate([qkv_piece, small], 0))
    first_parts = [p[i * head_cols : (i + 1) * head_cols] for i in range(3) for p in first_pieces]
    first_parts += [p[3 * head_cols :] for p in first_pieces]
    first_full = gather_width(jnp.concatenate(first_parts, 0))
    qkv_rows = 3 * tp * head_cols
    small_full = first_full[qkv_rows:].reshape(tp, small_rows, fsdp, width_part)

    def spread_ctx(values, bits):
        blocks = [values]
        for bit in range(bits):
            blocks = blocks + [exchange(b, "ctx", ctx, 1 << bit) for b in blocks]
        return blocks

    qkv_weights = spread_ctx(first_full[:qkv_rows], ctx_bits)
    o_piece = jnp.concatenate(tp_pieces(rows_at(w_o, at_ctx, head_cols)), 0)
    o_weights = jnp.concatenate(spread_ctx(gather_width(o_piece), ctx_bits), 0)
    in_piece = rows_at(w_in.T, at_ctx, hidden)
    in_own = gather_width(jnp.concatenate(tp_pieces(in_piece), 0))
    in_own = jnp.concatenate(spread_ctx(in_own, ctx_bits - 1), 0)
    in_weights = [in_own, exchange(in_own, "ctx", ctx, low_ctx)]
    out_weights = []
    for half in range(2):
        piece = rows_at(w_out, at_ctx ^ (half * low_ctx), hidden)
        piece = gather_width(jnp.concatenate(tp_pieces(piece), 0))
        out_weights.append(jnp.concatenate(spread_ctx(piece, ctx_bits - 1), 0))

    own_small = small_full[0].astype(F32)
    bias_attn, gain_one, shift_one, bias_out, gain_two, shift_two = (
        own_small[i].reshape(1, width) for i in range(6)
    )
    fsdp_order = at_fsdp ^ jnp.arange(fsdp)
    ctx_order = at_ctx ^ jnp.arange(ctx)
    tails = small_full[:, 6 : 6 + tail_rows].astype(F32)
    tails = jnp.take(tails.transpose(2, 0, 1, 3), fsdp_order, axis=0)
    tails = tails.reshape(fsdp, tp, tail_rows * width_part)
    head_count = b_qv.shape[1]
    qv_tail = tails[:, :, : b_qv.size].reshape(fsdp, tp, 2, head_count, head_size // fsdp)
    qv_bias = qv_tail.transpose(2, 1, 3, 0, 4).reshape(2, tp, ctx, head_cols)
    qv_bias = jnp.take(qv_bias, ctx_order, axis=2).transpose(2, 0, 1, 3)
    qv_bias = qv_bias.reshape(ctx, 2, tp * head_cols)
    in_tail = tails[:, :, b_qv.size : b_qv.size + b_in.size]
    in_tail = in_tail.reshape(fsdp, tp, b_in.shape[0], b_in.shape[1])
    in_bias = in_tail.transpose(1, 2, 0, 3).reshape(tp, ctx, hidden)
    in_bias = jnp.take(in_bias, ctx_order, axis=1).transpose(1, 0, 2)
    in_bias = in_bias.reshape(2, 1, low_ctx * tp * hidden)

    def own_rows(values):
        values = lax.dynamic_slice_in_dim(values, at_tp * own_seqs, own_seqs, 0)
        return reorder_width(values.reshape(rows, width))

    inputs, grad_final = own_rows(tokens), own_rows(cotangent)
    own_segments = lax.dynamic_slice_in_dim(segments, at_tp * own_seqs, own_seqs, 0)
    seg_blocks = own_segments.reshape(own_seqs, ctx, block_len)
    segs = jnp.concatenate(
        [
            lax.dynamic_index_in_dim(seg_blocks, at_ctx ^ j, 1, False)
            for j in range(ctx)
        ],
        1,
    )

    split_cols = width // ctx
    aligned = head_cols % head_size == 0
    if not aligned:
        want = ctx_order[:, None] * split_cols + jnp.arange(split_cols)[None, :]
        shard, inner = want // (ctx * head_cols), want % (ctx * head_cols)
        part, offset = inner // head_cols, inner % head_cols
        to_heads = ((part ^ at_ctx) * tp + (at_tp - shard) % tp) * head_cols + offset
        to_heads = to_heads.reshape(-1)
        from_heads = jnp.zeros_like(to_heads).at[to_heads].set(jnp.arange(width))

    def head_blocks(blocks):
        if aligned:
            return blocks
        moved = jnp.take(jnp.concatenate(blocks, 1), to_heads, axis=1)
        return [moved[:, j * split_cols : (j + 1) * split_cols] for j in range(ctx)]

    def column_blocks(blocks):
        if aligned:
            return blocks
        moved = jnp.take(jnp.concatenate(blocks, 1), from_heads, axis=1)
        return [moved[:, j * split_cols : (j + 1) * split_cols] for j in range(ctx)]

    def to_sequences(blocks):
        arrived = [blocks[0]] + [exchange(blocks[j], "ctx", ctx, j) for j in range(1, ctx)]
        cols = blocks[0].shape[1]
        return jnp.concatenate([b.reshape(own_seqs, block_len, cols) for b in arrived], 1)

    def to_rows(values):
        cols = values.shape[2]
        blocks = [
            values[:, j * block_len : (j + 1) * block_len].reshape(rows, cols) for j in range(ctx)
        ]
        return [blocks[0]] + [exchange(blocks[j], "ctx", ctx, j) for j in range(1, ctx)]

    qkv_blocks = []
    zero_bias = jnp.zeros((1, split_cols), F32)
    for j in range(ctx):
        bias = jnp.concatenate([qv_bias[j, 0:1], zero_bias, qv_bias[j, 1:2]], 1)
        qkv_blocks.append((dot_nt(inputs, qkv_weights[j]) + bias).astype(BF16))
    if not aligned:
        parts = [
            head_blocks([b[:, i * split_cols : (i + 1) * split_cols] for b in qkv_blocks])
            for i in range(3)
        ]
        qkv_blocks = [jnp.concatenate([p[j] for p in parts], 1) for j in range(ctx)]
    qkv_seq = to_sequences(qkv_blocks)
    query, key, value = (qkv_seq[:, :, i * split_cols : (i + 1) * split_cols] for i in range(3))
    mixed, lse = attend(query, key, value, segs, head_size)
    attended = jnp.concatenate(column_blocks(to_rows(mixed)), 1)

    attn_rows = dot_nn(attended, o_weights) + bias_attn
    first_in = inputs.astype(F32) + attn_rows
    normed, pull_first = jax.vjp(layer_norm, first_in, gain_one, shift_one)
    normed_low = normed.astype(BF16)
    pre_act = [dot_nt(normed_low, in_weights[h]) + in_bias[h] for h in range(2)]
    act_low = [gelu_exact(p).astype(BF16) for p in pre_act]
    mlp_rows = dot_nn(act_low[0], out_weights[0]) + dot_nn(act_low[1], out_weights[1]) + bias_out
    final_rows, pull_second = jax.vjp(layer_norm, normed + mlp_rows, gain_two, shift_two)

    def share_rows(values):
        values = reorder_width(values.astype(BF16)).reshape(own_seqs, block_len, width)
        pieces = tp_pieces(values)
        whole = jnp.zeros((seqs, block_len, width), BF16)
        for s in range(tp):
            start = ((at_tp - s) % tp) * own_seqs
            whole = lax.dynamic_update_slice_in_dim(whole, pieces[s], start, 0)
        return whole

    output = share_rows(final_rows)

    def add_low(left, right):
        return (left.astype(F32) + right.astype(F32)).astype(BF16)

    def fold_rows(values, bit):
        half = values.shape[0] // 2
        return add_low(values[:half], exchange(values[half:], "ctx", ctx, 1 << bit))

    def fold_width(values):
        for bit in reversed(range(fsdp_bits)):
            half = values.shape[1] // 2
            values = add_low(values[:, :half], exchange(values[:, half:], "fsdp", fsdp, 1 << bit))
        return values

    def fold_tp(pieces):
        total = pieces[1 % tp]
        for s in range(2, tp + 1):
            total = add_low(shift_tp(total), pieces[s % tp])
        return total

    def sum_shares(halves, width_first, split):
        for bit in reversed(range(ctx_bits - 1)):
            halves = [fold_rows(h, bit) for h in halves]
        if width_first:
            halves = [fold_width(h) for h in halves]
        total = add_low(halves[0], exchange(halves[1], "ctx", ctx, low_ctx))
        if not width_first:
            total = fold_width(total)
        return fold_tp(split(total))

    def split_even(total):
        count = total.shape[0] // tp
        return [total[s * count : (s + 1) * count] for s in range(tp)]

    def split_qkv(total):
        cut = [total[i * head_cols : (i + 1) * head_cols] for i in range(3 * tp)]
        return [jnp.concatenate([cut[i * tp + s] for i in range(3)], 0) for s in range(tp)]

    def join_ctx(share):
        blocks = jnp.stack(spread_ctx(share, ctx_bits), 0)
        return reorder(blocks, at_ctx, ctx_bits, 0).astype(F32)

    grad_second, grad_gain_second, grad_shift_second = pull_second(grad_final.astype(F32))
    grad_mlp = grad_second.astype(BF16)
    grad_bias_out = jnp.sum(grad_mlp, 0, dtype=F32)
    grad_pre, grad_out_halves, grad_in_halves = [], [], []
    for h in range(2):
        grad_out_halves.append(dot_tn(act_low[h], grad_mlp).astype(BF16))
    share_out = sum_shares(grad_out_halves, False, split_even)
    for h in range(2):
        grad_pre.append((dot_nt(grad_mlp, out_weights[h]) * gelu_slope(pre_act[h])).astype(BF16))
    grad_bias_in = jnp.stack([jnp.sum(g, 0, dtype=F32) for g in grad_pre])
    grad_normed = grad_second + (dot_nn(grad_pre[0], in_weights[0]) + dot_nn(grad_pre[1], in_weights[1]))
    grad_first, grad_gain_first, grad_shift_first = pull_first(grad_normed)
    grad_attn = grad_first.astype(BF16)
    grad_bias_attn = jnp.sum(grad_attn, 0, dtype=F32)
    grad_attended = dot_nt(grad_attn, o_weights).astype(BF16)
    grad_blocks = head_blocks(
        [grad_attended[:, j * split_cols : (j + 1) * split_cols] for j in range(ctx)]
    )
    grad_mixed = to_sequences(grad_blocks)
    for h in range(2):
        grad_in_halves.append(dot_tn(grad_pre[h], normed_low).astype(BF16))
    share_in = sum_shares(grad_in_halves, True, split_even)
    grad_o = dot_tn(attended, grad_attn).astype(BF16)
    half_o = grad_o.shape[0] // 2
    share_o = sum_shares([grad_o[:half_o], grad_o[half_o:]], True, split_even)

    grad_seq = jnp.concatenate(
        attend_grad(query, grad_mixed, mixed, key, value, segs, lse, head_size), 2
    )
    grad_qkv = to_rows(grad_seq)
    if not aligned:
        parts = [
            column_blocks([b[:, i * split_cols : (i + 1) * split_cols] for b in grad_qkv])
            for i in range(3)
        ]
        grad_qkv = [jnp.concatenate([p[j] for p in parts], 1) for j in range(ctx)]
    input_part = dot_nn(grad_qkv[0], qkv_weights[0])
    for j in range(1, ctx):
        input_part = input_part + dot_nn(grad_qkv[j], qkv_weights[j])
    grad_tokens = share_rows(grad_first + input_part)
    grad_qkv_w = [dot_tn(g, inputs).astype(BF16) for g in grad_qkv]

    def sum_qkv(blocks):
        total = [
            add_low(blocks[j], exchange(blocks[j + low_ctx], "ctx", ctx, low_ctx))
            for j in range(low_ctx)
        ]
        for bit in reversed(range(ctx_bits - 1)):
            half = len(total) // 2
            total = [
                add_low(total[j], exchange(total[j + half], "ctx", ctx, 1 << bit))
                for j in range(half)
            ]
        return fold_tp(split_qkv(fold_width(total[0])))

    share_qkv = sum_qkv(grad_qkv_w)

    def ctx_tp_order(values):
        blocks = values.reshape(values.shape[0], ctx, tp, -1)
        blocks = jnp.take(blocks, ctx_order, axis=1)
        blocks = jnp.take(blocks, (at_tp - jnp.arange(tp)) % tp, axis=2)
        return blocks.transpose(0, 2, 1, 3).reshape(values.shape[0], -1)

    def total_sum(values):
        for axis, size in (("ctx", ctx), ("fsdp", fsdp), ("tp", tp)):
            for bit in range(size.bit_length() - 1):
                values = values + exchange(values, axis, size, 1 << bit)
        return values

    small_sums = jnp.stack(
        [
            v.reshape(-1)
            for v in (
                grad_bias_attn,
                grad_gain_first,
                grad_shift_first,
                grad_bias_out,
                grad_gain_second,
                grad_shift_second,
            )
        ]
    )
    hidden_sums = ctx_tp_order(grad_bias_in.reshape(1, -1)).reshape(-1, width)
    small_sums = jnp.concatenate([reorder_width(small_sums), hidden_sums], 0)
    small_sums = total_sum(small_sums)
    width_start = at_fsdp * width_part
    width_sums = lax.dynamic_slice_in_dim(small_sums[:6], width_start, width_part, 1)
    hidden_own = lax.dynamic_slice_in_dim(
        small_sums[6:].reshape(tp, b_in.shape[0], fsdp, b_in.shape[1]), at_tp, 1, 0
    )
    grad_b_in = lax.dynamic_index_in_dim(hidden_own[0], at_fsdp, 1, False)
    qv_sums = [
        jnp.stack(
            [
                jnp.sum(g[:, i * split_cols : (i + 1) * split_cols], 0, dtype=F32)
                for g in grad_qkv
            ]
        )
        for i in (0, 2)
    ]
    qv_sums = total_sum(ctx_tp_order(jnp.stack(qv_sums).reshape(2, -1)))
    qv_own = lax.dynamic_index_in_dim(
        qv_sums.reshape(2, tp, head_count, fsdp, head_size // fsdp), at_tp, 1, False
    )
    grad_b_qv = lax.dynamic_index_in_dim(qv_own, at_fsdp, 2, False)

    grad_w_qkv = join_ctx(share_qkv.reshape(3, head_cols, width_part))
    grad_w_qkv = grad_w_qkv.transpose(1, 3, 0, 2).reshape(3, width_part, ctx * head_cols)
    grad_w_o = join_ctx(share_o).reshape(ctx * head_cols, width_part)
    grad_w_in = join_ctx(share_in).reshape(ctx * hidden, width_part).T
    grad_w_out = join_ctx(share_out).reshape(ctx * hidden, width_part)
    return (
        output,
        grad_tokens,
        grad_w_qkv,
        grad_b_qv,
        grad_w_o,
        width_sums[0],
        width_sums[1],
        width_sums[2],
        grad_w_in,
        grad_b_in,
        grad_w_out,
        width_sums[3],
        width_sums[4],
        width_sums[5],
    )


def solution(mesh):
    in_specs = (
        P("fsdp", "ctx", None),
        P("fsdp", None),
        P(None, "fsdp", "tp"),
        P(None, "tp", "fsdp"),
        P("tp", "fsdp"),
        P("fsdp"),
        P("fsdp"),
        P("fsdp"),
        P("fsdp", "tp"),
        P("tp", "fsdp"),
        P("tp", "fsdp"),
        P("fsdp"),
        P("fsdp"),
        P("fsdp"),
        P("fsdp", "ctx", None),
    )
    out_specs = (
        P("fsdp", "ctx", None),
        P("fsdp", "ctx", None),
        P(None, "fsdp", "tp"),
        P(None, "tp", "fsdp"),
        P("tp", "fsdp"),
        P("fsdp"),
        P("fsdp"),
        P("fsdp"),
        P("fsdp", "tp"),
        P("tp", "fsdp"),
        P("tp", "fsdp"),
        P("fsdp"),
        P("fsdp"),
        P("fsdp"),
    )
    sizes = tuple(mesh.shape[a] for a in ("fsdp", "ctx", "tp"))
    body = functools.partial(local, sizes)
    return jax.shard_map(body, mesh=mesh, in_specs=in_specs, out_specs=out_specs, check_vma=False)
```

time: 1390 us -> 863 us (0.62)
  waiting for transfers between devices: 776 us -> 454 us
  matrix products: 257 us -> 115 us
  blocking collectives: 126 us -> 0 us
  Pallas kernels: 0 us -> 86.4 us
  starting transfers between devices: 0.87 us -> 63.3 us
  other arithmetic: 123 us -> 72.3 us
  local copies, waits for them, and re-layouts: 85 us -> 59.9 us
    psum x4 -> x0, waiting for transfers between devices: 493 us -> none  [finish_sum(): return lax.psum(partial_rows.astype(jnp.bfloat16), 'tp').astype(jnp.float32)]
    ppermute x0 -> x100, waiting for transfers between devices: none -> 454 us  [the longest x67 255 us: exchange(): return lax.ppermute(values, axis, [(i, i ^ j) for i in range(size)])]
    all_gather x7 -> x0, waiting for transfers between devices: 147 us -> none  [the longest x1 31.9 us: local(): lax.all_gather(key_blocks, 'ctx', axis=1, tiled=True)]
    dot_general x40 -> x27, matrix products: 257 us -> 115 us  [the longest x9 49.6 us: dot_nt(): lax.dot_general(left, right, CONTRACT_LAST, preferred_element_type=F32)]
    reduce_scatter x6 -> x0, waiting for transfers between devices: 134 us -> none  [the longest x1 45.3 us: local(): lax.psum_scatter(grad_value_full.astype(jnp.bfloat16), 'ctx', scatter_dim...]
    all_gather x19 -> x0, blocking collectives: 101 us -> none  [the longest x1 8.86 us: local(): lax.all_gather(w_o, 'fsdp', axis=1, tiled=True)]
    pallas_call x0 -> x2, Pallas kernels: none -> 86.4 us  [the longest x1 52.3 us: attend_grad(): pl.pallas_call(functools.partial(attend_grad_kernel, head_size), grid=(se...]
    ppermute x0 -> x100, starting transfers between devices: none -> 63.3 us  [the longest x67 48.6 us: exchange(): return lax.ppermute(values, axis, [(i, i ^ j) for i in range(size)])]
  transfers between devices with their start and end apart: 17 -> 100, of which waited for: 15 -> 47; matrix products, arithmetic and copies ran while one was open for 21% -> 18% of each run, Pallas kernels for 0% -> 10%
where the time goes in v1:
time: 863 us; the launch traced here: 854 us
  waiting for transfers between devices  454 us (53%)
  matrix products  115 us (13%)
  Pallas kernels  86.4 us (10%)
  other arithmetic  72.3 us (8%)
  starting transfers between devices  63.3 us (7%)
  local copies, waits for them, and re-layouts  59.9 us (7%)
    ppermute x67, waiting for transfers between devices, exchange(): return lax.ppermute(values, axis, [(i, i ^ j) for i in range(size)])  255 us
    ppermute x33, waiting for transfers between devices, shift_tp(): return lax.ppermute(values, 'tp', [(i, (i + 1) % tp) for i in range(tp)])  199 us
    pallas_call x1, Pallas kernels, attend_grad(): pl.pallas_call(functools.partial(attend_grad_kernel, head_size), grid=(se...  52.3 us
    dot_general x9, matrix products, dot_nt(): lax.dot_general(left, right, CONTRACT_LAST, preferred_element_type=F32)  49.6 us
    ppermute x67, starting transfers between devices, exchange(): return lax.ppermute(values, axis, [(i, i ^ j) for i in range(size)])  48.6 us
    pallas_call x1, Pallas kernels, attend(): pl.pallas_call(functools.partial(attend_kernel, head_size), grid=(seq_cou...  34.2 us
    dot_general x9, matrix products, dot_tn(): lax.dot_general(left, right, CONTRACT_FIRST, preferred_element_type=F32)  33.2 us
    dot_general x9, matrix products, dot_nn(): return jnp.dot(left, right, preferred_element_type=F32)  32.1 us
  transfers between devices with their start and end apart: 100, of which 47 were waited for; matrix products, arithmetic and copies ran while one was open for 18% of the time, Pallas kernels for 10%

profile of v1, /device:TPU:0, one launch (start us, length us, event | category | flops | bytes accessed | tf_op | source)
XLA Modules:
  0.0 854.0 jit_solution(13116246728915814474)
XLA Ops:
  23.0 18.1 %collective-permute-done.1 = bf16[208,512]{1,0:T(8,128)(2,1)S(1)} collective-permute-done((bf16[208,512]{1,0:T(8,128)(2,1)S(1)}, bf16[208,512]{1,0:T(8,128)(2,1)S(1)}, u32[]{:S(2)}, u32[]{:S(2)}) %collective-permute-start.1) | collective-permute-done | bytes 213024 | tf_op jit(solution)/shard_map/ppermute | solution.py:226
  41.1 8.2 collective-permute-done.2
  54.9 5.2 collective-permute-done.14
  60.7 5.4 collective-permute-done.15
  86.1 5.6 collective-permute-done.22
  109.9 6.9 collective-permute-done.23
  124.1 17.3 %collective-permute-done.6 = bf16[768,1024]{1,0:T(8,128)(2,1)} collective-permute-done((bf16[768,1024]{1,0:T(8,128)(2,1)}, bf16[768,1024]{1,0:T(8,128)(2,1)}, u32[]{:S(2)}, u32[]{:S(2)}) %collective-permute-start.6) | collective-permute-done | bytes 1572896 | tf_op jit(solution)/shard_map/ppermute | solution.py:223
  145.0 30.0 %collective-permute-done.8 = bf16[768,1024]{1,0:T(8,128)(2,1)S(1)} collective-permute-done((bf16[768,1024]{1,0:T(8,128)(2,1)}, bf16[768,1024]{1,0:T(8,128)(2,1)S(1)}, u32[]{:S(2)}, u32[]{:S(2)}) %collective-permute-start.8) | collective-permute-done | bytes 1572896 | tf_op jit(solution)/shard_map/ppermute | solution.py:223
  177.5 6.9 pad_maximum_fusion
  186.4 5.4 collective-permute-done.7
  192.9 14.4 %collective-permute-done.9 = bf16[512,768]{1,0:T(8,128)(2,1)S(1)} collective-permute-done((bf16[512,768]{1,0:T(8,128)(2,1)S(1)}, bf16[512,768]{1,0:T(8,128)(2,1)S(1)}, u32[]{:S(2)}, u32[]{:S(2)}) %collective-permute-start.9) | collective-permute-done | bytes 786464 | tf_op jit(solution)/shard_map/ppermute | solution.py:223
  208.9 34.2 %attend.1 = (bf16[1,2048,256]{2,1,0:T(8,128)(2,1)S(1)}, f32[1,2,8,2048]{3,2,1,0:T(8,128)S(1)}) custom-call(bf16[1,2048,256]{2,1,0:T(8,128)(2,1)S(1)} %get-tuple-element.90.q_ref, bf16[1,2048,256]{2,1,0:T(8,128)(2,1)S(1)} %get-tuple-element.89.k_ref, bf16[1,2048,256]{2,1,0:T(8,128)(2,1)S(1)} %get-tuple-element.88.v_ref, ...), custom_call_target="tpu_custom_call" | custom-call | flops 4294967296 | bytes 4194304 | tf_op jit(solution)/shard_map/attend/pallas_call | solution.py:79
  250.4 76.3 %collective-permute-done.11 = bf16[512,256]{1,0:T(8,128)(2,1)S(1)} collective-permute-done((bf16[512,256]{1,0:T(8,128)(2,1)S(1)}, bf16[512,256]{1,0:T(8,128)(2,1)S(1)}, u32[]{:S(2)}, u32[]{:S(2)}) %collective-permute-start.11) | collective-permute-done | bytes 262176 | tf_op jit(solution)/shard_map/ppermute | solution.py:223
  336.8 5.3 multiply_convert_fusion
  342.1 5.7 fusion.54
  366.7 14.3 %convert_reduce_fusion.1 = (f32[2048]{0:T(1024)S(1)}, bf16[512,2048]{1,0:T(8,128)(2,1)}) fusion(f32[512,2048]{1,0:T(8,128)S(1)} %copy-done.84, f32[2048]{0:T(1024)S(1)} %bitcast.289, bf16[512,1024]{1,0:T(8,128)(2,1)S(1)} %get-tuple-element.72, bf16[1024,1024]{1,0:T(8,128)(2,1)S(1)} %collective-permute-done.29, ...), kind=kOutput, calls=%fused_computation.30 | convolution fusion | flops 2186278912 | bytes 11550720 | tf_op jit(solution)/shard_map/dot_general | solution.py:38
  381.0 6.1 convolution_convert_fusion.3
  387.1 14.9 %convert_reduce_fusion = (f32[2048]{0:T(1024)}, bf16[512,2048]{1,0:T(8,128)(2,1)S(1)}) fusion(f32[512,2048]{1,0:T(8,128)S(1)} %get-tuple-element.167, f32[2048]{0:T(1024)S(1)} %bitcast.287, bf16[512,1024]{1,0:T(8,128)(2,1)S(1)} %get-tuple-element.72, bf16[1024,1024]{1,0:T(8,128)(2,1)S(1)} %collective-permute-done.35, ...), kind=kOutput, calls=%fused_computation.29 | convolution fusion | flops 2186278912 | bytes 11550720 | tf_op jit(solution)/shard_map/dot_general | solution.py:38
  406.4 4.8 fusion.73
  460.1 52.3 %attend_grad.1 = (bf16[1,2048,256]{2,1,0:T(8,128)(2,1)}, bf16[1,2048,256]{2,1,0:T(8,128)(2,1)}, bf16[1,2048,256]{2,1,0:T(8,128)(2,1)}) custom-call(bf16[1,2048,256]{2,1,0:T(8,128)(2,1)} %copy-done.6, bf16[1,2048,256]{2,1,0:T(8,128)(2,1)} %pad_maximum_fusion.12.do_ref, bf16[1,2048,256]{2,1,0:T(8,128)(2,1)} %copy-done.3, bf16[1,2048,256]{2,1,0:T(8,128)(2,1)} %copy-done.5, ...), custom_call_target="tpu_custom_call" | custom-call | flops 10737418240 | bytes 8388608 | tf_op jit(solution)/shard_map/attend_grad/pallas_call | solution.py:161
  540.1 18.4 %collective-permute-done.67 = bf16[256,512]{1,0:T(8,128)(2,1)} collective-permute-done((bf16[256,512]{1,0:T(8,128)(2,1)S(1)}, bf16[256,512]{1,0:T(8,128)(2,1)}, u32[]{:S(2)}, u32[]{:S(2)}) %collective-permute-start.67) | collective-permute-done | bytes 262176 | tf_op jit(solution)/shard_map/ppermute | solution.py:223
  609.1 14.3 %collective-permute-done.37 = bf16[1,512,1024]{2,1,0:T(8,128)(2,1)} collective-permute-done((bf16[1,512,1024]{2,1,0:T(8,128)(2,1)}, bf16[1,512,1024]{2,1,0:T(8,128)(2,1)}, u32[]{:S(2)}, u32[]{:S(2)}) %collective-permute-start.37) | collective-permute-done | bytes 1048608 | tf_op jit(solution)/shard_map/ppermute | solution.py:226
  623.9 22.0 %collective-permute-done.45 = bf16[1,512,1024]{2,1,0:T(8,128)(2,1)} collective-permute-done((bf16[1,512,1024]{2,1,0:T(8,128)(2,1)}, bf16[1,512,1024]{2,1,0:T(8,128)(2,1)}, u32[]{:S(2)}, u32[]{:S(2)}) %collective-permute-start.45) | collective-permute-done | bytes 1048608 | tf_op jit(solution)/shard_map/ppermute | solution.py:226
  652.3 16.0 %collective-permute-done.38 = bf16[1,512,1024]{2,1,0:T(8,128)(2,1)S(1)} collective-permute-done((bf16[1,512,1024]{2,1,0:T(8,128)(2,1)}, bf16[1,512,1024]{2,1,0:T(8,128)(2,1)S(1)}, u32[]{:S(2)}, u32[]{:S(2)}) %collective-permute-start.38) | collective-permute-done | bytes 1048608 | tf_op jit(solution)/shard_map/ppermute | solution.py:226
  669.4 19.1 %collective-permute-done.46 = bf16[1,512,1024]{2,1,0:T(8,128)(2,1)S(1)} collective-permute-done((bf16[1,512,1024]{2,1,0:T(8,128)(2,1)}, bf16[1,512,1024]{2,1,0:T(8,128)(2,1)S(1)}, u32[]{:S(2)}, u32[]{:S(2)}) %collective-permute-start.46) | collective-permute-done | bytes 1048608 | tf_op jit(solution)/shard_map/ppermute | solution.py:226
  695.2 52.8 %collective-permute-done.83 = bf16[1024,512]{1,0:T(8,128)(2,1)S(1)} collective-permute-done((bf16[1024,512]{1,0:T(8,128)(2,1)S(1)}, bf16[1024,512]{1,0:T(8,128)(2,1)S(1)}, u32[]{:S(2)}, u32[]{:S(2)}) %collective-permute-start.83) | collective-permute-done | bytes 1048608 | tf_op jit(solution)/shard_map/ppermute | solution.py:223
  750.7 25.8 %collective-permute-done.84 = bf16[256,512]{1,0:T(8,128)(2,1)S(1)} collective-permute-done((bf16[256,512]{1,0:T(8,128)(2,1)S(1)}, bf16[256,512]{1,0:T(8,128)(2,1)S(1)}, u32[]{:S(2)}, u32[]{:S(2)}) %collective-permute-start.84) | collective-permute-done | bytes 262176 | tf_op jit(solution)/shard_map/ppermute | solution.py:226
  779.2 8.7 %collective-permute-done.85 = bf16[256,512]{1,0:T(8,128)(2,1)S(1)} collective-permute-done((bf16[256,512]{1,0:T(8,128)(2,1)S(1)}, bf16[256,512]{1,0:T(8,128)(2,1)S(1)}, u32[]{:S(2)}, u32[]{:S(2)}) %collective-permute-start.85) | collective-permute-done | bytes 262176 | tf_op jit(solution)/shard_map/ppermute | solution.py:226
  788.5 7.7 collective-permute-done.86
  800.0 7.9 collective-permute-done.53
  824.5 5.7 collective-permute-done.96
  843.6 5.1 collective-permute-done.98
  (614 shorter events, 309.8 us)
Async XLA Ops:
  13.5 54.4 %collective-permute-start.20 = (bf16[256,512]{0,1:T(8,128)(2,1)S(1)}, bf16[256,512]{0,1:T(8,128)(2,1)}, u32[]{:S(2)}, u32[]{:S(2)}) collective-permute-start(bf16[256,512]{0,1:T(8,128)(2,1)S(1)} %dynamic-slice_bitcast_fusion.2), channel_id=1, source_target_pairs={{0,1},{1,2},{2,3},{3,0},{4,5},{5,6},{6,7},{7,4},{8,9},{9,10},{10,1... | collective-permute-start | bytes 786440 | tf_op jit(solution)/shard_map/ppermute | solution.py:226
  15.9 52.0 %collective-permute-start.31 = (bf16[256,512]{1,0:T(8,128)(2,1)S(1)}, bf16[256,512]{1,0:T(8,128)(2,1)}, u32[]{:S(2)}, u32[]{:S(2)}) collective-permute-start(bf16[256,512]{1,0:T(8,128)(2,1)S(1)} %get-tuple-element.121), channel_id=1, source_target_pairs={{0,1},{1,2},{2,3},{3,0},{4,5},{5,6},{6,7},{7,4},{8,9},{9,10},{10,1... | collective-permute-start | bytes 786440 | tf_op jit(solution)/shard_map/ppermute | solution.py:226
  15.9 56.9 %collective-permute-start.25 = (bf16[256,512]{1,0:T(8,128)(2,1)}, bf16[256,512]{1,0:T(8,128)(2,1)}, u32[]{:S(2)}, u32[]{:S(2)}) collective-permute-start(bf16[256,512]{1,0:T(8,128)(2,1)} %get-tuple-element.120), channel_id=1, source_target_pairs={{0,1},{1,2},{2,3},{3,0},{4,5},{5,6},{6,7},{7,4},{8,9},{9,10},{10,1... | collective-permute-start | bytes 786440 | tf_op jit(solution)/shard_map/ppermute | solution.py:226
  82.3 102.0 %collective-permute-start.17 = (bf16[256,1024]{1,0:T(8,128)(2,1)}, bf16[256,1024]{1,0:T(8,128)(2,1)}, u32[]{:S(2)}, u32[]{:S(2)}) collective-permute-start(bf16[256,1024]{1,0:T(8,128)(2,1)} %pad_maximum_fusion.13), channel_id=1, source_target_pairs={{0,4},{4,0},{8,12},{12,8},{1,5},{5,1},{9,13},{13,9},{2,6},{6,2},{1... | collective-permute-start | bytes 1572872 | tf_op jit(solution)/shard_map/ppermute | solution.py:223
  108.9 66.1 %collective-permute-start.8 = (bf16[768,1024]{1,0:T(8,128)(2,1)}, bf16[768,1024]{1,0:T(8,128)(2,1)S(1)}, u32[]{:S(2)}, u32[]{:S(2)}) collective-permute-start(bf16[768,1024]{1,0:T(8,128)(2,1)} %collective-permute-done.4), channel_id=1, source_target_pairs={{0,8},{4,12},{8,0},{12,4},{1,9},{5,13},{9,1},{13,5},{2,10},{6,14},... | collective-permute-start | bytes 4718600 | tf_op jit(solution)/shard_map/ppermute | solution.py:223
  118.5 57.9 %collective-permute-start.24 = (bf16[1024,1024]{0,1:T(8,128)(2,1)S(1)}, bf16[1024,1024]{0,1:T(8,128)(2,1)S(1)}, u32[]{:S(2)}, u32[]{:S(2)}) collective-permute-start(bf16[1024,1024]{0,1:T(8,128)(2,1)S(1)} %pad_maximum_fusion.5), channel_id=1, source_target_pairs={{0,4},{4,0},{8,12},{12,8},{1,5},{5,1},{9,13},{13,9},{2,6},{6,2},{1... | collective-permute-start | bytes 6291464 | tf_op jit(solution)/shard_map/ppermute | solution.py:223
  123.5 62.4 %collective-permute-start.5 = (bf16[512,768]{1,0:T(8,128)(2,1)S(1)}, bf16[512,768]{1,0:T(8,128)(2,1)S(1)}, u32[]{:S(2)}, u32[]{:S(2)}) collective-permute-start(bf16[512,768]{1,0:T(8,128)(2,1)S(1)} %add_convert_fusion.19), channel_id=1, source_target_pairs={{0,4},{4,0},{8,12},{12,8},{1,5},{5,1},{9,13},{13,9},{2,6},{6,2},{1... | collective-permute-start | bytes 2359304 | tf_op jit(solution)/shard_map/ppermute | solution.py:223
  143.9 48.0 %collective-permute-start.7 = (bf16[512,768]{1,0:T(8,128)(2,1)S(1)}, bf16[512,768]{1,0:T(8,128)(2,1)S(1)}, u32[]{:S(2)}, u32[]{:S(2)}) collective-permute-start(bf16[512,768]{1,0:T(8,128)(2,1)S(1)} %add_convert_fusion.18), channel_id=1, source_target_pairs={{0,8},{4,12},{8,0},{12,4},{1,9},{5,13},{9,1},{13,5},{2,10},{6,14},... | collective-permute-start | bytes 2359304 | tf_op jit(solution)/shard_map/ppermute | solution.py:223
  176.3 66.9 %collective-permute-start.18 = (bf16[256,1024]{1,0:T(8,128)(2,1)}, bf16[256,1024]{1,0:T(8,128)(2,1)}, u32[]{:S(2)}, u32[]{:S(2)}) collective-permute-start(bf16[256,1024]{1,0:T(8,128)(2,1)} %pad_maximum_fusion.13), channel_id=1, source_target_pairs={{0,8},{4,12},{8,0},{12,4},{1,9},{5,13},{9,1},{13,5},{2,10},{6,14},... | collective-permute-start | bytes 1572872 | tf_op jit(solution)/shard_map/ppermute | solution.py:223
  184.3 60.4 %collective-permute-start.34 = (bf16[1024,512]{1,0:T(8,128)(2,1)}, bf16[1024,512]{1,0:T(8,128)(2,1)}, u32[]{:S(2)}, u32[]{:S(2)}) collective-permute-start(bf16[1024,512]{1,0:T(8,128)(2,1)} %pad_maximum_fusion.11), channel_id=1, source_target_pairs={{0,16},{16,0},{1,17},{17,1},{2,18},{18,2},{3,19},{19,3},{4,20},{20... | collective-permute-start | bytes 3145736 | tf_op jit(solution)/shard_map/ppermute | solution.py:223
  185.9 59.8 %collective-permute-start.28 = (bf16[1024,512]{1,0:T(8,128)(2,1)S(1)}, bf16[1024,512]{1,0:T(8,128)(2,1)}, u32[]{:S(2)}, u32[]{:S(2)}) collective-permute-start(bf16[1024,512]{1,0:T(8,128)(2,1)S(1)} %copy-done.43), channel_id=1, source_target_pairs={{0,16},{16,0},{1,17},{17,1},{2,18},{18,2},{3,19},{19,3},{4,20},{20... | collective-permute-start | bytes 3145736 | tf_op jit(solution)/shard_map/ppermute | solution.py:223
  191.9 57.6 %collective-permute-start.19 = (bf16[256,1024]{1,0:T(8,128)(2,1)}, bf16[256,1024]{1,0:T(8,128)(2,1)}, u32[]{:S(2)}, u32[]{:S(2)}) collective-permute-start(bf16[256,1024]{1,0:T(8,128)(2,1)} %collective-permute-done.17), channel_id=1, source_target_pairs={{0,8},{4,12},{8,0},{12,4},{1,9},{5,13},{9,1},{13,5},{2,10},{6,14},... | collective-permute-start | bytes 1572872 | tf_op jit(solution)/shard_map/ppermute | solution.py:223
  207.3 129.5 %collective-permute-start.30 = (bf16[2048,1024]{0,1:T(8,128)(2,1)S(1)}, bf16[2048,1024]{0,1:T(8,128)(2,1)}, u32[]{:S(2)}, u32[]{:S(2)}) collective-permute-start(bf16[2048,1024]{0,1:T(8,128)(2,1)S(1)} %pad_maximum_fusion), channel_id=1, source_target_pairs={{0,8},{4,12},{8,0},{12,4},{1,9},{5,13},{9,1},{13,5},{2,10},{6,14},... | collective-permute-start | bytes 12582920 | tf_op jit(solution)/shard_map/ppermute | solution.py:223
  244.8 81.9 %collective-permute-start.11 = (bf16[512,256]{1,0:T(8,128)(2,1)S(1)}, bf16[512,256]{1,0:T(8,128)(2,1)S(1)}, u32[]{:S(2)}, u32[]{:S(2)}) collective-permute-start(bf16[512,256]{1,0:T(8,128)(2,1)S(1)} %get-tuple-element.124), channel_id=1, source_target_pairs={{0,8},{4,12},{8,0},{12,4},{1,9},{5,13},{9,1},{13,5},{2,10},{6,14},... | collective-permute-start | bytes 786440 | tf_op jit(solution)/shard_map/ppermute | solution.py:223
  245.7 83.3 %collective-permute-start.12 = (bf16[512,256]{1,0:T(8,128)(2,1)S(1)}, bf16[512,256]{1,0:T(8,128)(2,1)S(1)}, u32[]{:S(2)}, u32[]{:S(2)}) collective-permute-start(bf16[512,256]{1,0:T(8,128)(2,1)S(1)} %get-tuple-element.123), channel_id=1, source_target_pairs={{0,12},{4,8},{8,4},{12,0},{1,13},{5,9},{9,5},{13,1},{2,14},{6,10},... | collective-permute-start | bytes 786440 | tf_op jit(solution)/shard_map/ppermute | solution.py:223
  249.5 92.6 %collective-permute-start.35 = (bf16[1024,1024]{1,0:T(8,128)(2,1)S(1)}, bf16[1024,1024]{1,0:T(8,128)(2,1)S(1)}, u32[]{:S(2)}, u32[]{:S(2)}) collective-permute-start(bf16[1024,1024]{1,0:T(8,128)(2,1)S(1)} %pad_maximum_fusion.7), channel_id=1, source_target_pairs={{0,4},{4,0},{8,12},{12,8},{1,5},{5,1},{9,13},{13,9},{2,6},{6,2},{1... | collective-permute-start | bytes 6291464 | tf_op jit(solution)/shard_map/ppermute | solution.py:223
  250.3 97.6 %collective-permute-start.29 = (bf16[1024,1024]{1,0:T(8,128)(2,1)S(1)}, bf16[1024,1024]{1,0:T(8,128)(2,1)S(1)}, u32[]{:S(2)}, u32[]{:S(2)}) collective-permute-start(bf16[1024,1024]{1,0:T(8,128)(2,1)S(1)} %pad_maximum_fusion.6), channel_id=1, source_target_pairs={{0,4},{4,0},{8,12},{12,8},{1,5},{5,1},{9,13},{13,9},{2,6},{6,2},{1... | collective-permute-start | bytes 6291464 | tf_op jit(solution)/shard_map/ppermute | solution.py:223
  436.9 84.4 %collective-permute-start.63 = (bf16[256,1024]{1,0:T(8,128)(2,1)}, bf16[256,1024]{1,0:T(8,128)(2,1)}, u32[]{:S(2)}, u32[]{:S(2)}) collective-permute-start(bf16[256,1024]{1,0:T(8,128)(2,1)} %get-tuple-element.94), channel_id=1, source_target_pairs={{0,4},{4,0},{8,12},{12,8},{1,5},{5,1},{9,13},{13,9},{2,6},{6,2},{1... | collective-permute-start | bytes 1572872 | tf_op jit(solution)/shard_map/ppermute | solution.py:223
  455.7 65.9 %collective-permute-start.65 = (bf16[256,1024]{1,0:T(8,128)(2,1)}, bf16[256,1024]{1,0:T(8,128)(2,1)}, u32[]{:S(2)}, u32[]{:S(2)}) collective-permute-start(bf16[256,1024]{1,0:T(8,128)(2,1)} %get-tuple-element.95), channel_id=1, source_target_pairs={{0,4},{4,0},{8,12},{12,8},{1,5},{5,1},{9,13},{13,9},{2,6},{6,2},{1... | collective-permute-start | bytes 1572872 | tf_op jit(solution)/shard_map/ppermute | solution.py:223
  457.1 75.6 %collective-permute-start.36 = (bf16[1,512,1024]{2,1,0:T(8,128)(2,1)}, bf16[1,512,1024]{2,1,0:T(8,128)(2,1)}, u32[]{:S(2)}, u32[]{:S(2)}) collective-permute-start(bf16[1,512,1024]{2,1,0:T(8,128)(2,1)} %get-tuple-element.83), channel_id=1, source_target_pairs={{0,1},{1,2},{2,3},{3,0},{4,5},{5,6},{6,7},{7,4},{8,9},{9,10},{10,1... | collective-permute-start | bytes 3145736 | tf_op jit(solution)/shard_map/ppermute | solution.py:226
  516.0 45.4 %collective-permute-start.43 = (bf16[512,768]{1,0:T(8,128)(2,1)}, bf16[512,768]{1,0:T(8,128)(2,1)}, u32[]{:S(2)}, u32[]{:S(2)}) collective-permute-start(bf16[512,768]{1,0:T(8,128)(2,1)} %get-tuple-element.86), channel_id=1, source_target_pairs={{0,8},{4,12},{8,0},{12,4},{1,9},{5,13},{9,1},{13,5},{2,10},{6,14},... | collective-permute-start | bytes 2359304 | tf_op jit(solution)/shard_map/ppermute | solution.py:223
  540.1 83.4 %collective-permute-start.91 = (bf16[1024,1024]{1,0:T(8,128)(2,1)}, bf16[1024,1024]{1,0:T(8,128)(2,1)}, u32[]{:S(2)}, u32[]{:S(2)}) collective-permute-start(bf16[1024,1024]{1,0:T(8,128)(2,1)} %slice.704), channel_id=1, source_target_pairs={{0,4},{4,0},{8,12},{12,8},{1,5},{5,1},{9,13},{13,9},{2,6},{6,2},{1... | collective-permute-start | bytes 6291464 | tf_op jit(solution)/shard_map/ppermute | solution.py:223
  558.5 47.2 %collective-permute-start.79 = (bf16[1024,1024]{1,0:T(8,128)(2,1)}, bf16[1024,1024]{1,0:T(8,128)(2,1)}, u32[]{:S(2)}, u32[]{:S(2)}) collective-permute-start(bf16[1024,1024]{1,0:T(8,128)(2,1)} %slice.687), channel_id=1, source_target_pairs={{0,4},{4,0},{8,12},{12,8},{1,5},{5,1},{9,13},{13,9},{2,6},{6,2},{1... | collective-permute-start | bytes 6291464 | tf_op jit(solution)/shard_map/ppermute | solution.py:223
  596.2 52.5 %collective-permute-start.49 = (bf16[768,1024]{1,0:T(8,128)(2,1)}, bf16[768,1024]{1,0:T(8,128)(2,1)}, u32[]{:S(2)}, u32[]{:S(2)}) collective-permute-start(bf16[768,1024]{1,0:T(8,128)(2,1)} %convolution_convert_fusion.5), channel_id=1, source_target_pairs={{0,8},{4,12},{8,0},{12,4},{1,9},{5,13},{9,1},{13,5},{2,10},{6,14},... | collective-permute-start | bytes 4718600 | tf_op jit(solution)/shard_map/ppermute | solution.py:223
  597.2 48.7 %collective-permute-start.45 = (bf16[1,512,1024]{2,1,0:T(8,128)(2,1)}, bf16[1,512,1024]{2,1,0:T(8,128)(2,1)}, u32[]{:S(2)}, u32[]{:S(2)}) collective-permute-start(bf16[1,512,1024]{2,1,0:T(8,128)(2,1)} %get-tuple-element.76), channel_id=1, source_target_pairs={{0,1},{1,2},{2,3},{3,0},{4,5},{5,6},{6,7},{7,4},{8,9},{9,10},{10,1... | collective-permute-start | bytes 3145736 | tf_op jit(solution)/shard_map/ppermute | solution.py:226
  605.7 46.1 %collective-permute-start.82 = (bf16[1024,512]{1,0:T(8,128)(2,1)S(1)}, bf16[1024,512]{1,0:T(8,128)(2,1)S(1)}, u32[]{:S(2)}, u32[]{:S(2)}) collective-permute-start(bf16[1024,512]{1,0:T(8,128)(2,1)S(1)} %slice.693), channel_id=1, source_target_pairs={{0,16},{16,0},{1,17},{17,1},{2,18},{18,2},{3,19},{19,3},{4,20},{20... | collective-permute-start | bytes 3145736 | tf_op jit(solution)/shard_map/ppermute | solution.py:223
  648.7 99.9 %collective-permute-start.48 = (bf16[768,1024]{1,0:T(8,128)(2,1)S(1)}, bf16[768,1024]{1,0:T(8,128)(2,1)S(1)}, u32[]{:S(2)}, u32[]{:S(2)}) collective-permute-start(bf16[768,1024]{1,0:T(8,128)(2,1)S(1)} %copy-done.80), channel_id=1, source_target_pairs={{0,8},{4,12},{8,0},{12,4},{1,9},{5,13},{9,1},{13,5},{2,10},{6,14},... | collective-permute-start | bytes 4718600 | tf_op jit(solution)/shard_map/ppermute | solution.py:223
  651.9 97.2 %collective-permute-start.50 = (bf16[768,1024]{1,0:T(8,128)(2,1)S(1)}, bf16[768,1024]{1,0:T(8,128)(2,1)S(1)}, u32[]{:S(2)}, u32[]{:S(2)}) collective-permute-start(bf16[768,1024]{1,0:T(8,128)(2,1)S(1)} %add_convert_fusion.6), channel_id=1, source_target_pairs={{0,4},{4,0},{8,12},{12,8},{1,5},{5,1},{9,13},{13,9},{2,6},{6,2},{1... | collective-permute-start | bytes 4718600 | tf_op jit(solution)/shard_map/ppermute | solution.py:223
  668.3 108.7 %collective-permute-start.90 = (bf16[1024,1024]{1,0:T(8,128)(2,1)S(1)}, bf16[1024,1024]{1,0:T(8,128)(2,1)S(1)}, u32[]{:S(2)}, u32[]{:S(2)}) collective-permute-start(bf16[1024,1024]{1,0:T(8,128)(2,1)S(1)} %copy-done.29), channel_id=1, source_target_pairs={{0,4},{4,0},{8,12},{12,8},{1,5},{5,1},{9,13},{13,9},{2,6},{6,2},{1... | collective-permute-start | bytes 6291464 | tf_op jit(solution)/shard_map/ppermute | solution.py:223
  668.3 108.7 %collective-permute-start.92 = (bf16[1024,1024]{1,0:T(8,128)(2,1)S(1)}, bf16[1024,1024]{1,0:T(8,128)(2,1)S(1)}, u32[]{:S(2)}, u32[]{:S(2)}) collective-permute-start(bf16[1024,1024]{1,0:T(8,128)(2,1)S(1)} %add_convert_fusion.1), channel_id=1, source_target_pairs={{0,8},{4,12},{8,0},{12,4},{1,9},{5,13},{9,1},{13,5},{2,10},{6,14},... | collective-permute-start | bytes 6291464 | tf_op jit(solution)/shard_map/ppermute | solution.py:223
  688.5 59.5 %collective-permute-start.83 = (bf16[1024,512]{1,0:T(8,128)(2,1)S(1)}, bf16[1024,512]{1,0:T(8,128)(2,1)S(1)}, u32[]{:S(2)}, u32[]{:S(2)}) collective-permute-start(bf16[1024,512]{1,0:T(8,128)(2,1)S(1)} %add_convert_fusion.10), channel_id=1, source_target_pairs={{0,8},{4,12},{8,0},{12,4},{1,9},{5,13},{9,1},{13,5},{2,10},{6,14},... | collective-permute-start | bytes 3145736 | tf_op jit(solution)/shard_map/ppermute | solution.py:223
  748.0 48.4 %collective-permute-start.47 = (bf16[1,512,1024]{2,1,0:T(8,128)(2,1)S(1)}, bf16[1,512,1024]{2,1,0:T(8,128)(2,1)S(1)}, u32[]{:S(2)}, u32[]{:S(2)}) collective-permute-start(bf16[1,512,1024]{2,1,0:T(8,128)(2,1)S(1)} %collective-permute-done.46), channel_id=1, source_target_pairs={{0,1},{1,2},{2,3},{3,0},{4,5},{5,6},{6,7},{7,4},{8,9},{9,10},{10,1... | collective-permute-start | bytes 3145736 | tf_op jit(solution)/shard_map/ppermute | solution.py:226
  (158 other events, 3346.4 us)

commit v2 on v1

--- a/solution.py
+++ b/solution.py
@@ -234,14 +234,10 @@
         return blocks
 
     def reorder_width(values):
-        if fsdp == 1:
-            return values
-        blocks = values.reshape(values.shape[0], fsdp, width_part)
         for bit in range(fsdp_bits):
             order = [i ^ (1 << bit) for i in range(fsdp)]
             parts = [values[:, i * width_part : (i + 1) * width_part] for i in order]
             values = jnp.where((at_fsdp >> bit) & 1 == 1, jnp.concatenate(parts, 1), values)
-        del blocks
         return values
 
     def tp_pieces(piece):
@@ -256,13 +252,34 @@
             values = jnp.concatenate([values, exchange(values, "fsdp", fsdp, 1 << bit)], 1)
         return values
 
-    def rows_at(values, place, count):
-        return lax.dynamic_slice_in_dim(values, place * count, count, 0)
-
+    def spread_near(values):
+        blocks = [values]
+        for bit in range(ctx_bits - 1):
+            blocks = blocks + [exchange(b, "ctx", ctx, 1 << bit) for b in blocks]
+        return blocks
+
+    def near_rows(values, count, both):
+        halves = range(2) if both else range(1)
+        return [
+            lax.dynamic_slice_in_dim(values, (at_ctx ^ (h * low_ctx)) * count, count, 0)
+            for h in halves
+        ]
+
+    def cut(values, count):
+        return [values[i : i + count] for i in range(0, values.shape[0], count)]
+
+    per_group = max(1, LANES // head_cols)
+    groups = tp // per_group
+    group_cols = per_group * head_cols
     qkv_turned = jnp.swapaxes(w_qkv, 1, 2)
-    qkv_piece = lax.dynamic_slice_in_dim(qkv_turned, at_ctx * head_cols, head_cols, 1).reshape(
-        3 * head_cols, width_part
-    )
+    qkv_pieces = []
+    for h in range(2):
+        start = (at_ctx ^ (h * low_ctx)) * head_cols
+        qkv_pieces.append(
+            lax.dynamic_slice_in_dim(qkv_turned, start, head_cols, 1).reshape(
+                3 * head_cols, width_part
+            )
+        )
     small_width = [v.reshape(1, -1) for v in (b_o, ln1_gain, ln1_bias, b_out, ln2_gain, ln2_bias)]
     small_tail = jnp.concatenate([b_qv.reshape(-1), b_in.reshape(-1)])
     tail_rows = -(-small_tail.shape[0] // width_part)
@@ -270,31 +287,49 @@
     small = jnp.concatenate(small_width + [small_tail.reshape(tail_rows, width_part)], 0)
     small = jnp.pad(small, ((0, -small.shape[0] % 16), (0, 0)))
     small_rows = small.shape[0]
-    first_pieces = tp_pieces(jnp.concatenate([qkv_piece, small], 0))
-    first_parts = [p[i * head_cols : (i + 1) * head_cols] for i in range(3) for p in first_pieces]
-    first_parts += [p[3 * head_cols :] for p in first_pieces]
-    first_full = gather_width(jnp.concatenate(first_parts, 0))
-    qkv_rows = 3 * tp * head_cols
-    small_full = first_full[qkv_rows:].reshape(tp, small_rows, fsdp, width_part)
-
-    def spread_ctx(values, bits):
-        blocks = [values]
-        for bit in range(bits):
-            blocks = blocks + [exchange(b, "ctx", ctx, 1 << bit) for b in blocks]
-        return blocks
-
-    qkv_weights = spread_ctx(first_full[:qkv_rows], ctx_bits)
-    o_piece = jnp.concatenate(tp_pieces(rows_at(w_o, at_ctx, head_cols)), 0)
-    o_weights = jnp.concatenate(spread_ctx(gather_width(o_piece), ctx_bits), 0)
-    in_piece = rows_at(w_in.T, at_ctx, hidden)
-    in_own = gather_width(jnp.concatenate(tp_pieces(in_piece), 0))
-    in_own = jnp.concatenate(spread_ctx(in_own, ctx_bits - 1), 0)
-    in_weights = [in_own, exchange(in_own, "ctx", ctx, low_ctx)]
-    out_weights = []
-    for half in range(2):
-        piece = rows_at(w_out, at_ctx ^ (half * low_ctx), hidden)
-        piece = gather_width(jnp.concatenate(tp_pieces(piece), 0))
-        out_weights.append(jnp.concatenate(spread_ctx(piece, ctx_bits - 1), 0))
+    first_rows = 6 * head_cols + small_rows
+    with jax.named_scope("get_qkv"):
+        first_pieces = tp_pieces(jnp.concatenate(qkv_pieces + [small], 0))
+        early = (tp + 1) // 2
+        first_full = [
+            part
+            for group in (first_pieces[:early], first_pieces[early:])
+            if group
+            for part in cut(gather_width(jnp.concatenate(group, 0)), first_rows)
+        ]
+        unit = [cut(p[: 6 * head_cols], head_cols) for p in first_full]
+        own_qkv = jnp.concatenate(
+            [
+                unit[g * per_group + s][h * 3 + i]
+                for h in range(2)
+                for g in range(groups)
+                for i in range(3)
+                for s in range(per_group)
+            ],
+            0,
+        )
+        qkv_weights = spread_near(own_qkv)
+    small_full = jnp.stack([p[6 * head_cols :] for p in first_full])
+    small_full = small_full.reshape(tp, small_rows, fsdp, width_part)
+    with jax.named_scope("get_in"):
+        in_piece = near_rows(w_in.T, hidden, False)[0]
+        in_own = gather_width(jnp.concatenate(tp_pieces(in_piece), 0))
+        in_own = jnp.concatenate([in_own, exchange(in_own, "ctx", ctx, low_ctx)], 0)
+        in_weights = spread_near(in_own)
+    with jax.named_scope("get_out"):
+        o_parts, out_parts = near_rows(w_o, head_cols, True), near_rows(w_out, hidden, True)
+        pieces = tp_pieces(jnp.concatenate(o_parts + out_parts, 0))
+        o_parts = [p[h * head_cols : (h + 1) * head_cols] for h in range(2) for p in pieces]
+        out_parts = [
+            p[2 * head_cols + h * hidden : 2 * head_cols + (h + 1) * hidden]
+            for h in range(2)
+            for p in pieces
+        ]
+        both_own = gather_width(jnp.concatenate(o_parts + out_parts, 0))
+        both_weights = spread_near(both_own)
+        o_rows = 2 * tp * head_cols
+        o_weights = [w[:o_rows] for w in both_weights]
+        out_weights = [w[o_rows:] for w in both_weights]
 
     own_small = small_full[0].astype(F32)
     bias_attn, gain_one, shift_one, bias_out, gain_two, shift_two = (
@@ -303,18 +338,21 @@
     fsdp_order = at_fsdp ^ jnp.arange(fsdp)
     ctx_order = at_ctx ^ jnp.arange(ctx)
     tails = small_full[:, 6 : 6 + tail_rows].astype(F32)
-    tails = jnp.take(tails.transpose(2, 0, 1, 3), fsdp_order, axis=0)
+    tails = reorder(tails.transpose(2, 0, 1, 3), at_fsdp, fsdp_bits, 0)
     tails = tails.reshape(fsdp, tp, tail_rows * width_part)
     head_count = b_qv.shape[1]
     qv_tail = tails[:, :, : b_qv.size].reshape(fsdp, tp, 2, head_count, head_size // fsdp)
     qv_bias = qv_tail.transpose(2, 1, 3, 0, 4).reshape(2, tp, ctx, head_cols)
-    qv_bias = jnp.take(qv_bias, ctx_order, axis=2).transpose(2, 0, 1, 3)
-    qv_bias = qv_bias.reshape(ctx, 2, tp * head_cols)
+    qv_bias = reorder(qv_bias, at_ctx, ctx_bits, 2)
     in_tail = tails[:, :, b_qv.size : b_qv.size + b_in.size]
     in_tail = in_tail.reshape(fsdp, tp, b_in.shape[0], b_in.shape[1])
     in_bias = in_tail.transpose(1, 2, 0, 3).reshape(tp, ctx, hidden)
-    in_bias = jnp.take(in_bias, ctx_order, axis=1).transpose(1, 0, 2)
-    in_bias = in_bias.reshape(2, 1, low_ctx * tp * hidden)
+    in_bias = reorder(in_bias, at_ctx, ctx_bits, 1).reshape(tp, 2, low_ctx, hidden)
+    in_bias = in_bias.transpose(2, 1, 0, 3).reshape(low_ctx, 1, 2 * tp * hidden)
+    qv_bias = qv_bias.reshape(2, groups, per_group, 2, low_ctx, head_cols)
+    qv_bias = qv_bias.transpose(4, 3, 1, 0, 2, 5).reshape(low_ctx, 2, groups, 2, group_cols)
+    qkv_bias = jnp.stack([qv_bias[:, :, :, 0], jnp.zeros_like(qv_bias[:, :, :, 0]), qv_bias[:, :, :, 1]], 3)
+    qkv_bias = qkv_bias.reshape(low_ctx, 1, 6 * tp * head_cols)
 
     def own_rows(values):
         values = lax.dynamic_slice_in_dim(values, at_tp * own_seqs, own_seqs, 0)
@@ -324,15 +362,11 @@
     own_segments = lax.dynamic_slice_in_dim(segments, at_tp * own_seqs, own_seqs, 0)
     seg_blocks = own_segments.reshape(own_seqs, ctx, block_len)
     segs = jnp.concatenate(
-        [
-            lax.dynamic_index_in_dim(seg_blocks, at_ctx ^ j, 1, False)
-            for j in range(ctx)
-        ],
-        1,
+        [lax.dynamic_index_in_dim(seg_blocks, at_ctx ^ j, 1, False) for j in range(ctx)], 1
     )
 
+    aligned = head_cols % head_size == 0
     split_cols = width // ctx
-    aligned = head_cols % head_size == 0
     if not aligned:
         want = ctx_order[:, None] * split_cols + jnp.arange(split_cols)[None, :]
         shard, inner = want // (ctx * head_cols), want % (ctx * head_cols)
@@ -341,17 +375,24 @@
         to_heads = to_heads.reshape(-1)
         from_heads = jnp.zeros_like(to_heads).at[to_heads].set(jnp.arange(width))
 
-    def head_blocks(blocks):
+    def move_columns(blocks, order):
         if aligned:
             return blocks
-        moved = jnp.take(jnp.concatenate(blocks, 1), to_heads, axis=1)
-        return [moved[:, j * split_cols : (j + 1) * split_cols] for j in range(ctx)]
-
-    def column_blocks(blocks):
-        if aligned:
-            return blocks
-        moved = jnp.take(jnp.concatenate(blocks, 1), from_heads, axis=1)
-        return [moved[:, j * split_cols : (j + 1) * split_cols] for j in range(ctx)]
+        parts = blocks[0][0].shape[1] // group_cols
+        moved = []
+        for i in range(parts):
+            cols = slice(i * group_cols, (i + 1) * group_cols)
+            flat = jnp.concatenate([b[:, cols] for per in blocks for b in per], 1)
+            moved.append(jnp.take(flat, order, axis=1))
+        result = []
+        for j in range(ctx):
+            result.append([])
+            for g in range(groups):
+                start = j * split_cols + g * group_cols
+                result[j].append(
+                    jnp.concatenate([m[:, start : start + group_cols] for m in moved], 1)
+                )
+        return result
 
     def to_sequences(blocks):
         arrived = [blocks[0]] + [exchange(blocks[j], "ctx", ctx, j) for j in range(1, ctx)]
@@ -365,48 +406,81 @@
         ]
         return [blocks[0]] + [exchange(blocks[j], "ctx", ctx, j) for j in range(1, ctx)]
 
-    qkv_blocks = []
-    zero_bias = jnp.zeros((1, split_cols), F32)
-    for j in range(ctx):
-        bias = jnp.concatenate([qv_bias[j, 0:1], zero_bias, qv_bias[j, 1:2]], 1)
-        qkv_blocks.append((dot_nt(inputs, qkv_weights[j]) + bias).astype(BF16))
-    if not aligned:
-        parts = [
-            head_blocks([b[:, i * split_cols : (i + 1) * split_cols] for b in qkv_blocks])
-            for i in range(3)
+    def by_block(near_values, cols):
+        return [
+            [
+                near_values[j % low_ctx][
+                    :, ((j // low_ctx) * groups + g) * cols : ((j // low_ctx) * groups + g + 1) * cols
+                ]
+                for g in range(groups)
+            ]
+            for j in range(ctx)
         ]
-        qkv_blocks = [jnp.concatenate([p[j] for p in parts], 1) for j in range(ctx)]
-    qkv_seq = to_sequences(qkv_blocks)
-    query, key, value = (qkv_seq[:, :, i * split_cols : (i + 1) * split_cols] for i in range(3))
-    mixed, lse = attend(query, key, value, segs, head_size)
-    attended = jnp.concatenate(column_blocks(to_rows(mixed)), 1)
-
-    attn_rows = dot_nn(attended, o_weights) + bias_attn
+
+    def by_near(blocks):
+        return [
+            jnp.concatenate(
+                [blocks[h * low_ctx + n][g] for h in range(2) for g in range(groups)], 1
+            )
+            for n in range(low_ctx)
+        ]
+
+    qkv_near = [
+        (dot_nt(inputs, qkv_weights[n]) + qkv_bias[n]).astype(BF16) for n in range(low_ctx)
+    ]
+    qkv_blocks = move_columns(by_block(qkv_near, 3 * group_cols), None if aligned else to_heads)
+    heads_in, mixed_parts, mixed_blocks = [], [], [[] for _ in range(ctx)]
+    for g in range(groups):
+        with jax.named_scope("to_sequences"):
+            qkv_seq = to_sequences([b[g] for b in qkv_blocks])
+        parts = [qkv_seq[:, :, i * group_cols : (i + 1) * group_cols] for i in range(3)]
+        mixed, lse = attend(*parts, segs, head_size)
+        heads_in.append((parts, lse))
+        mixed_parts.append(mixed)
+        with jax.named_scope("to_rows"):
+            for j, block in enumerate(to_rows(mixed)):
+                mixed_blocks[j].append(block)
+    attended = by_near(move_columns(mixed_blocks, None if aligned else from_heads))
+
+    attn_rows = bias_attn
+    for n in range(low_ctx):
+        attn_rows = attn_rows + dot_nn(attended[n], o_weights[n])
     first_in = inputs.astype(F32) + attn_rows
     normed, pull_first = jax.vjp(layer_norm, first_in, gain_one, shift_one)
     normed_low = normed.astype(BF16)
-    pre_act = [dot_nt(normed_low, in_weights[h]) + in_bias[h] for h in range(2)]
+    pre_act = [dot_nt(normed_low, in_weights[n]) + in_bias[n] for n in range(low_ctx)]
     act_low = [gelu_exact(p).astype(BF16) for p in pre_act]
-    mlp_rows = dot_nn(act_low[0], out_weights[0]) + dot_nn(act_low[1], out_weights[1]) + bias_out
+    mlp_rows = bias_out
+    for n in range(low_ctx):
+        mlp_rows = mlp_rows + dot_nn(act_low[n], out_weights[n])
     final_rows, pull_second = jax.vjp(layer_norm, normed + mlp_rows, gain_two, shift_two)
 
-    def share_rows(values):
-        values = reorder_width(values.astype(BF16)).reshape(own_seqs, block_len, width)
-        pieces = tp_pieces(values)
+    def turned_rows(values):
+        return reorder_width(values.astype(BF16)).reshape(own_seqs, block_len, width)
+
+    def place_rows(pieces):
         whole = jnp.zeros((seqs, block_len, width), BF16)
         for s in range(tp):
             start = ((at_tp - s) % tp) * own_seqs
             whole = lax.dynamic_update_slice_in_dim(whole, pieces[s], start, 0)
         return whole
 
-    output = share_rows(final_rows)
+    def gate(values, waited):
+        values, waited = lax.optimization_barrier((values, waited))
+        return values, waited
+
+    output_pieces = [turned_rows(final_rows)]
+
+    def next_output():
+        with jax.named_scope("share_output"):
+            return shift_tp(output_pieces[-1]) if len(output_pieces) < tp else output_pieces[0]
+
+    def keep_output(piece):
+        if len(output_pieces) < tp:
+            output_pieces.append(piece)
 
     def add_low(left, right):
         return (left.astype(F32) + right.astype(F32)).astype(BF16)
-
-    def fold_rows(values, bit):
-        half = values.shape[0] // 2
-        return add_low(values[:half], exchange(values[half:], "ctx", ctx, 1 << bit))
 
     def fold_width(values):
         for bit in reversed(range(fsdp_bits)):
@@ -414,102 +488,127 @@
             values = add_low(values[:, :half], exchange(values[:, half:], "fsdp", fsdp, 1 << bit))
         return values
 
+    def fold_half(values):
+        half = values.shape[0] // 2
+        return add_low(values[:half], exchange(values[half:], "ctx", ctx, low_ctx))
+
     def fold_tp(pieces):
-        total = pieces[1 % tp]
-        for s in range(2, tp + 1):
-            total = add_low(shift_tp(total), pieces[s % tp])
-        return total
-
-    def sum_shares(halves, width_first, split):
+        total = pieces[0].astype(F32)
+        for s in range(1, tp):
+            pairs = [(t, (t - s) % tp) for t in range(tp)]
+            total = total + lax.ppermute(pieces[s], "tp", pairs).astype(F32)
+        return total.astype(BF16)
+
+    def fold_near(near_values):
         for bit in reversed(range(ctx_bits - 1)):
-            halves = [fold_rows(h, bit) for h in halves]
-        if width_first:
-            halves = [fold_width(h) for h in halves]
-        total = add_low(halves[0], exchange(halves[1], "ctx", ctx, low_ctx))
-        if not width_first:
-            total = fold_width(total)
-        return fold_tp(split(total))
-
-    def split_even(total):
-        count = total.shape[0] // tp
-        return [total[s * count : (s + 1) * count] for s in range(tp)]
-
-    def split_qkv(total):
-        cut = [total[i * head_cols : (i + 1) * head_cols] for i in range(3 * tp)]
-        return [jnp.concatenate([cut[i * tp + s] for i in range(3)], 0) for s in range(tp)]
+            half = len(near_values) // 2
+            near_values = [
+                add_low(near_values[n], exchange(near_values[n + half], "ctx", ctx, 1 << bit))
+                for n in range(half)
+            ]
+        return near_values[0]
+
+    def join_halves(arrays):
+        if len(arrays) == 1:
+            return arrays[0]
+        tops = [a[: a.shape[0] // 2] for a in arrays]
+        return jnp.concatenate(tops + [a[a.shape[0] // 2 :] for a in arrays], 0)
 
     def join_ctx(share):
-        blocks = jnp.stack(spread_ctx(share, ctx_bits), 0)
+        blocks = share
+        for bit in range(ctx_bits):
+            blocks = jnp.concatenate([blocks, exchange(blocks, "ctx", ctx, 1 << bit)], 0)
+        blocks = blocks.reshape((ctx,) + share.shape)
         return reorder(blocks, at_ctx, ctx_bits, 0).astype(F32)
 
     grad_second, grad_gain_second, grad_shift_second = pull_second(grad_final.astype(F32))
     grad_mlp = grad_second.astype(BF16)
     grad_bias_out = jnp.sum(grad_mlp, 0, dtype=F32)
-    grad_pre, grad_out_halves, grad_in_halves = [], [], []
-    for h in range(2):
-        grad_out_halves.append(dot_tn(act_low[h], grad_mlp).astype(BF16))
-    share_out = sum_shares(grad_out_halves, False, split_even)
-    for h in range(2):
-        grad_pre.append((dot_nt(grad_mlp, out_weights[h]) * gelu_slope(pre_act[h])).astype(BF16))
+    with jax.named_scope("sum_out"):
+        sum_out = fold_near([dot_tn(a, grad_mlp).astype(BF16) for a in act_low])
+    grad_pre = [
+        (dot_nt(grad_mlp, out_weights[n]) * gelu_slope(pre_act[n])).astype(BF16)
+        for n in range(low_ctx)
+    ]
+    grad_pre, (sum_out, piece) = gate(grad_pre, (sum_out, next_output()))
+    keep_output(piece)
+    with jax.named_scope("sum_out"):
+        sum_out = fold_width(sum_out)
     grad_bias_in = jnp.stack([jnp.sum(g, 0, dtype=F32) for g in grad_pre])
-    grad_normed = grad_second + (dot_nn(grad_pre[0], in_weights[0]) + dot_nn(grad_pre[1], in_weights[1]))
+    with jax.named_scope("sum_in"):
+        grad_in = [dot_tn(g, normed_low).astype(BF16) for g in grad_pre]
+    grad_normed = grad_second
+    for n in range(low_ctx):
+        grad_normed = grad_normed + dot_nn(grad_pre[n], in_weights[n])
     grad_first, grad_gain_first, grad_shift_first = pull_first(grad_normed)
     grad_attn = grad_first.astype(BF16)
     grad_bias_attn = jnp.sum(grad_attn, 0, dtype=F32)
-    grad_attended = dot_nt(grad_attn, o_weights).astype(BF16)
-    grad_blocks = head_blocks(
-        [grad_attended[:, j * split_cols : (j + 1) * split_cols] for j in range(ctx)]
-    )
-    grad_mixed = to_sequences(grad_blocks)
-    for h in range(2):
-        grad_in_halves.append(dot_tn(grad_pre[h], normed_low).astype(BF16))
-    share_in = sum_shares(grad_in_halves, True, split_even)
-    grad_o = dot_tn(attended, grad_attn).astype(BF16)
-    half_o = grad_o.shape[0] // 2
-    share_o = sum_shares([grad_o[:half_o], grad_o[half_o:]], True, split_even)
-
-    grad_seq = jnp.concatenate(
-        attend_grad(query, grad_mixed, mixed, key, value, segs, lse, head_size), 2
-    )
-    grad_qkv = to_rows(grad_seq)
-    if not aligned:
-        parts = [
-            column_blocks([b[:, i * split_cols : (i + 1) * split_cols] for b in grad_qkv])
-            for i in range(3)
+    grad_attended = [dot_nt(grad_attn, o_weights[n]).astype(BF16) for n in range(low_ctx)]
+    grad_blocks = move_columns(by_block(grad_attended, group_cols), None if aligned else to_heads)
+    with jax.named_scope("to_sequences_grad"):
+        grad_mixed = to_sequences([jnp.concatenate(b, 1) for b in grad_blocks])
+    with jax.named_scope("sum_in"):
+        grad_o = [dot_tn(a, grad_attn).astype(BF16) for a in attended]
+        sum_in = fold_near([join_halves([i, o]) for i, o in zip(grad_in, grad_o)])
+    grad_mixed, (sum_out, sum_in, piece) = gate(grad_mixed, (sum_out, sum_in, next_output()))
+    keep_output(piece)
+    with jax.named_scope("sum_in"):
+        sum_in = fold_width(sum_in)
+    with jax.named_scope("sum_out"):
+        sum_out = fold_half(sum_out)
+
+    grad_qkv = [[] for _ in range(ctx)]
+    for g in range(groups):
+        parts, lse = heads_in[g]
+        if g == groups - 1:
+            parts, (sum_out, piece) = gate(parts, (sum_out, next_output()))
+            keep_output(piece)
+            with jax.named_scope("sum_out"):
+                share_out = fold_tp(cut(sum_out, hidden))
+        cols = slice(g * group_cols, (g + 1) * group_cols)
+        grads = attend_grad(
+            parts[0], grad_mixed[:, :, cols], mixed_parts[g], parts[1], parts[2], segs, lse, head_size
+        )
+        with jax.named_scope("to_rows_grad"):
+            for j, block in enumerate(to_rows(jnp.concatenate(grads, 2))):
+                grad_qkv[j].append(block)
+    while len(output_pieces) < tp:
+        output_pieces.append(next_output())
+    output = place_rows(output_pieces)
+    grad_qkv, (share_out, sum_in) = gate(grad_qkv, (share_out, sum_in))
+    with jax.named_scope("sum_in"):
+        sum_in = fold_half(sum_in)
+        in_rows = tp * hidden
+        in_cut, o_cut = cut(sum_in[:in_rows], hidden), cut(sum_in[in_rows:], head_cols)
+        share_in = fold_tp([jnp.concatenate([i, o], 0) for i, o in zip(in_cut, o_cut)])
+    with jax.named_scope("join_out_in"):
+        joined = join_ctx(jnp.concatenate([share_out, share_in], 0))
+        grad_w_out = joined[:, :hidden].reshape(ctx * hidden, width_part)
+        grad_w_in = joined[:, hidden : 2 * hidden].reshape(ctx * hidden, width_part).T
+        grad_w_o = joined[:, 2 * hidden :].reshape(ctx * head_cols, width_part)
+    grad_near = by_near(move_columns(grad_qkv, None if aligned else from_heads))
+    input_part = grad_first
+    for n in range(low_ctx):
+        input_part = input_part + dot_nn(grad_near[n], qkv_weights[n])
+    with jax.named_scope("share_grad_tokens"):
+        grad_tokens = place_rows(tp_pieces(turned_rows(input_part)))
+    with jax.named_scope("sum_qkv"):
+        total = fold_near([dot_tn(g, inputs).astype(BF16) for g in grad_near])
+        total = cut(fold_width(fold_half(total)), head_cols)
+        pieces = []
+        for s in range(tp):
+            at = (s // per_group) * 3 * per_group + s % per_group
+            pieces.append(jnp.concatenate([total[at + i * per_group] for i in range(3)], 0))
+        share_qkv = fold_tp(pieces)
+    with jax.named_scope("join_qkv"):
+        grad_w_qkv = join_ctx(share_qkv).reshape(ctx, 3, head_cols, width_part)
+        grad_w_qkv = grad_w_qkv.transpose(1, 3, 0, 2).reshape(3, width_part, ctx * head_cols)
+
+    def tp_order(values, axis):
+        moved = [
+            lax.dynamic_index_in_dim(values, (at_tp - t) % tp, axis, True) for t in range(tp)
         ]
-        grad_qkv = [jnp.concatenate([p[j] for p in parts], 1) for j in range(ctx)]
-    input_part = dot_nn(grad_qkv[0], qkv_weights[0])
-    for j in range(1, ctx):
-        input_part = input_part + dot_nn(grad_qkv[j], qkv_weights[j])
-    grad_tokens = share_rows(grad_first + input_part)
-    grad_qkv_w = [dot_tn(g, inputs).astype(BF16) for g in grad_qkv]
-
-    def sum_qkv(blocks):
-        total = [
-            add_low(blocks[j], exchange(blocks[j + low_ctx], "ctx", ctx, low_ctx))
-            for j in range(low_ctx)
-        ]
-        for bit in reversed(range(ctx_bits - 1)):
-            half = len(total) // 2
-            total = [
-                add_low(total[j], exchange(total[j + half], "ctx", ctx, 1 << bit))
-                for j in range(half)
-            ]
-        return fold_tp(split_qkv(fold_width(total[0])))
-
-    share_qkv = sum_qkv(grad_qkv_w)
-
-    def ctx_tp_order(values):
-        blocks = values.reshape(values.shape[0], ctx, tp, -1)
-        blocks = jnp.take(blocks, ctx_order, axis=1)
-        blocks = jnp.take(blocks, (at_tp - jnp.arange(tp)) % tp, axis=2)
-        return blocks.transpose(0, 2, 1, 3).reshape(values.shape[0], -1)
-
-    def total_sum(values):
-        for axis, size in (("ctx", ctx), ("fsdp", fsdp), ("tp", tp)):
-            for bit in range(size.bit_length() - 1):
-                values = values + exchange(values, axis, size, 1 << bit)
-        return values
+        return jnp.concatenate(moved, axis)
 
     small_sums = jnp.stack(
         [
@@ -524,35 +623,28 @@
             )
         ]
     )
-    hidden_sums = ctx_tp_order(grad_bias_in.reshape(1, -1)).reshape(-1, width)
-    small_sums = jnp.concatenate([reorder_width(small_sums), hidden_sums], 0)
-    small_sums = total_sum(small_sums)
-    width_start = at_fsdp * width_part
-    width_sums = lax.dynamic_slice_in_dim(small_sums[:6], width_start, width_part, 1)
-    hidden_own = lax.dynamic_slice_in_dim(
-        small_sums[6:].reshape(tp, b_in.shape[0], fsdp, b_in.shape[1]), at_tp, 1, 0
+    in_sums = grad_bias_in.reshape(low_ctx, 2, tp, hidden).transpose(1, 0, 2, 3)
+    in_sums = reorder(in_sums.reshape(ctx, tp, hidden), at_ctx, ctx_bits, 0)
+    in_sums = tp_order(in_sums.transpose(1, 0, 2), 0).reshape(-1, width)
+    qv_sums = jnp.stack([jnp.sum(g, 0, dtype=F32) for g in grad_near])
+    qv_sums = qv_sums.reshape(low_ctx, 2, groups, 3, per_group, head_cols)
+    qv_sums = qv_sums.transpose(3, 1, 0, 2, 4, 5).reshape(3, ctx, tp, head_cols)
+    qv_sums = reorder(jnp.stack([qv_sums[0], qv_sums[2]]), at_ctx, ctx_bits, 1)
+    qv_sums = tp_order(qv_sums.transpose(0, 2, 1, 3), 1).reshape(2, width)
+    small_sums = jnp.concatenate([reorder_width(small_sums), in_sums, qv_sums], 0)
+    with jax.named_scope("sum_small"):
+        for axis, size in (("ctx", ctx), ("fsdp", fsdp), ("tp", tp)):
+            for bit in range(size.bit_length() - 1):
+                small_sums = small_sums + exchange(small_sums, axis, size, 1 << bit)
+    width_sums = lax.dynamic_slice_in_dim(small_sums[:6], at_fsdp * width_part, width_part, 1)
+    hidden_own = lax.dynamic_index_in_dim(
+        small_sums[6:-2].reshape(tp, b_in.shape[0], fsdp, b_in.shape[1]), at_tp, 0, False
     )
-    grad_b_in = lax.dynamic_index_in_dim(hidden_own[0], at_fsdp, 1, False)
-    qv_sums = [
-        jnp.stack(
-            [
-                jnp.sum(g[:, i * split_cols : (i + 1) * split_cols], 0, dtype=F32)
-                for g in grad_qkv
-            ]
-        )
-        for i in (0, 2)
-    ]
-    qv_sums = total_sum(ctx_tp_order(jnp.stack(qv_sums).reshape(2, -1)))
+    grad_b_in = lax.dynamic_index_in_dim(hidden_own, at_fsdp, 1, False)
     qv_own = lax.dynamic_index_in_dim(
-        qv_sums.reshape(2, tp, head_count, fsdp, head_size // fsdp), at_tp, 1, False
+        small_sums[-2:].reshape(2, tp, head_count, fsdp, head_size // fsdp), at_tp, 1, False
     )
     grad_b_qv = lax.dynamic_index_in_dim(qv_own, at_fsdp, 2, False)
-
-    grad_w_qkv = join_ctx(share_qkv.reshape(3, head_cols, width_part))
-    grad_w_qkv = grad_w_qkv.transpose(1, 3, 0, 2).reshape(3, width_part, ctx * head_cols)
-    grad_w_o = join_ctx(share_o).reshape(ctx * head_cols, width_part)
-    grad_w_in = join_ctx(share_in).reshape(ctx * hidden, width_part).T
-    grad_w_out = join_ctx(share_out).reshape(ctx * hidden, width_part)
     return (
         output,
         grad_tokens,

time: 863 us -> 780 us (0.904)
  waiting for transfers between devices: 454 us -> 337 us
  local copies, waits for them, and re-layouts: 59.9 us -> 106 us
  matrix products: 115 us -> 86 us
  other arithmetic: 72.3 us -> 95.3 us
    ppermute x33 -> x15, waiting for transfers between devices: 199 us -> 86.2 us  [shift_tp(): return lax.ppermute(values, 'tp', [(i, (i + 1) % tp) for i in range(tp)])]
    ppermute x67 -> x47, waiting for transfers between devices: 255 us -> 189 us  [exchange(): return lax.ppermute(values, axis, [(i, i ^ j) for i in range(size)])]
    ppermute x0 -> x9, waiting for transfers between devices: none -> 61.9 us  [fold_tp(): total = total + lax.ppermute(pieces[s], 'tp', pairs).astype(F32)]
    unnamed x202 -> x235, local copies, waits for them, and re-layouts: 14 us -> 49.4 us
    dot_general x9 -> x8, matrix products: 49.6 us -> 32 us  [dot_nt(): lax.dot_general(left, right, CONTRACT_LAST, preferred_element_type=F32)]
    ppermute x67 -> x47, starting transfers between devices: 48.6 us -> 33.9 us  [exchange(): return lax.ppermute(values, axis, [(i, i ^ j) for i in range(size)])]
    concatenate x8 -> x17, other arithmetic: 12.1 us -> 25.8 us  [the longest x1 13.6 us: join_halves(): return jnp.concatenate(tops + [a[a.shape[0] // 2:] for a in arrays], 0)]
    ppermute x0 -> x9, starting transfers between devices: none -> 11.2 us  [fold_tp(): total = total + lax.ppermute(pieces[s], 'tp', pairs).astype(F32)]
  transfers between devices with their start and end apart: 100 -> 71, of which waited for: 47 -> 32; matrix products, arithmetic and copies ran while one was open for 18% -> 29% of each run, Pallas kernels for 10% -> 11%
where the time goes in v2:
time: 780 us; the launch traced here: 771 us
  waiting for transfers between devices  337 us (43%)
  local copies, waits for them, and re-layouts  106 us (14%)
  other arithmetic  95.3 us (12%)
  Pallas kernels  87.9 us (11%)
  matrix products  86 us (11%)
  starting transfers between devices  56.2 us (7%)
    ppermute x47, waiting for transfers between devices, exchange(): return lax.ppermute(values, axis, [(i, i ^ j) for i in range(size)])  189 us
    ppermute x15, waiting for transfers between devices, shift_tp(): return lax.ppermute(values, 'tp', [(i, (i + 1) % tp) for i in range(tp)])  86.2 us
    ppermute x9, waiting for transfers between devices, fold_tp(): total = total + lax.ppermute(pieces[s], 'tp', pairs).astype(F32)  61.9 us
    pallas_call x2, Pallas kernels, attend_grad(): pl.pallas_call(functools.partial(attend_grad_kernel, head_size), grid=(se...  54.5 us
    unnamed x235, local copies, waits for them, and re-layouts  49.4 us
    ppermute x47, starting transfers between devices, exchange(): return lax.ppermute(values, axis, [(i, i ^ j) for i in range(size)])  33.9 us
    pallas_call x2, Pallas kernels, attend(): pl.pallas_call(functools.partial(attend_kernel, head_size), grid=(seq_cou...  33.3 us
    dot_general x8, matrix products, dot_nt(): lax.dot_general(left, right, CONTRACT_LAST, preferred_element_type=F32)  32 us
  transfers between devices with their start and end apart: 71, of which 32 were waited for; matrix products, arithmetic and copies ran while one was open for 29% of the time, Pallas kernels for 11%

profile of v2, /device:TPU:0, one launch (start us, length us, event | category | flops | bytes accessed | tf_op | source)
XLA Modules:
  0.0 770.6 jit_solution(817787786862033539)
XLA Ops:
  16.5 22.4 %collective-permute-done.23 = bf16[256,512]{0,1:T(8,128)(2,1)S(1)} collective-permute-done((bf16[256,512]{0,1:T(8,128)(2,1)S(1)}, bf16[256,512]{0,1:T(8,128)(2,1)S(1)}, u32[]{:S(2)}, u32[]{:S(2)}) %collective-permute-start.23) | collective-permute-done | bytes 262176 | tf_op jit(solution)/shard_map/get_in/ppermute | solution.py:226
  42.7 7.2 collective-permute-done.24
  53.1 5.6 collective-permute-done.2
  67.0 18.4 %collective-permute-done.3 = bf16[400,512]{1,0:T(8,128)(2,1)S(1)} collective-permute-done((bf16[400,512]{1,0:T(8,128)(2,1)S(1)}, bf16[400,512]{1,0:T(8,128)(2,1)S(1)}, u32[]{:S(2)}, u32[]{:S(2)}) %collective-permute-start.3) | collective-permute-done | bytes 409632 | tf_op jit(solution)/shard_map/get_qkv/ppermute | solution.py:226
  102.3 10.2 %collective-permute-done.16 = bf16[640,512]{1,0:T(8,128)(2,1)S(1)} collective-permute-done((bf16[640,512]{1,0:T(8,128)(2,1)}, bf16[640,512]{1,0:T(8,128)(2,1)S(1)}, u32[]{:S(2)}, u32[]{:S(2)}) %collective-permute-start.16) | collective-permute-done | bytes 655392 | tf_op jit(solution)/shard_map/get_out/ppermute | solution.py:226
  153.6 29.4 %collective-permute-done.17 = bf16[2560,512]{1,0:T(8,128)(2,1)} collective-permute-done((bf16[2560,512]{1,0:T(8,128)(2,1)}, bf16[2560,512]{1,0:T(8,128)(2,1)}, u32[]{:S(2)}, u32[]{:S(2)}) %collective-permute-start.17) | collective-permute-done | bytes 2621472 | tf_op jit(solution)/shard_map/get_out/ppermute | solution.py:223
  183.0 5.6 pad_maximum_fusion
  194.4 7.4 pad_maximum_fusion.2
  206.1 16.7 %attend.3 = (bf16[1,2048,128]{2,1,0:T(8,128)(2,1)S(1)}, f32[1,1,8,2048]{3,2,1,0:T(8,128)S(1)}) custom-call(bf16[1,2048,128]{2,1,0:T(8,128)(2,1)S(1)} %get-tuple-element.61.q_ref, bf16[1,2048,128]{2,1,0:T(8,128)(2,1)S(1)} %get-tuple-element.62.k_ref, bf16[1,2048,128]{2,1,0:T(8,128)(2,1)S(1)} %get-tuple-element.63.v_ref, ...), custom_call_target="tpu_custom_call" | custom-call | flops 2147483648 | bytes 2097152 | tf_op jit(solution)/shard_map/attend/pallas_call | solution.py:79
  225.0 16.7 %attend.2 = (bf16[1,2048,128]{2,1,0:T(8,128)(2,1)S(1)}, f32[1,1,8,2048]{3,2,1,0:T(8,128)S(1)}) custom-call(bf16[1,2048,128]{2,1,0:T(8,128)(2,1)S(1)} %get-tuple-element.154.q_ref, bf16[1,2048,128]{2,1,0:T(8,128)(2,1)S(1)} %get-tuple-element.153.k_ref, bf16[1,2048,128]{2,1,0:T(8,128)(2,1)S(1)} %get-tuple-element.152.v_ref, ...), custom_call_target="tpu_custom_call" | custom-call | flops 2147483648 | bytes 2097152 | tf_op jit(solution)/shard_map/attend/pallas_call | solution.py:79
  245.1 5.0 collective-permute-done.20
  265.7 5.3 fusion.82
  295.6 5.4 fusion.5
  301.1 6.1 fusion.11
  307.2 5.4 add_convert_fusion.1
  312.7 9.8 %collective-permute-done.30 = bf16[1,512,1024]{2,1,0:T(8,128)(2,1)S(1)} collective-permute-done((bf16[1,512,1024]{2,1,0:T(8,128)(2,1)S(1)}, bf16[1,512,1024]{2,1,0:T(8,128)(2,1)S(1)}, u32[]{:S(2)}, u32[]{:S(2)}) %collective-permute-start.30) | collective-permute-done | bytes 1048608 | tf_op jit(solution)/shard_map/share_output/ppermute | solution.py:226
  336.1 13.6 %pad_maximum_fusion.1 = bf16[2560,1024]{1,0:T(8,128)(2,1)} fusion(bf16[256,1024]{1,0:T(8,128)(2,1)S(1)} %get-tuple-element.186, bf16[1024,1024]{1,0:T(8,128)(2,1)S(1)} %get-tuple-element.136, bf16[256,1024]{1,0:T(8,128)(2,1)S(1)} %get-tuple-element.185, bf16[1024,1024]{1,0:T(8,128)(2,1)S(1)} %get-tuple-element.135), kind=kLoop, calls=%fused_computation.10 | loop fusion | flops 20971520 | bytes 10485760 | tf_op jit(solution)/shard_map/sum_in/concatenate | solution.py:515
  372.7 25.6 %collective-permute-done.34 = bf16[2048,512]{1,0:T(8,128)(2,1)} collective-permute-done((bf16[2048,512]{1,0:T(8,128)(2,1)S(1)}, bf16[2048,512]{1,0:T(8,128)(2,1)}, u32[]{:S(2)}, u32[]{:S(2)}) %collective-permute-start.34) | collective-permute-done | bytes 2097184 | tf_op jit(solution)/shard_map/sum_out/ppermute | solution.py:223
  400.6 14.4 %add_convert_fusion = bf16[2560,1024]{1,0:T(8,128)(2,1)S(1)} fusion(bf16[2560,1024]{1,0:T(8,128)(2,1)} %collective-permute-done.35, bf16[256,1024]{1,0:T(8,128)(2,1)S(1)} %get-tuple-element.184, bf16[1024,1024]{1,0:T(8,128)(2,1)S(1)} %get-tuple-element.134, bf16[256,1024]{1,0:T(8,128)(2,1)S(1)} %get-tuple-element.183, bf16[1024,1024]{1,0:T(8,128)(2,1)S(1)} %get-tuple-element.133), kind=kLoop, calls=%fused_computation | loop fusion | flops 28835840 | bytes 15728640 | tf_op jit(solution)/shard_map/sum_in/convert_element_type | solution.py:483
  420.7 27.2 %attend_grad.2 = (bf16[1,2048,128]{2,1,0:T(8,128)(2,1)}, bf16[1,2048,128]{2,1,0:T(8,128)(2,1)}, bf16[1,2048,128]{2,1,0:T(8,128)(2,1)}) custom-call(bf16[1,2048,128]{2,1,0:T(8,128)(2,1)} %copy-done.10, bf16[1,2048,128]{2,1,0:T(8,128)(2,1)} %get-tuple-element.182.do_ref, bf16[1,2048,128]{2,1,0:T(8,128)(2,1)} %copy-done.4, bf16[1,2048,128]{2,1,0:T(8,128)(2,1)} %copy-done.9, ...), custom_call_target="tpu_custom_call" | custom-call | flops 5368709120 | bytes 4194304 | tf_op jit(solution)/shard_map/attend_grad/pallas_call | solution.py:161
  459.6 27.3 %attend_grad.3 = (bf16[1,2048,128]{2,1,0:T(8,128)(2,1)}, bf16[1,2048,128]{2,1,0:T(8,128)(2,1)}, bf16[1,2048,128]{2,1,0:T(8,128)(2,1)}) custom-call(bf16[1,2048,128]{2,1,0:T(8,128)(2,1)} %copy-done.7, bf16[1,2048,128]{2,1,0:T(8,128)(2,1)} %get-tuple-element.181.do_ref, bf16[1,2048,128]{2,1,0:T(8,128)(2,1)} %copy-done.3, bf16[1,2048,128]{2,1,0:T(8,128)(2,1)} %copy-done.6, ...), custom_call_target="tpu_custom_call" | custom-call | flops 5368709120 | bytes 4194304 | tf_op jit(solution)/shard_map/attend_grad/pallas_call | solution.py:161
  503.5 6.9 collective-permute-done.43
  510.4 10.0 %collective-permute-done.42 = bf16[512,384]{1,0:T(8,128)(2,1)S(1)} collective-permute-done((bf16[512,384]{1,0:T(8,128)(2,1)S(1)}, bf16[512,384]{1,0:T(8,128)(2,1)S(1)}, u32[]{:S(2)}, u32[]{:S(2)}) %collective-permute-start.42) | collective-permute-done | bytes 393248 | tf_op jit(solution)/shard_map/to_rows_grad/ppermute | solution.py:223
  520.3 6.4 collective-permute-done.44
  554.2 10.6 %collective-permute-done.65 = bf16[1280,512]{1,0:T(8,128)(2,1)} collective-permute-done((bf16[1280,512]{1,0:T(8,128)(2,1)}, bf16[1280,512]{1,0:T(8,128)(2,1)}, u32[]{:S(2)}, u32[]{:S(2)}) %collective-permute-start.65) | collective-permute-done | bytes 1310752 | tf_op jit(solution)/shard_map/sum_in/ppermute | solution.py:223
  571.2 8.4 %collective-permute-done.49 = bf16[1,512,1024]{2,1,0:T(8,128)(2,1)} collective-permute-done((bf16[1,512,1024]{2,1,0:T(8,128)(2,1)S(1)}, bf16[1,512,1024]{2,1,0:T(8,128)(2,1)}, u32[]{:S(2)}, u32[]{:S(2)}) %collective-permute-start.49) | collective-permute-done | bytes 1048608 | tf_op jit(solution)/shard_map/share_grad_tokens/ppermute | solution.py:226
  580.3 5.2 collective-permute-done.66
  585.5 43.5 %collective-permute-done.67 = bf16[320,512]{1,0:T(8,128)(2,1)S(1)} collective-permute-done((bf16[320,512]{1,0:T(8,128)(2,1)S(1)}, bf16[320,512]{1,0:T(8,128)(2,1)S(1)}, u32[]{:S(2)}, u32[]{:S(2)}) %collective-permute-start.67) | collective-permute-done | bytes 327712 | tf_op jit(solution)/shard_map/sum_in/ppermute | solution.py:499
  640.5 34.8 %collective-permute-done.61 = f32[12,1024]{1,0:T(8,128)S(1)} collective-permute-done((f32[12,1024]{1,0:T(8,128)S(1)}, f32[12,1024]{1,0:T(8,128)S(1)}, u32[]{:S(2)}, u32[]{:S(2)}) %collective-permute-start.61) | collective-permute-done | bytes 49184 | tf_op jit(solution)/shard_map/sum_small/ppermute | solution.py:223
  688.7 21.4 %collective-permute-done.64 = f32[12,1024]{1,0:T(8,128)S(1)} collective-permute-done((f32[12,1024]{1,0:T(8,128)S(1)}, f32[12,1024]{1,0:T(8,128)S(1)}, u32[]{:S(2)}, u32[]{:S(2)}) %collective-permute-start.64) | collective-permute-done | bytes 49184 | tf_op jit(solution)/shard_map/sum_small/ppermute | solution.py:223
  723.1 15.0 %collective-permute-done.54 = bf16[768,512]{1,0:T(8,128)(2,1)S(1)} collective-permute-done((bf16[768,512]{1,0:T(8,128)(2,1)S(1)}, bf16[768,512]{1,0:T(8,128)(2,1)S(1)}, u32[]{:S(2)}, u32[]{:S(2)}) %collective-permute-start.54) | collective-permute-done | bytes 786464 | tf_op jit(solution)/shard_map/sum_qkv/ppermute | solution.py:223
  745.7 8.6 %collective-permute-done.56 = bf16[192,512]{1,0:T(8,128)(2,1)S(1)} collective-permute-done((bf16[192,512]{1,0:T(8,128)(2,1)S(1)}, bf16[192,512]{1,0:T(8,128)(2,1)S(1)}, u32[]{:S(2)}, u32[]{:S(2)}) %collective-permute-start.56) | collective-permute-done | bytes 196640 | tf_op jit(solution)/shard_map/sum_qkv/ppermute | solution.py:499
  (604 shorter events, 312.0 us)
Async XLA Ops:
  4.5 48.5 %collective-permute-start.14 = (bf16[640,512]{1,0:T(8,128)(2,1)}, bf16[640,512]{1,0:T(8,128)(2,1)}, u32[]{:S(2)}, u32[]{:S(2)}) collective-permute-start(bf16[640,512]{1,0:T(8,128)(2,1)} %pad_maximum_fusion.14), channel_id=1, source_target_pairs={{0,1},{1,2},{2,3},{3,0},{4,5},{5,6},{6,7},{7,4},{8,9},{9,10},{10,1... | collective-permute-start | bytes 1966088 | tf_op jit(solution)/shard_map/get_out/ppermute | solution.py:226
  41.2 45.6 %collective-permute-start.1 = (bf16[800,512]{1,0:T(8,128)(2,1)}, bf16[800,512]{1,0:T(8,128)(2,1)}, u32[]{:S(2)}, u32[]{:S(2)}) collective-permute-start(bf16[800,512]{1,0:T(8,128)(2,1)} %pad_maximum_fusion.11), channel_id=1, source_target_pairs={{0,16},{16,0},{1,17},{17,1},{2,18},{18,2},{3,19},{19,3},{4,20},{20... | collective-permute-start | bytes 2457608 | tf_op jit(solution)/shard_map/get_qkv/ppermute | solution.py:223
  53.0 42.9 %collective-permute-start.15 = (bf16[640,512]{1,0:T(8,128)(2,1)}, bf16[640,512]{1,0:T(8,128)(2,1)}, u32[]{:S(2)}, u32[]{:S(2)}) collective-permute-start(bf16[640,512]{1,0:T(8,128)(2,1)} %collective-permute-done.14), channel_id=1, source_target_pairs={{0,1},{1,2},{2,3},{3,0},{4,5},{5,6},{6,7},{7,4},{8,9},{9,10},{10,1... | collective-permute-start | bytes 1966088 | tf_op jit(solution)/shard_map/get_out/ppermute | solution.py:226
  65.4 32.6 %collective-permute-start.26 = (bf16[1024,512]{0,1:T(8,128)(2,1)}, bf16[1024,512]{0,1:T(8,128)(2,1)}, u32[]{:S(2)}, u32[]{:S(2)}) collective-permute-start(bf16[1024,512]{0,1:T(8,128)(2,1)} %pad_maximum_fusion.9), channel_id=1, source_target_pairs={{0,16},{16,0},{1,17},{17,1},{2,18},{18,2},{3,19},{19,3},{4,20},{20... | collective-permute-start | bytes 3145736 | tf_op jit(solution)/shard_map/get_in/ppermute | solution.py:223
  85.4 42.4 %collective-permute-start.4 = (bf16[800,512]{1,0:T(8,128)(2,1)S(1)}, bf16[800,512]{1,0:T(8,128)(2,1)S(1)}, u32[]{:S(2)}, u32[]{:S(2)}) collective-permute-start(bf16[800,512]{1,0:T(8,128)(2,1)S(1)} %constant_dynamic-update-slice_fusion), channel_id=1, source_target_pairs={{0,16},{16,0},{1,17},{17,1},{2,18},{18,2},{3,19},{19,3},{4,20},{20... | collective-permute-start | bytes 2457608 | tf_op jit(solution)/shard_map/get_qkv/ppermute | solution.py:223
  100.8 92.4 %collective-permute-start.27 = (bf16[1024,1024]{0,1:T(8,128)(2,1)}, bf16[1024,1024]{0,1:T(8,128)(2,1)}, u32[]{:S(2)}, u32[]{:S(2)}) collective-permute-start(bf16[1024,1024]{0,1:T(8,128)(2,1)} %pad_maximum_fusion.4), channel_id=1, source_target_pairs={{0,8},{4,12},{8,0},{12,4},{1,9},{5,13},{9,1},{13,5},{2,10},{6,14},... | collective-permute-start | bytes 6291464 | tf_op jit(solution)/shard_map/get_in/ppermute | solution.py:223
  126.8 56.1 %collective-permute-start.17 = (bf16[2560,512]{1,0:T(8,128)(2,1)}, bf16[2560,512]{1,0:T(8,128)(2,1)}, u32[]{:S(2)}, u32[]{:S(2)}) collective-permute-start(bf16[2560,512]{1,0:T(8,128)(2,1)} %slice_dynamic-update-slice_fusion), channel_id=1, source_target_pairs={{0,16},{16,0},{1,17},{17,1},{2,18},{18,2},{3,19},{19,3},{4,20},{20... | collective-permute-start | bytes 7864328 | tf_op jit(solution)/shard_map/get_out/ppermute | solution.py:223
  145.9 42.8 %collective-permute-start.5 = (bf16[1536,1024]{1,0:T(8,128)(2,1)}, bf16[1536,1024]{1,0:T(8,128)(2,1)}, u32[]{:S(2)}, u32[]{:S(2)}) collective-permute-start(bf16[1536,1024]{1,0:T(8,128)(2,1)} %fusion.60), channel_id=1, source_target_pairs={{0,4},{4,0},{8,12},{12,8},{1,5},{5,1},{9,13},{13,9},{2,6},{6,2},{1... | collective-permute-start | bytes 9437192 | tf_op jit(solution)/shard_map/get_qkv/ppermute | solution.py:223
  151.1 50.7 %collective-permute-start.10 = (bf16[512,384]{1,0:T(8,128)(2,1)}, bf16[512,384]{1,0:T(8,128)(2,1)S(1)}, u32[]{:S(2)}, u32[]{:S(2)}) collective-permute-start(bf16[512,384]{1,0:T(8,128)(2,1)} %get-tuple-element.156), channel_id=1, source_target_pairs={{0,8},{4,12},{8,0},{12,4},{1,9},{5,13},{9,1},{13,5},{2,10},{6,14},... | collective-permute-start | bytes 1179656 | tf_op jit(solution)/shard_map/to_sequences/ppermute | solution.py:223
  152.2 70.6 %collective-permute-start.7 = (bf16[512,384]{1,0:T(8,128)(2,1)}, bf16[512,384]{1,0:T(8,128)(2,1)}, u32[]{:S(2)}, u32[]{:S(2)}) collective-permute-start(bf16[512,384]{1,0:T(8,128)(2,1)} %get-tuple-element.158), channel_id=1, source_target_pairs={{0,8},{4,12},{8,0},{12,4},{1,9},{5,13},{9,1},{13,5},{2,10},{6,14},... | collective-permute-start | bytes 1179656 | tf_op jit(solution)/shard_map/to_sequences/ppermute | solution.py:223
  188.6 69.6 %collective-permute-start.22 = (bf16[2560,1024]{1,0:T(8,128)(2,1)}, bf16[2560,1024]{1,0:T(8,128)(2,1)}, u32[]{:S(2)}, u32[]{:S(2)}) collective-permute-start(bf16[2560,1024]{1,0:T(8,128)(2,1)} %pad_maximum_fusion), channel_id=1, source_target_pairs={{0,4},{4,0},{8,12},{12,8},{1,5},{5,1},{9,13},{13,9},{2,6},{6,2},{1... | collective-permute-start | bytes 15728648 | tf_op jit(solution)/shard_map/get_out/ppermute | solution.py:223
  201.8 69.2 %collective-permute-start.28 = (bf16[2048,1024]{0,1:T(8,128)(2,1)S(1)}, bf16[2048,1024]{0,1:T(8,128)(2,1)S(1)}, u32[]{:S(2)}, u32[]{:S(2)}) collective-permute-start(bf16[2048,1024]{0,1:T(8,128)(2,1)S(1)} %pad_maximum_fusion.2), channel_id=1, source_target_pairs={{0,4},{4,0},{8,12},{12,8},{1,5},{5,1},{9,13},{13,9},{2,6},{6,2},{1... | collective-permute-start | bytes 12582920 | tf_op jit(solution)/shard_map/get_in/ppermute | solution.py:223
  349.8 50.9 %collective-permute-start.35 = (bf16[2560,1024]{1,0:T(8,128)(2,1)}, bf16[2560,1024]{1,0:T(8,128)(2,1)}, u32[]{:S(2)}, u32[]{:S(2)}) collective-permute-start(bf16[2560,1024]{1,0:T(8,128)(2,1)} %pad_maximum_fusion.1), channel_id=1, source_target_pairs={{0,4},{4,0},{8,12},{12,8},{1,5},{5,1},{9,13},{13,9},{2,6},{6,2},{1... | collective-permute-start | bytes 15728648 | tf_op jit(solution)/shard_map/sum_in/ppermute | solution.py:223
  350.0 48.2 %collective-permute-start.34 = (bf16[2048,512]{1,0:T(8,128)(2,1)S(1)}, bf16[2048,512]{1,0:T(8,128)(2,1)}, u32[]{:S(2)}, u32[]{:S(2)}) collective-permute-start(bf16[2048,512]{1,0:T(8,128)(2,1)S(1)} %slice.818), channel_id=1, source_target_pairs={{0,16},{16,0},{1,17},{17,1},{2,18},{18,2},{3,19},{19,3},{4,20},{20... | collective-permute-start | bytes 6291464 | tf_op jit(solution)/shard_map/sum_out/ppermute | solution.py:223
  371.1 44.0 %collective-permute-start.36 = (bf16[1,512,1024]{2,1,0:T(8,128)(2,1)S(1)}, bf16[1,512,1024]{2,1,0:T(8,128)(2,1)}, u32[]{:S(2)}, u32[]{:S(2)}) collective-permute-start(bf16[1,512,1024]{2,1,0:T(8,128)(2,1)S(1)} %copy-done.58), channel_id=1, source_target_pairs={{0,1},{1,2},{2,3},{3,0},{4,5},{5,6},{6,7},{7,4},{8,9},{9,10},{10,1... | collective-permute-start | bytes 3145736 | tf_op jit(solution)/shard_map/share_output/ppermute | solution.py:226
  416.9 78.5 %collective-permute-start.48 = (bf16[2560,512]{1,0:T(8,128)(2,1)}, bf16[2560,512]{1,0:T(8,128)(2,1)}, u32[]{:S(2)}, u32[]{:S(2)}) collective-permute-start(bf16[2560,512]{1,0:T(8,128)(2,1)} %slice.844), channel_id=1, source_target_pairs={{0,16},{16,0},{1,17},{17,1},{2,18},{18,2},{3,19},{19,3},{4,20},{20... | collective-permute-start | bytes 7864328 | tf_op jit(solution)/shard_map/sum_in/ppermute | solution.py:223
  418.4 34.1 %collective-permute-start.37 = (bf16[1024,512]{1,0:T(8,128)(2,1)}, bf16[1024,512]{1,0:T(8,128)(2,1)}, u32[]{:S(2)}, u32[]{:S(2)}) collective-permute-start(bf16[1024,512]{1,0:T(8,128)(2,1)} %slice.828), channel_id=1, source_target_pairs={{0,8},{4,12},{8,0},{12,4},{1,9},{5,13},{9,1},{13,5},{2,10},{6,14},... | collective-permute-start | bytes 3145736 | tf_op jit(solution)/shard_map/sum_out/ppermute | solution.py:223
  419.6 34.4 %collective-permute-start.38 = (bf16[1,512,1024]{2,1,0:T(8,128)(2,1)}, bf16[1,512,1024]{2,1,0:T(8,128)(2,1)}, u32[]{:S(2)}, u32[]{:S(2)}) collective-permute-start(bf16[1,512,1024]{2,1,0:T(8,128)(2,1)} %collective-permute-done.36), channel_id=1, source_target_pairs={{0,1},{1,2},{2,3},{3,0},{4,5},{5,6},{6,7},{7,4},{8,9},{9,10},{10,1... | collective-permute-start | bytes 3145736 | tf_op jit(solution)/shard_map/share_output/ppermute | solution.py:226
  452.5 42.0 %collective-permute-start.39 = (bf16[512,384]{1,0:T(8,128)(2,1)S(1)}, bf16[512,384]{1,0:T(8,128)(2,1)}, u32[]{:S(2)}, u32[]{:S(2)}) collective-permute-start(bf16[512,384]{1,0:T(8,128)(2,1)S(1)} %get-tuple-element.150), channel_id=1, source_target_pairs={{0,4},{4,0},{8,12},{12,8},{1,5},{5,1},{9,13},{13,9},{2,6},{6,2},{1... | collective-permute-start | bytes 1179656 | tf_op jit(solution)/shard_map/to_rows_grad/ppermute | solution.py:223
  455.1 36.2 %collective-permute-start.45 = (bf16[256,512]{1,0:T(8,128)(2,1)S(1)}, bf16[256,512]{1,0:T(8,128)(2,1)S(1)}, u32[]{:S(2)}, u32[]{:S(2)}) collective-permute-start(bf16[256,512]{1,0:T(8,128)(2,1)S(1)} %get-tuple-element.178), channel_id=1, source_target_pairs={{0,3},{1,0},{2,1},{3,2},{4,7},{5,4},{6,5},{7,6},{8,11},{9,8},{10,9... | collective-permute-start | bytes 786440 | tf_op jit(solution)/shard_map/sum_out/ppermute | solution.py:499
  458.9 33.2 %collective-permute-start.46 = (bf16[256,512]{1,0:T(8,128)(2,1)S(1)}, bf16[256,512]{1,0:T(8,128)(2,1)S(1)}, u32[]{:S(2)}, u32[]{:S(2)}) collective-permute-start(bf16[256,512]{1,0:T(8,128)(2,1)S(1)} %get-tuple-element.180), channel_id=1, source_target_pairs={{0,2},{1,3},{2,0},{3,1},{4,6},{5,7},{6,4},{7,5},{8,10},{9,11},{10,... | collective-permute-start | bytes 786440 | tf_op jit(solution)/shard_map/sum_out/ppermute | solution.py:499
  458.9 33.7 %collective-permute-start.47 = (bf16[256,512]{1,0:T(8,128)(2,1)S(1)}, bf16[256,512]{1,0:T(8,128)(2,1)S(1)}, u32[]{:S(2)}, u32[]{:S(2)}) collective-permute-start(bf16[256,512]{1,0:T(8,128)(2,1)S(1)} %get-tuple-element.179), channel_id=1, source_target_pairs={{0,1},{1,2},{2,3},{3,0},{4,5},{5,6},{6,7},{7,4},{8,9},{9,10},{10,1... | collective-permute-start | bytes 786440 | tf_op jit(solution)/shard_map/sum_out/ppermute | solution.py:499
  532.9 31.8 %collective-permute-start.65 = (bf16[1280,512]{1,0:T(8,128)(2,1)}, bf16[1280,512]{1,0:T(8,128)(2,1)}, u32[]{:S(2)}, u32[]{:S(2)}) collective-permute-start(bf16[1280,512]{1,0:T(8,128)(2,1)} %slice.891), channel_id=1, source_target_pairs={{0,8},{4,12},{8,0},{12,4},{1,9},{5,13},{9,1},{13,5},{2,10},{6,14},... | collective-permute-start | bytes 3932168 | tf_op jit(solution)/shard_map/sum_in/ppermute | solution.py:223
  533.9 96.3 %collective-permute-start.52 = (bf16[1536,1024]{1,0:T(8,128)(2,1)}, bf16[1536,1024]{1,0:T(8,128)(2,1)}, u32[]{:S(2)}, u32[]{:S(2)}) collective-permute-start(bf16[1536,1024]{1,0:T(8,128)(2,1)} %convolution_convert_fusion), channel_id=1, source_target_pairs={{0,4},{4,0},{8,12},{12,8},{1,5},{5,1},{9,13},{13,9},{2,6},{6,2},{1... | collective-permute-start | bytes 9437192 | tf_op jit(solution)/shard_map/sum_qkv/ppermute | solution.py:223
  569.9 59.2 %collective-permute-start.67 = (bf16[320,512]{1,0:T(8,128)(2,1)S(1)}, bf16[320,512]{1,0:T(8,128)(2,1)S(1)}, u32[]{:S(2)}, u32[]{:S(2)}) collective-permute-start(bf16[320,512]{1,0:T(8,128)(2,1)S(1)} %pad_maximum_fusion.20), channel_id=1, source_target_pairs={{0,2},{1,3},{2,0},{3,1},{4,6},{5,7},{6,4},{7,5},{8,10},{9,11},{10,... | collective-permute-start | bytes 983048 | tf_op jit(solution)/shard_map/sum_in/ppermute | solution.py:499
  570.5 58.5 %collective-permute-start.68 = (bf16[320,512]{1,0:T(8,128)(2,1)S(1)}, bf16[320,512]{1,0:T(8,128)(2,1)S(1)}, u32[]{:S(2)}, u32[]{:S(2)}) collective-permute-start(bf16[320,512]{1,0:T(8,128)(2,1)S(1)} %pad_maximum_fusion.21), channel_id=1, source_target_pairs={{0,1},{1,2},{2,3},{3,0},{4,5},{5,6},{6,7},{7,4},{8,9},{9,10},{10,1... | collective-permute-start | bytes 983048 | tf_op jit(solution)/shard_map/sum_in/ppermute | solution.py:499
  579.6 104.5 %collective-permute-start.50 = (bf16[1,512,1024]{2,1,0:T(8,128)(2,1)}, bf16[1,512,1024]{2,1,0:T(8,128)(2,1)}, u32[]{:S(2)}, u32[]{:S(2)}) collective-permute-start(bf16[1,512,1024]{2,1,0:T(8,128)(2,1)} %collective-permute-done.49), channel_id=1, source_target_pairs={{0,1},{1,2},{2,3},{3,0},{4,5},{5,6},{6,7},{7,4},{8,9},{9,10},{10,1... | collective-permute-start | bytes 3145736 | tf_op jit(solution)/shard_map/share_grad_tokens/ppermute | solution.py:226
  630.2 54.0 %collective-permute-start.69 = (bf16[576,512]{1,0:T(8,128)(2,1)}, bf16[576,512]{1,0:T(8,128)(2,1)S(1)}, u32[]{:S(2)}, u32[]{:S(2)}) collective-permute-start(bf16[576,512]{1,0:T(8,128)(2,1)} %get-tuple-element.212), channel_id=1, source_target_pairs={{0,4},{4,0},{8,12},{12,8},{1,5},{5,1},{9,13},{13,9},{2,6},{6,2},{1... | collective-permute-start | bytes 1769480 | tf_op jit(solution)/shard_map/join_out_in/ppermute | solution.py:223
  636.9 79.9 %collective-permute-start.53 = (bf16[768,1024]{1,0:T(8,128)(2,1)}, bf16[768,1024]{1,0:T(8,128)(2,1)}, u32[]{:S(2)}, u32[]{:S(2)}) collective-permute-start(bf16[768,1024]{1,0:T(8,128)(2,1)} %slice.1042), channel_id=1, source_target_pairs={{0,8},{4,12},{8,0},{12,4},{1,9},{5,13},{9,1},{13,5},{2,10},{6,14},... | collective-permute-start | bytes 4718600 | tf_op jit(solution)/shard_map/sum_qkv/ppermute | solution.py:223
  639.7 35.7 %collective-permute-start.61 = (f32[12,1024]{1,0:T(8,128)S(1)}, f32[12,1024]{1,0:T(8,128)S(1)}, u32[]{:S(2)}, u32[]{:S(2)}) collective-permute-start(f32[12,1024]{1,0:T(8,128)S(1)} %add.389), channel_id=1, source_target_pairs={{0,8},{4,12},{8,0},{12,4},{1,9},{5,13},{9,1},{13,5},{2,10},{6,14},... | collective-permute-start | bytes 147464 | tf_op jit(solution)/shard_map/sum_small/ppermute | solution.py:223
  684.1 36.5 %collective-permute-start.51 = (bf16[1,512,1024]{2,1,0:T(8,128)(2,1)}, bf16[1,512,1024]{2,1,0:T(8,128)(2,1)}, u32[]{:S(2)}, u32[]{:S(2)}) collective-permute-start(bf16[1,512,1024]{2,1,0:T(8,128)(2,1)} %collective-permute-done.50), channel_id=1, source_target_pairs={{0,1},{1,2},{2,3},{3,0},{4,5},{5,6},{6,7},{7,4},{8,9},{9,10},{10,1... | collective-permute-start | bytes 3145736 | tf_op jit(solution)/shard_map/share_grad_tokens/ppermute | solution.py:226
  685.3 37.6 %collective-permute-start.70 = (bf16[1152,512]{1,0:T(8,128)(2,1)}, bf16[1152,512]{1,0:T(8,128)(2,1)S(1)}, u32[]{:S(2)}, u32[]{:S(2)}) collective-permute-start(bf16[1152,512]{1,0:T(8,128)(2,1)} %pad_maximum_fusion.8), channel_id=1, source_target_pairs={{0,8},{4,12},{8,0},{12,4},{1,9},{5,13},{9,1},{13,5},{2,10},{6,14},... | collective-permute-start | bytes 3538952 | tf_op jit(solution)/shard_map/join_out_in/ppermute | solution.py:223
  (134 other events, 2054.1 us)

commit v3 on v2

--- a/solution.py
+++ b/solution.py
@@ -1,4 +1,6 @@
 import functools
+import itertools
+import math
 
 import jax
 import jax.numpy as jnp
@@ -46,9 +48,52 @@
     return jnp.dot(left, right, preferred_element_type=F32)
 
 
-def attend_kernel(head_size, q_ref, k_ref, v_ref, sq_ref, sk_ref, o_ref, lse_ref):
+def assemble(arrays, plan, shapes, name):
+    def kernel(*refs):
+        ins, outs = refs[: len(arrays)], refs[len(arrays) :]
+        for out, row, col, count, wide, sources in plan:
+            step = math.gcd(count, 64)
+
+            def body(i, carry, out=out, row=row, col=col, wide=wide, sources=sources, step=step):
+                offset = i * step
+                parts = []
+                for source, at_row, at_col in sources:
+                    start = pl.multiple_of(at_row + offset, 16)
+                    parts.append(ins[source][pl.ds(start, step), at_col : at_col + wide])
+                value = parts[0]
+                if len(parts) > 1:
+                    value = sum(p.astype(F32) for p in parts).astype(BF16)
+                outs[out][pl.ds(pl.multiple_of(row + offset, 16), step), col : col + wide] = value
+                return carry
+
+            lax.fori_loop(0, count // step, body, 0)
+
+    size = sum(a.size for a in arrays) + sum(r * c for r, c in shapes)
+    return pl.pallas_call(
+        kernel,
+        in_specs=[pl.BlockSpec(memory_space=pltpu.VMEM)] * len(arrays),
+        out_specs=[pl.BlockSpec(memory_space=pltpu.VMEM)] * len(shapes),
+        out_shape=[jax.ShapeDtypeStruct(shape, BF16) for shape in shapes],
+        cost_estimate=pl.CostEstimate(flops=size, bytes_accessed=2 * size, transcendentals=0),
+        name=name,
+    )(*arrays)
+
+
+def attend_kernel(head_size, count, *refs):
+    blocks, (sq_ref, sk_ref) = refs[:count], refs[count : count + 2]
+    out_refs, lse_ref, qkv = refs[count + 2 : 2 * count + 2], refs[-2], refs[-1]
+    step = pl.program_id(1)
+    block_len, block = blocks[0].shape[1], sq_ref.shape[1]
+    per = block_len // block
+
+    @pl.when(step == 0)
+    def _():
+        for j in range(count):
+            qkv[j * block_len : (j + 1) * block_len, :] = blocks[j][0]
+
     lane_head = lax.broadcasted_iota(jnp.int32, (1, LANES), 1) // head_size
-    query, key, value = q_ref[0], k_ref[0], v_ref[0]
+    query = qkv[pl.ds(pl.multiple_of(step * block, block), block), :LANES]
+    key, value = qkv[:, LANES : 2 * LANES], qkv[:, 2 * LANES :]
     same_doc = sq_ref[0] == sk_ref[0]
     heads = LANES // head_size
     mixed = jnp.zeros(query.shape, F32)
@@ -63,73 +108,76 @@
         part = dot_nn(exp_scores.astype(BF16), value) / denominator
         mixed = jnp.where(own, part, mixed)
         lse = jnp.where(own, row_max * SCALE_LOG2 + jnp.log2(denominator), lse)
-    o_ref[0] = mixed.astype(BF16)
+    mixed = mixed.astype(BF16)
+    for j in range(count):
+
+        @pl.when(step // per == j)
+        def _(j=j):
+            start = pl.multiple_of(step % per * block, block)
+            out_refs[j][0, pl.ds(start, block), :] = mixed
+
     turned = lse.T
     for head in range(heads):
-        lse_ref[0, 0, head : head + 1, :] = turned[head * head_size : head * head_size + 1, :]
-
-
-def attend(query, key, value, segs, head_size):
-    seq_count, length, cols = query.shape
-    block = min(256, length)
-    pairs = cols // LANES
-    flops = 4 * seq_count * length * length * cols
-    row_spec = pl.BlockSpec((1, block, LANES), lambda s, p, i: (s, i, p))
-    full_spec = pl.BlockSpec((1, length, LANES), lambda s, p, i: (s, 0, p))
-    return pl.pallas_call(
-        functools.partial(attend_kernel, head_size),
-        grid=(seq_count, pairs, length // block),
-        in_specs=[
-            row_spec,
-            full_spec,
-            full_spec,
-            pl.BlockSpec((1, block, 1), lambda s, p, i: (s, i, 0)),
-            pl.BlockSpec((1, 1, length), lambda s, p, i: (s, 0, 0)),
+        lse_ref[0, head : head + 1, :] = turned[head * head_size : head * head_size + 1, :]
+
+
+def attend(blocks, segs, head_size):
+    count = len(blocks)
+    seq_count, block_len, cols = blocks[0].shape
+    length = count * block_len
+    block = min(256, block_len)
+    elements = seq_count * length * length * LANES
+    block_spec = pl.BlockSpec((1, block_len, cols), lambda s, i: (s, 0, 0))
+    out_spec = pl.BlockSpec((1, block_len, LANES), lambda s, i: (s, 0, 0))
+    results = pl.pallas_call(
+        functools.partial(attend_kernel, head_size, count),
+        grid=(seq_count, length // block),
+        in_specs=[block_spec] * count
+        + [
+            pl.BlockSpec((1, block, 1), lambda s, i: (s, i, 0)),
+            pl.BlockSpec((1, 1, length), lambda s, i: (s, 0, 0)),
         ],
-        out_specs=[row_spec, pl.BlockSpec((1, 1, 8, block), lambda s, p, i: (s, p, 0, i))],
-        out_shape=[
-            jax.ShapeDtypeStruct(query.shape, BF16),
-            jax.ShapeDtypeStruct((seq_count, pairs, 8, length), F32),
-        ],
+        out_specs=[out_spec] * count + [pl.BlockSpec((1, 8, block), lambda s, i: (s, 0, i))],
+        out_shape=[jax.ShapeDtypeStruct((seq_count, block_len, LANES), BF16)] * count
+        + [jax.ShapeDtypeStruct((seq_count, 8, length), F32)],
+        scratch_shapes=[pltpu.VMEM((length, cols), BF16)],
         compiler_params=pltpu.CompilerParams(vmem_limit_bytes=48 << 20),
         cost_estimate=pl.CostEstimate(
-            flops=flops,
-            bytes_accessed=8 * seq_count * length * cols,
-            transcendentals=seq_count * length * length * cols // head_size,
+            flops=4 * elements,
+            bytes_accessed=8 * seq_count * length * LANES,
+            transcendentals=elements // head_size,
         ),
         name="attend",
-    )(query, key, value, segs[:, :, None], segs[:, None, :])
-
-
-def attend_grad_kernel(
-    head_size,
-    q_ref,
-    do_ref,
-    o_ref,
-    k_ref,
-    v_ref,
-    sq_ref,
-    sk_ref,
-    lse_ref,
-    dq_ref,
-    dk_ref,
-    dv_ref,
-    kt_ref,
-    dk_sum,
-    dv_sum,
-):
-    step = pl.program_id(2)
-    lane_head = lax.broadcasted_iota(jnp.int32, (1, LANES), 1) // head_size
-    query, grad_out, key, value = q_ref[0], do_ref[0], k_ref[0], v_ref[0]
+    )(*blocks, segs[:, :, None], segs[:, None, :])
+    return results[:count], results[count]
+
+
+def attend_grad_kernel(head_size, count, *refs):
+    blocks, do_refs, o_refs = refs[:count], refs[count : 2 * count], refs[2 * count : 3 * count]
+    sq_ref, sk_ref, lse_ref = refs[3 * count : 3 * count + 3]
+    out_refs = refs[3 * count + 3 : 4 * count + 3]
+    qkv, grad_seq, mixed_seq, kt_ref, dk_sum, dv_sum = refs[4 * count + 3 :]
+    step = pl.program_id(1)
+    block_len, block = blocks[0].shape[1], sq_ref.shape[2]
+    per = block_len // block
 
     @pl.when(step == 0)
     def _():
-        kt_ref[...] = k_ref[0].T
+        for j in range(count):
+            rows = slice(j * block_len, (j + 1) * block_len)
+            qkv[rows, :] = blocks[j][0]
+            grad_seq[rows, :] = do_refs[j][0]
+            mixed_seq[rows, :] = o_refs[j][0]
+        kt_ref[...] = qkv[:, LANES : 2 * LANES].T
         dk_sum[...] = jnp.zeros_like(dk_sum)
         dv_sum[...] = jnp.zeros_like(dv_sum)
 
+    lane_head = lax.broadcasted_iota(jnp.int32, (1, LANES), 1) // head_size
+    own_rows = pl.ds(pl.multiple_of(step * block, block), block)
+    query, key, value = qkv[own_rows, :LANES], qkv[:, LANES : 2 * LANES], qkv[:, 2 * LANES :]
+    grad_out = grad_seq[own_rows, :]
     same_doc = sk_ref[0] == sq_ref[0]
-    products = (grad_out.astype(F32) * o_ref[0].astype(F32)).T
+    products = (grad_out.astype(F32) * mixed_seq[own_rows, :].astype(F32)).T
     grad_query = []
     for head in range(LANES // head_size):
         own = lane_head == head
@@ -137,55 +185,65 @@
         row_delta = jnp.sum(products[rows], 0, keepdims=True)
         query_own = jnp.where(own, query, jnp.zeros_like(query))
         grad_own = jnp.where(own, grad_out, jnp.zeros_like(grad_out))
-        scores = dot_nt(key, query_own) * SCALE_LOG2 - lse_ref[0, 0, head : head + 1, :]
+        scores = dot_nt(key, query_own) * SCALE_LOG2 - lse_ref[0, head : head + 1, :]
         probs = jnp.exp2(jnp.where(same_doc, scores, NEG_LARGE))
         grad_probs = dot_nt(value, grad_own)
         grad_scores = (probs * (grad_probs - row_delta)).astype(BF16)
         dv_sum[...] += dot_nn(probs.astype(BF16), grad_own)
         dk_sum[...] += dot_nn(grad_scores, query_own)
         grad_query.append(dot_nn(kt_ref[rows, :], grad_scores))
-    dq_ref[0] = (jnp.concatenate(grad_query, 0).T * SCALE_QK).astype(BF16)
-
-    @pl.when(step == pl.num_programs(2) - 1)
+    grad_query = (jnp.concatenate(grad_query, 0).T * SCALE_QK).astype(BF16)
+    for j in range(count):
+
+        @pl.when(step // per == j)
+        def _(j=j):
+            start = pl.multiple_of(step % per * block, block)
+            out_refs[j][0, pl.ds(start, block), :LANES] = grad_query
+
+    @pl.when(step == pl.num_programs(1) - 1)
     def _():
-        dk_ref[0] = (dk_sum[...] * SCALE_QK).astype(BF16)
-        dv_ref[0] = dv_sum[...].astype(BF16)
-
-
-def attend_grad(query, grad_out, mixed, key, value, segs, lse, head_size):
-    seq_count, length, cols = query.shape
-    block = min(256, length)
-    pairs = cols // LANES
-    row_spec = pl.BlockSpec((1, block, LANES), lambda s, p, i: (s, i, p))
-    full_spec = pl.BlockSpec((1, length, LANES), lambda s, p, i: (s, 0, p))
+        for j in range(count):
+            rows = slice(j * block_len, (j + 1) * block_len)
+            out_refs[j][0, :, LANES : 2 * LANES] = (dk_sum[rows, :] * SCALE_QK).astype(BF16)
+            out_refs[j][0, :, 2 * LANES :] = dv_sum[rows, :].astype(BF16)
+
+
+def attend_grad(blocks, grad_blocks, group, mixed_blocks, segs, lse, head_size):
+    count = len(blocks)
+    seq_count, block_len, cols = blocks[0].shape
+    length = count * block_len
+    block = min(256, block_len)
+    elements = seq_count * length * length * LANES
+    block_spec = pl.BlockSpec((1, block_len, cols), lambda s, i: (s, 0, 0))
     return pl.pallas_call(
-        functools.partial(attend_grad_kernel, head_size),
-        grid=(seq_count, pairs, length // block),
-        in_specs=[
-            row_spec,
-            row_spec,
-            row_spec,
-            full_spec,
-            full_spec,
-            pl.BlockSpec((1, 1, block), lambda s, p, i: (s, 0, i)),
-            pl.BlockSpec((1, length, 1), lambda s, p, i: (s, 0, 0)),
-            pl.BlockSpec((1, 1, 8, block), lambda s, p, i: (s, p, 0, i)),
+        functools.partial(attend_grad_kernel, head_size, count),
+        grid=(seq_count, length // block),
+        in_specs=[block_spec] * count
+        + [pl.BlockSpec((1, block_len, LANES), lambda s, i: (s, 0, group))] * count
+        + [pl.BlockSpec((1, block_len, LANES), lambda s, i: (s, 0, 0))] * count
+        + [
+            pl.BlockSpec((1, 1, block), lambda s, i: (s, 0, i)),
+            pl.BlockSpec((1, length, 1), lambda s, i: (s, 0, 0)),
+            pl.BlockSpec((1, 8, block), lambda s, i: (s, 0, i)),
         ],
-        out_specs=[row_spec, full_spec, full_spec],
-        out_shape=[jax.ShapeDtypeStruct(query.shape, BF16)] * 3,
+        out_specs=[block_spec] * count,
+        out_shape=[jax.ShapeDtypeStruct(blocks[0].shape, BF16)] * count,
         scratch_shapes=[
+            pltpu.VMEM((length, cols), BF16),
+            pltpu.VMEM((length, LANES), BF16),
+            pltpu.VMEM((length, LANES), BF16),
             pltpu.VMEM((LANES, length), BF16),
             pltpu.VMEM((length, LANES), F32),
             pltpu.VMEM((length, LANES), F32),
         ],
         compiler_params=pltpu.CompilerParams(vmem_limit_bytes=56 << 20),
         cost_estimate=pl.CostEstimate(
-            flops=10 * seq_count * length * length * cols,
-            bytes_accessed=16 * seq_count * length * cols,
-            transcendentals=seq_count * length * length * cols // head_size,
+            flops=10 * elements,
+            bytes_accessed=16 * seq_count * length * LANES,
+            transcendentals=elements // head_size,
         ),
         name="attend_grad",
-    )(query, grad_out, mixed, key, value, segs[:, None, :], segs[:, :, None], lse)
+    )(*blocks, *grad_blocks, *mixed_blocks, segs[:, None, :], segs[:, :, None], lse)
 
 
 def local(
@@ -247,11 +305,6 @@
             pieces.append(piece)
         return pieces
 
-    def gather_width(values):
-        for bit in range(fsdp_bits):
-            values = jnp.concatenate([values, exchange(values, "fsdp", fsdp, 1 << bit)], 1)
-        return values
-
     def spread_near(values):
         blocks = [values]
         for bit in range(ctx_bits - 1):
@@ -271,7 +324,7 @@
     per_group = max(1, LANES // head_cols)
     groups = tp // per_group
     group_cols = per_group * head_cols
-    qkv_turned = jnp.swapaxes(w_qkv, 1, 2)
+    qkv_turned, w_in_turned = jnp.swapaxes(w_qkv, 1, 2), w_in.T
     qkv_pieces = []
     for h in range(2):
         start = (at_ctx ^ (h * low_ctx)) * head_cols
@@ -287,50 +340,45 @@
     small = jnp.concatenate(small_width + [small_tail.reshape(tail_rows, width_part)], 0)
     small = jnp.pad(small, ((0, -small.shape[0] % 16), (0, 0)))
     small_rows = small.shape[0]
-    first_rows = 6 * head_cols + small_rows
+    def gate(values, waited):
+        return lax.optimization_barrier((values, waited))
+
+    def width_parts(piece):
+        parts = [piece]
+        for bit in range(fsdp_bits):
+            parts = parts + [exchange(p, "fsdp", fsdp, 1 << bit) for p in parts]
+        return parts
+
+    def full_pieces(piece, waits=()):
+        pieces = []
+        for s in range(tp - 1):
+            parts, moved = width_parts(piece), shift_tp(piece)
+            (parts, piece), _ = gate((parts, moved), list(waits[s : s + 1]))
+            pieces.append(parts)
+        return pieces + [width_parts(piece)]
+
+    def place_pieces(pieces, runs, shapes, name):
+        arrays = [part for parts in pieces for part in parts]
+        plan = [
+            (out, row, i * width_part, count, width_part, [(s * fsdp + i, at_row, 0)])
+            for out, row, s, at_row, count in runs
+            for i in range(fsdp)
+        ]
+        return assemble(arrays, plan, shapes, name)
+
     with jax.named_scope("get_qkv"):
-        first_pieces = tp_pieces(jnp.concatenate(qkv_pieces + [small], 0))
-        early = (tp + 1) // 2
-        first_full = [
-            part
-            for group in (first_pieces[:early], first_pieces[early:])
-            if group
-            for part in cut(gather_width(jnp.concatenate(group, 0)), first_rows)
-        ]
-        unit = [cut(p[: 6 * head_cols], head_cols) for p in first_full]
-        own_qkv = jnp.concatenate(
-            [
-                unit[g * per_group + s][h * 3 + i]
-                for h in range(2)
-                for g in range(groups)
-                for i in range(3)
-                for s in range(per_group)
-            ],
-            0,
+        first_pieces = full_pieces(jnp.concatenate(qkv_pieces + [small], 0))
+        runs, row = [], 0
+        for h, g, i, s in itertools.product(range(2), range(groups), range(3), range(per_group)):
+            runs.append((0, row, g * per_group + s, (h * 3 + i) * head_cols, head_cols))
+            row += head_cols
+        for s in range(tp):
+            runs.append((1, s * small_rows, s, 6 * head_cols, small_rows))
+        own_qkv, small_full = place_pieces(
+            first_pieces, runs, [(row, width), (tp * small_rows, width)], "place_qkv"
         )
         qkv_weights = spread_near(own_qkv)
-    small_full = jnp.stack([p[6 * head_cols :] for p in first_full])
     small_full = small_full.reshape(tp, small_rows, fsdp, width_part)
-    with jax.named_scope("get_in"):
-        in_piece = near_rows(w_in.T, hidden, False)[0]
-        in_own = gather_width(jnp.concatenate(tp_pieces(in_piece), 0))
-        in_own = jnp.concatenate([in_own, exchange(in_own, "ctx", ctx, low_ctx)], 0)
-        in_weights = spread_near(in_own)
-    with jax.named_scope("get_out"):
-        o_parts, out_parts = near_rows(w_o, head_cols, True), near_rows(w_out, hidden, True)
-        pieces = tp_pieces(jnp.concatenate(o_parts + out_parts, 0))
-        o_parts = [p[h * head_cols : (h + 1) * head_cols] for h in range(2) for p in pieces]
-        out_parts = [
-            p[2 * head_cols + h * hidden : 2 * head_cols + (h + 1) * hidden]
-            for h in range(2)
-            for p in pieces
-        ]
-        both_own = gather_width(jnp.concatenate(o_parts + out_parts, 0))
-        both_weights = spread_near(both_own)
-        o_rows = 2 * tp * head_cols
-        o_weights = [w[:o_rows] for w in both_weights]
-        out_weights = [w[o_rows:] for w in both_weights]
-
     own_small = small_full[0].astype(F32)
     bias_attn, gain_one, shift_one, bias_out, gain_two, shift_two = (
         own_small[i].reshape(1, width) for i in range(6)
@@ -394,17 +442,14 @@
                 )
         return result
 
+    def trade(blocks):
+        return [blocks[0]] + [exchange(blocks[j], "ctx", ctx, j) for j in range(1, ctx)]
+
     def to_sequences(blocks):
-        arrived = [blocks[0]] + [exchange(blocks[j], "ctx", ctx, j) for j in range(1, ctx)]
-        cols = blocks[0].shape[1]
-        return jnp.concatenate([b.reshape(own_seqs, block_len, cols) for b in arrived], 1)
-
-    def to_rows(values):
-        cols = values.shape[2]
-        blocks = [
-            values[:, j * block_len : (j + 1) * block_len].reshape(rows, cols) for j in range(ctx)
-        ]
-        return [blocks[0]] + [exchange(blocks[j], "ctx", ctx, j) for j in range(1, ctx)]
+        return [b.reshape(own_seqs, block_len, b.shape[1]) for b in trade(blocks)]
+
+    def to_rows(blocks):
+        return trade([b.reshape(rows, b.shape[2]) for b in blocks])
 
     def by_block(near_values, cols):
         return [
@@ -430,21 +475,52 @@
     ]
     qkv_blocks = move_columns(by_block(qkv_near, 3 * group_cols), None if aligned else to_heads)
     heads_in, mixed_parts, mixed_blocks = [], [], [[] for _ in range(ctx)]
+    with jax.named_scope("to_sequences"):
+        all_seq = [to_sequences([b[g] for b in qkv_blocks]) for g in range(groups)]
     for g in range(groups):
-        with jax.named_scope("to_sequences"):
-            qkv_seq = to_sequences([b[g] for b in qkv_blocks])
-        parts = [qkv_seq[:, :, i * group_cols : (i + 1) * group_cols] for i in range(3)]
-        mixed, lse = attend(*parts, segs, head_size)
-        heads_in.append((parts, lse))
+        qkv_seq = all_seq[g]
+        mixed, lse = attend(qkv_seq, segs, head_size)
+        heads_in.append((qkv_seq, lse))
         mixed_parts.append(mixed)
         with jax.named_scope("to_rows"):
             for j, block in enumerate(to_rows(mixed)):
                 mixed_blocks[j].append(block)
+    waited = [first_pieces[-1][0]] + [parts[1:] for parts in first_pieces[:-1]]
+    waits = [qkv_near, all_seq[0], (all_seq[-1], mixed_parts[0])]
+    with jax.named_scope("get_in"):
+        piece = jnp.concatenate(
+            near_rows(w_o, head_cols, True) + near_rows(w_in_turned, hidden, True), 0
+        )
+        piece, _ = gate(piece, waited)
+        in_pieces = full_pieces(piece, waits)
+
+    def both_halves(pieces, parts, name):
+        runs, row, start = [], 0, 0
+        for count in parts:
+            for h, s in itertools.product(range(2), range(tp)):
+                runs.append((0, row, s, start + h * count, count))
+                row += count
+            start += 2 * count
+        return spread_near(place_pieces(pieces, runs, [(row, width)], name)[0])
+
+    with jax.named_scope("get_in"):
+        both_weights = both_halves(in_pieces, (head_cols, hidden), "place_in")
+        o_rows = 2 * tp * head_cols
+        o_weights = [w[:o_rows] for w in both_weights]
+        in_weights = [w[o_rows:] for w in both_weights]
     attended = by_near(move_columns(mixed_blocks, None if aligned else from_heads))
 
     attn_rows = bias_attn
     for n in range(low_ctx):
         attn_rows = attn_rows + dot_nn(attended[n], o_weights[n])
+    with jax.named_scope("get_out"):
+        piece = jnp.concatenate(near_rows(w_out, hidden, True), 0)
+        waited = [in_pieces[-1][0], mixed_parts[0]] + [parts[1:] for parts in in_pieces[:-1]]
+        piece, _ = gate(piece, (waited, all_seq[-1]))
+        early = [b[0] for b in mixed_blocks[1:]] if groups > 1 else []
+        late = [b[-1] for b in mixed_blocks[1:]]
+        out_pieces = full_pieces(piece, [(mixed_parts[-1], early), late, attn_rows])
+        out_weights = both_halves(out_pieces, (hidden,), "place_out")
     first_in = inputs.astype(F32) + attn_rows
     normed, pull_first = jax.vjp(layer_norm, first_in, gain_one, shift_one)
     normed_low = normed.astype(BF16)
@@ -465,10 +541,6 @@
             whole = lax.dynamic_update_slice_in_dim(whole, pieces[s], start, 0)
         return whole
 
-    def gate(values, waited):
-        values, waited = lax.optimization_barrier((values, waited))
-        return values, waited
-
     output_pieces = [turned_rows(final_rows)]
 
     def next_output():
@@ -482,8 +554,8 @@
     def add_low(left, right):
         return (left.astype(F32) + right.astype(F32)).astype(BF16)
 
-    def fold_width(values):
-        for bit in reversed(range(fsdp_bits)):
+    def fold_width(values, bits=fsdp_bits):
+        for bit in reversed(range(bits)):
             half = values.shape[1] // 2
             values = add_low(values[:, :half], exchange(values[:, half:], "fsdp", fsdp, 1 << bit))
         return values
@@ -507,12 +579,6 @@
                 for n in range(half)
             ]
         return near_values[0]
-
-    def join_halves(arrays):
-        if len(arrays) == 1:
-            return arrays[0]
-        tops = [a[: a.shape[0] // 2] for a in arrays]
-        return jnp.concatenate(tops + [a[a.shape[0] // 2 :] for a in arrays], 0)
 
     def join_ctx(share):
         blocks = share
@@ -549,11 +615,32 @@
         grad_mixed = to_sequences([jnp.concatenate(b, 1) for b in grad_blocks])
     with jax.named_scope("sum_in"):
         grad_o = [dot_tn(a, grad_attn).astype(BF16) for a in attended]
-        sum_in = fold_near([join_halves([i, o]) for i, o in zip(grad_in, grad_o)])
+        arrays = []
+        for near_values in (grad_in, grad_o):
+            for bit in reversed(range(1, ctx_bits - 1)):
+                half = len(near_values) // 2
+                near_values = [
+                    add_low(near_values[n], exchange(near_values[n + half], "ctx", ctx, 1 << bit))
+                    for n in range(half)
+                ]
+            arrays.append(near_values[0])
+            if ctx_bits > 1:
+                arrays.append(exchange(near_values[1], "ctx", ctx, 1))
+        each = len(arrays) // 2
+        in_half, o_half = tp * hidden, tp * head_cols
+        plan, side = [], width // 2
+        for h, c in itertools.product(range(2), range(2)):
+            row = h * (in_half + o_half)
+            for first, at, count in ((0, row, in_half), (each, row + in_half, o_half)):
+                sources = [(first + i, h * count, c * side) for i in range(each)]
+                plan.append((c, at, 0, count, side, sources))
+        sum_in = assemble(arrays, plan, [(2 * (in_half + o_half), side)] * 2, "merge_in")
     grad_mixed, (sum_out, sum_in, piece) = gate(grad_mixed, (sum_out, sum_in, next_output()))
     keep_output(piece)
     with jax.named_scope("sum_in"):
-        sum_in = fold_width(sum_in)
+        top = fsdp_bits - 1
+        sum_in = add_low(sum_in[0], exchange(sum_in[1], "fsdp", fsdp, 1 << top))
+        sum_in = fold_width(sum_in, top)
     with jax.named_scope("sum_out"):
         sum_out = fold_half(sum_out)
 
@@ -565,12 +652,9 @@
             keep_output(piece)
             with jax.named_scope("sum_out"):
                 share_out = fold_tp(cut(sum_out, hidden))
-        cols = slice(g * group_cols, (g + 1) * group_cols)
-        grads = attend_grad(
-            parts[0], grad_mixed[:, :, cols], mixed_parts[g], parts[1], parts[2], segs, lse, head_size
-        )
+        grads = attend_grad(parts, grad_mixed, g, mixed_parts[g], segs, lse, head_size)
         with jax.named_scope("to_rows_grad"):
-            for j, block in enumerate(to_rows(jnp.concatenate(grads, 2))):
+            for j, block in enumerate(to_rows(grads)):
                 grad_qkv[j].append(block)
     while len(output_pieces) < tp:
         output_pieces.append(next_output())
@@ -578,32 +662,12 @@
     grad_qkv, (share_out, sum_in) = gate(grad_qkv, (share_out, sum_in))
     with jax.named_scope("sum_in"):
         sum_in = fold_half(sum_in)
-        in_rows = tp * hidden
-        in_cut, o_cut = cut(sum_in[:in_rows], hidden), cut(sum_in[in_rows:], head_cols)
-        share_in = fold_tp([jnp.concatenate([i, o], 0) for i, o in zip(in_cut, o_cut)])
-    with jax.named_scope("join_out_in"):
-        joined = join_ctx(jnp.concatenate([share_out, share_in], 0))
-        grad_w_out = joined[:, :hidden].reshape(ctx * hidden, width_part)
-        grad_w_in = joined[:, hidden : 2 * hidden].reshape(ctx * hidden, width_part).T
-        grad_w_o = joined[:, 2 * hidden :].reshape(ctx * head_cols, width_part)
     grad_near = by_near(move_columns(grad_qkv, None if aligned else from_heads))
     input_part = grad_first
     for n in range(low_ctx):
         input_part = input_part + dot_nn(grad_near[n], qkv_weights[n])
     with jax.named_scope("share_grad_tokens"):
         grad_tokens = place_rows(tp_pieces(turned_rows(input_part)))
-    with jax.named_scope("sum_qkv"):
-        total = fold_near([dot_tn(g, inputs).astype(BF16) for g in grad_near])
-        total = cut(fold_width(fold_half(total)), head_cols)
-        pieces = []
-        for s in range(tp):
-            at = (s // per_group) * 3 * per_group + s % per_group
-            pieces.append(jnp.concatenate([total[at + i * per_group] for i in range(3)], 0))
-        share_qkv = fold_tp(pieces)
-    with jax.named_scope("join_qkv"):
-        grad_w_qkv = join_ctx(share_qkv).reshape(ctx, 3, head_cols, width_part)
-        grad_w_qkv = grad_w_qkv.transpose(1, 3, 0, 2).reshape(3, width_part, ctx * head_cols)
-
     def tp_order(values, axis):
         moved = [
             lax.dynamic_index_in_dim(values, (at_tp - t) % tp, axis, True) for t in range(tp)
@@ -632,10 +696,44 @@
     qv_sums = reorder(jnp.stack([qv_sums[0], qv_sums[2]]), at_ctx, ctx_bits, 1)
     qv_sums = tp_order(qv_sums.transpose(0, 2, 1, 3), 1).reshape(2, width)
     small_sums = jnp.concatenate([reorder_width(small_sums), in_sums, qv_sums], 0)
-    with jax.named_scope("sum_small"):
-        for axis, size in (("ctx", ctx), ("fsdp", fsdp), ("tp", tp)):
-            for bit in range(size.bit_length() - 1):
-                small_sums = small_sums + exchange(small_sums, axis, size, 1 << bit)
+
+    def sum_small(values, axis, size, bits):
+        with jax.named_scope("sum_small"):
+            for bit in bits:
+                values = values + exchange(values, axis, size, 1 << bit)
+        return values
+
+    with jax.named_scope("sum_qkv"):
+        total = fold_near([dot_tn(g, inputs).astype(BF16) for g in grad_near])
+        small_sums = sum_small(small_sums, "ctx", ctx, range(ctx_bits - 1))
+        (total, small_sums), _ = gate((total, small_sums), ())
+        total = fold_half(total)
+        small_sums = sum_small(small_sums, "ctx", ctx, range(ctx_bits - 1, ctx_bits))
+        (total, small_sums, sum_in), _ = gate((total, small_sums, sum_in), ())
+        total = fold_width(total)
+    with jax.named_scope("sum_in"):
+        in_rows = tp * hidden
+        in_cut, o_cut = cut(sum_in[:in_rows], hidden), cut(sum_in[in_rows:], head_cols)
+        share_in = fold_tp([jnp.concatenate([i, o], 0) for i, o in zip(in_cut, o_cut)])
+    with jax.named_scope("sum_qkv"):
+        (total, share_in, small_sums), _ = gate((total, share_in, small_sums), ())
+        small_sums = sum_small(small_sums, "fsdp", fsdp, range(fsdp_bits))
+        total = cut(total, head_cols)
+        pieces = []
+        for s in range(tp):
+            at = (s // per_group) * 3 * per_group + s % per_group
+            pieces.append(jnp.concatenate([total[at + i * per_group] for i in range(3)], 0))
+        share_qkv = fold_tp(pieces)
+    with jax.named_scope("join_out_in"):
+        joined = join_ctx(jnp.concatenate([share_out, share_in], 0))
+        grad_w_out = joined[:, :hidden].reshape(ctx * hidden, width_part)
+        grad_w_in = joined[:, hidden : 2 * hidden].reshape(ctx * hidden, width_part).T
+        grad_w_o = joined[:, 2 * hidden :].reshape(ctx * head_cols, width_part)
+    with jax.named_scope("join_qkv"):
+        (share_qkv, small_sums), _ = gate((share_qkv, small_sums), ())
+        grad_w_qkv = join_ctx(share_qkv).reshape(ctx, 3, head_cols, width_part)
+        grad_w_qkv = grad_w_qkv.transpose(1, 3, 0, 2).reshape(3, width_part, ctx * head_cols)
+        small_sums = sum_small(small_sums, "tp", tp, range(tp.bit_length() - 1))
     width_sums = lax.dynamic_slice_in_dim(small_sums[:6], at_fsdp * width_part, width_part, 1)
     hidden_own = lax.dynamic_index_in_dim(
         small_sums[6:-2].reshape(tp, b_in.shape[0], fsdp, b_in.shape[1]), at_tp, 0, False

time: 780 us -> 667 us (0.86)
  other arithmetic: 95.3 us -> 29.1 us
  local copies, waits for them, and re-layouts: 106 us -> 58.6 us
  waiting for transfers between devices: 337 us -> 303 us
  Pallas kernels: 87.9 us -> 112 us
  starting transfers between devices: 56.2 us -> 66.6 us
    ppermute x15, waiting for transfers between devices: 86.2 us -> 40.6 us  [shift_tp(): return lax.ppermute(values, 'tp', [(i, (i + 1) % tp) for i in range(tp)])]
    concatenate x14 -> x3, other arithmetic: 37.6 us -> 0.11 us  [the longest x1 0.05 us: local(): jnp.concatenate(near_rows(w_o, head_cols, True) + near_rows(w_in_turned,...]
    unnamed x235 -> x262, local copies, waits for them, and re-layouts: 49.4 us -> 22 us
    pallas_call x4 -> x8, Pallas kernels: 87.9 us -> 112 us  [the longest x2 54.9 us: attend_grad(): pl.pallas_call(functools.partial(attend_grad_kernel, head_size, count), g...]
    ppermute x47 -> x55, waiting for transfers between devices: 189 us -> 207 us  [exchange(): return lax.ppermute(values, axis, [(i, i ^ j) for i in range(size)])]
    convert_element_type x7 -> x6, other arithmetic: 25.2 us -> 9.22 us  [add_low(): return (left.astype(F32) + right.astype(F32)).astype(BF16)]
    ppermute x47 -> x55, starting transfers between devices: 33.9 us -> 46.8 us  [exchange(): return lax.ppermute(values, axis, [(i, i ^ j) for i in range(size)])]
  transfers between devices with their start and end apart: 71 -> 79, of which waited for: 32 -> 38; matrix products, arithmetic and copies ran while one was open for 29% -> 18% of each run, Pallas kernels for 11% -> 15%
where the time goes in v3:
time: 667 us; the launch traced here: 658 us
  waiting for transfers between devices  303 us (45%)
  Pallas kernels  112 us (17%)
  matrix products  85.3 us (13%)
  starting transfers between devices  66.6 us (10%)
  local copies, waits for them, and re-layouts  58.6 us (9%)
  other arithmetic  29.1 us (4%)
    ppermute x55, waiting for transfers between devices, exchange(): return lax.ppermute(values, axis, [(i, i ^ j) for i in range(size)])  207 us
    pallas_call x2, Pallas kernels, attend_grad(): pl.pallas_call(functools.partial(attend_grad_kernel, head_size, count), g...  54.9 us
    ppermute x9, waiting for transfers between devices, fold_tp(): total = total + lax.ppermute(pieces[s], 'tp', pairs).astype(F32)  54.8 us
    ppermute x55, starting transfers between devices, exchange(): return lax.ppermute(values, axis, [(i, i ^ j) for i in range(size)])  46.8 us
    ppermute x15, waiting for transfers between devices, shift_tp(): return lax.ppermute(values, 'tp', [(i, (i + 1) % tp) for i in range(tp)])  40.6 us
    pallas_call x2, Pallas kernels, attend(): pl.pallas_call(functools.partial(attend_kernel, head_size, count), grid=(...  35.5 us
    dot_general x8, matrix products, dot_nt(): lax.dot_general(left, right, CONTRACT_LAST, preferred_element_type=F32)  31.6 us
    dot_general x8, matrix products, dot_tn(): lax.dot_general(left, right, CONTRACT_FIRST, preferred_element_type=F32)  29.1 us
  transfers between devices with their start and end apart: 79, of which 38 were waited for; matrix products, arithmetic and copies ran while one was open for 18% of the time, Pallas kernels for 15%

profile of v3, /device:TPU:0, one launch (start us, length us, event | category | flops | bytes accessed | tf_op | source)
XLA Modules:
  0.0 657.9 jit_solution(5222764711223773580)
XLA Ops:
  7.7 7.9 %collective-permute-done.refs_1_ = bf16[400,512]{1,0:T(8,128)(2,1)S(1)} collective-permute-done((bf16[400,512]{1,0:T(8,128)(2,1)S(1)}, bf16[400,512]{1,0:T(8,128)(2,1)S(1)}, u32[]{:S(2)}, u32[]{:S(2)}) %collective-permute-start) | collective-permute-done | bytes 409632 | tf_op jit(solution)/shard_map/get_qkv/ppermute | solution.py:281
  19.8 9.2 %collective-permute-done.2.refs_3_ = bf16[400,512]{1,0:T(8,128)(2,1)S(1)} collective-permute-done((bf16[400,512]{1,0:T(8,128)(2,1)S(1)}, bf16[400,512]{1,0:T(8,128)(2,1)S(1)}, u32[]{:S(2)}, u32[]{:S(2)}) %collective-permute-start.2) | collective-permute-done | bytes 409632 | tf_op jit(solution)/shard_map/get_qkv/ppermute | solution.py:281
  34.2 6.9 %collective-permute-done.4.refs_5_ = bf16[400,512]{1,0:T(8,128)(2,1)S(1)} collective-permute-done((bf16[400,512]{1,0:T(8,128)(2,1)S(1)}, bf16[400,512]{1,0:T(8,128)(2,1)S(1)}, u32[]{:S(2)}, u32[]{:S(2)}) %collective-permute-start.4) | collective-permute-done | bytes 409632 | tf_op jit(solution)/shard_map/get_qkv/ppermute | solution.py:281
  79.8 8.8 %collective-permute-done.10 = bf16[512,384]{1,0:T(8,128)(2,1)S(1)} collective-permute-done((bf16[512,384]{1,0:T(8,128)(2,1)S(1)}, bf16[512,384]{1,0:T(8,128)(2,1)S(1)}, u32[]{:S(2)}, u32[]{:S(2)}) %collective-permute-start.10) | collective-permute-done | bytes 393248 | tf_op jit(solution)/shard_map/to_sequences/ppermute | solution.py:281
  98.4 17.7 %attend.2 = (bf16[1,512,128]{2,1,0:T(8,128)(2,1)S(1)}, bf16[1,512,128]{2,1,0:T(8,128)(2,1)S(1)}, bf16[1,512,128]{2,1,0:T(8,128)(2,1)S(1)}, bf16[1,512,128]{2,1,0:T(8,128)(2,1)S(1)}, f32[1,8,2048]{2,1,0:T(8,128)S(1)}) custom-call(bf16[1,512,384]{2,1,0:T(8,128)(2,1)S(1)} %get-tuple-element.256.refs_0_, bf16[1,512,384]{2,1,0:T(8,128)(2,1)S(1)} %bitcast.200, ...), custom_call_target="tpu_custom_call" | custom-call | flops 2147483648 | bytes 2097152 | tf_op jit(solution)/shard_map/attend/pallas_call | solution.py:132
  121.2 15.9 %collective-permute-done.22.refs_7_ = bf16[640,512]{1,0:T(8,128)(2,1)S(1)} collective-permute-done((bf16[640,512]{1,0:T(8,128)(2,1)}, bf16[640,512]{1,0:T(8,128)(2,1)S(1)}, u32[]{:S(2)}, u32[]{:S(2)}) %collective-permute-start.22) | collective-permute-done | bytes 655392 | tf_op jit(solution)/shard_map/get_in/ppermute | solution.py:281
  138.0 5.4 place_in.1
  151.8 17.7 %attend.3 = (bf16[1,512,128]{2,1,0:T(8,128)(2,1)S(1)}, bf16[1,512,128]{2,1,0:T(8,128)(2,1)S(1)}, bf16[1,512,128]{2,1,0:T(8,128)(2,1)S(1)}, bf16[1,512,128]{2,1,0:T(8,128)(2,1)S(1)}, f32[1,8,2048]{2,1,0:T(8,128)S(1)}) custom-call(bf16[1,512,384]{2,1,0:T(8,128)(2,1)S(1)} %get-tuple-element.157.refs_0_, bf16[1,512,384]{2,1,0:T(8,128)(2,1)S(1)} %bitcast.207, ...), custom_call_target="tpu_custom_call" | custom-call | flops 2147483648 | bytes 2097152 | tf_op jit(solution)/shard_map/attend/pallas_call | solution.py:132
  174.1 5.4 collective-permute-done.26
  179.6 5.3 collective-permute-done.30.refs_3_
  193.3 7.5 %collective-permute-done.32.refs_5_ = bf16[512,512]{1,0:T(8,128)(2,1)S(1)} collective-permute-done((bf16[512,512]{1,0:T(8,128)(2,1)S(1)}, bf16[512,512]{1,0:T(8,128)(2,1)S(1)}, u32[]{:S(2)}, u32[]{:S(2)}) %collective-permute-start.32) | collective-permute-done | bytes 524320 | tf_op jit(solution)/shard_map/get_out/ppermute | solution.py:281
  206.3 9.3 %collective-permute-done.34.refs_7_ = bf16[512,512]{1,0:T(8,128)(2,1)} collective-permute-done((bf16[512,512]{1,0:T(8,128)(2,1)}, bf16[512,512]{1,0:T(8,128)(2,1)}, u32[]{:S(2)}, u32[]{:S(2)}) %collective-permute-start.34) | collective-permute-done | bytes 524320 | tf_op jit(solution)/shard_map/get_out/ppermute | solution.py:281
  215.6 4.6 place_out.1
  221.2 6.4 multiply_convert_fusion.1
  234.5 4.8 fusion.63
  259.2 6.5 fusion.11
  265.7 5.4 add_convert_fusion
  271.1 8.1 %collective-permute-done.37 = bf16[1,512,1024]{2,1,0:T(8,128)(2,1)} collective-permute-done((bf16[1,512,1024]{2,1,0:T(8,128)(2,1)S(1)}, bf16[1,512,1024]{2,1,0:T(8,128)(2,1)}, u32[]{:S(2)}, u32[]{:S(2)}) %collective-permute-start.37) | collective-permute-done | bytes 1048608 | tf_op jit(solution)/shard_map/share_output/ppermute | solution.py:284
  310.1 32.7 %collective-permute-done.41 = bf16[2048,512]{1,0:T(8,128)(2,1)S(1)} collective-permute-done((bf16[2048,512]{1,0:T(8,128)(2,1)}, bf16[2048,512]{1,0:T(8,128)(2,1)S(1)}, u32[]{:S(2)}, u32[]{:S(2)}) %collective-permute-start.41) | collective-permute-done | bytes 2097184 | tf_op jit(solution)/shard_map/sum_out/ppermute | solution.py:281
  347.1 7.9 %merge_in.1 = (bf16[2560,512]{1,0:T(8,128)(2,1)}, bf16[2560,512]{1,0:T(8,128)(2,1)}) custom-call(bf16[2048,1024]{1,0:T(8,128)(2,1)} %convolution_convert_fusion.3.refs_0_, bf16[2048,1024]{1,0:T(8,128)(2,1)} %collective-permute-done.42.refs_1_, bf16[512,1024]{1,0:T(8,128)(2,1)} %convolution_convert_fusion.6.refs_2_, ...), custom_call_target="tpu_custom_call" | custom-call | flops 7864320 | bytes 15728640 | tf_op jit(solution)/shard_map/sum_in/merge_in/pallas_call | solution.py:72
  358.1 27.3 %attend_grad.2 = (bf16[1,512,384]{2,1,0:T(8,128)(2,1)}, bf16[1,512,384]{2,1,0:T(8,128)(2,1)}, bf16[1,512,384]{2,1,0:T(8,128)(2,1)}, bf16[1,512,384]{2,1,0:T(8,128)(2,1)}) custom-call(bf16[1,512,384]{2,1,0:T(8,128)(2,1)} %copy-done.4, bf16[1,512,384]{2,1,0:T(8,128)(2,1)} %bitcast.201, bf16[1,512,384]{2,1,0:T(8,128)(2,1)} %bitcast.199, ...), custom_call_target="tpu_custom_call" | custom-call | flops 5368709120 | bytes 4194304 | tf_op jit(solution)/shard_map/attend_grad/pallas_call | solution.py:218
  390.6 27.5 %attend_grad.3 = (bf16[1,512,384]{2,1,0:T(8,128)(2,1)}, bf16[1,512,384]{2,1,0:T(8,128)(2,1)}, bf16[1,512,384]{2,1,0:T(8,128)(2,1)}, bf16[1,512,384]{2,1,0:T(8,128)(2,1)}) custom-call(bf16[1,512,384]{2,1,0:T(8,128)(2,1)} %copy-done.3, bf16[1,512,384]{2,1,0:T(8,128)(2,1)} %bitcast.206, bf16[1,512,384]{2,1,0:T(8,128)(2,1)} %bitcast.205, ...), custom_call_target="tpu_custom_call" | custom-call | flops 5368709120 | bytes 4194304 | tf_op jit(solution)/shard_map/attend_grad/pallas_call | solution.py:218
  424.3 6.0 collective-permute-done.49
  430.3 6.5 collective-permute-done.51
  436.8 10.4 %collective-permute-done.50 = bf16[512,384]{1,0:T(8,128)(2,1)S(1)} collective-permute-done((bf16[512,384]{1,0:T(8,128)(2,1)}, bf16[512,384]{1,0:T(8,128)(2,1)S(1)}, u32[]{:S(2)}, u32[]{:S(2)}) %collective-permute-start.50) | collective-permute-done | bytes 393248 | tf_op jit(solution)/shard_map/to_rows_grad/ppermute | solution.py:281
  447.2 6.4 collective-permute-done.52
  489.9 13.2 %collective-permute-done.57 = bf16[1,512,1024]{2,1,0:T(8,128)(2,1)} collective-permute-done((bf16[1,512,1024]{2,1,0:T(8,128)(2,1)}, bf16[1,512,1024]{2,1,0:T(8,128)(2,1)}, u32[]{:S(2)}, u32[]{:S(2)}) %collective-permute-start.57) | collective-permute-done | bytes 1048608 | tf_op jit(solution)/shard_map/share_grad_tokens/ppermute | solution.py:284
  507.1 19.3 %collective-permute-done.63 = f32[12,1024]{1,0:T(8,128)S(1)} collective-permute-done((f32[12,1024]{1,0:T(8,128)S(1)}, f32[12,1024]{1,0:T(8,128)S(1)}, u32[]{:S(2)}, u32[]{:S(2)}) %collective-permute-start.63) | collective-permute-done | bytes 49184 | tf_op jit(solution)/shard_map/sum_qkv/sum_small/ppermute | solution.py:281
  540.2 43.7 %collective-permute-done.67 = bf16[320,512]{1,0:T(8,128)(2,1)S(1)} collective-permute-done((bf16[320,512]{1,0:T(8,128)(2,1)S(1)}, bf16[320,512]{1,0:T(8,128)(2,1)S(1)}, u32[]{:S(2)}, u32[]{:S(2)}) %collective-permute-start.67) | collective-permute-done | bytes 327712 | tf_op jit(solution)/shard_map/sum_in/ppermute | solution.py:571
  592.0 9.2 %collective-permute-done.70 = bf16[192,512]{1,0:T(8,128)(2,1)S(1)} collective-permute-done((bf16[192,512]{1,0:T(8,128)(2,1)S(1)}, bf16[192,512]{1,0:T(8,128)(2,1)S(1)}, u32[]{:S(2)}, u32[]{:S(2)}) %collective-permute-start.70) | collective-permute-done | bytes 196640 | tf_op jit(solution)/shard_map/sum_qkv/ppermute | solution.py:571
  617.5 8.8 %collective-permute-done.74 = bf16[384,512]{1,0:T(8,128)(2,1)S(1)} collective-permute-done((bf16[384,512]{1,0:T(8,128)(2,1)S(1)}, bf16[384,512]{1,0:T(8,128)(2,1)S(1)}, u32[]{:S(2)}, u32[]{:S(2)}) %collective-permute-start.74) | collective-permute-done | bytes 393248 | tf_op jit(solution)/shard_map/join_qkv/ppermute | solution.py:281
  630.4 18.3 %collective-permute-done.78 = bf16[1152,512]{1,0:T(8,128)(2,1)} collective-permute-done((bf16[1152,512]{1,0:T(8,128)(2,1)}, bf16[1152,512]{1,0:T(8,128)(2,1)}, u32[]{:S(2)}, u32[]{:S(2)}) %collective-permute-start.78) | collective-permute-done | bytes 1179680 | tf_op jit(solution)/shard_map/join_out_in/ppermute | solution.py:281
  (611 shorter events, 264.2 us)
Async XLA Ops:
  94.6 25.7 %collective-permute-start.20 = (bf16[640,512]{1,0:T(8,128)(2,1)}, bf16[640,512]{1,0:T(8,128)(2,1)}, u32[]{:S(2)}, u32[]{:S(2)}) collective-permute-start(bf16[640,512]{1,0:T(8,128)(2,1)} %collective-permute-done.19.refs_4_), channel_id=1, source_target_pairs={{0,16},{16,0},{1,17},{17,1},{2,18},{18,2},{3,19},{19,3},{4,20},{20... | collective-permute-start | bytes 1966088 | tf_op jit(solution)/shard_map/get_in/ppermute | solution.py:281
  95.7 24.6 %collective-permute-start.21 = (bf16[640,512]{1,0:T(8,128)(2,1)}, bf16[640,512]{1,0:T(8,128)(2,1)}, u32[]{:S(2)}, u32[]{:S(2)}) collective-permute-start(bf16[640,512]{1,0:T(8,128)(2,1)} %collective-permute-done.19.refs_4_), channel_id=1, source_target_pairs={{0,1},{1,2},{2,3},{3,0},{4,5},{5,6},{6,7},{7,4},{8,9},{9,10},{10,1... | collective-permute-start | bytes 1966088 | tf_op jit(solution)/shard_map/get_in/ppermute | solution.py:284
  96.2 22.6 %collective-permute-start.12 = (bf16[512,384]{1,0:T(8,128)(2,1)}, bf16[512,384]{1,0:T(8,128)(2,1)S(1)}, u32[]{:S(2)}, u32[]{:S(2)}) collective-permute-start(bf16[512,384]{1,0:T(8,128)(2,1)} %get-tuple-element.253), channel_id=1, source_target_pairs={{0,8},{4,12},{8,0},{12,4},{1,9},{5,13},{9,1},{13,5},{2,10},{6,14},... | collective-permute-start | bytes 1179656 | tf_op jit(solution)/shard_map/to_sequences/ppermute | solution.py:281
  143.4 47.5 %collective-permute-start.27 = (bf16[2560,1024]{1,0:T(8,128)(2,1)}, bf16[2560,1024]{1,0:T(8,128)(2,1)S(1)}, u32[]{:S(2)}, u32[]{:S(2)}) collective-permute-start(bf16[2560,1024]{1,0:T(8,128)(2,1)} %place_in.1), channel_id=1, source_target_pairs={{0,4},{4,0},{8,12},{12,8},{1,5},{5,1},{9,13},{13,9},{2,6},{6,2},{1... | collective-permute-start | bytes 15728648 | tf_op jit(solution)/shard_map/get_in/ppermute | solution.py:281
  144.7 26.3 %collective-permute-start.28 = (bf16[512,512]{1,0:T(8,128)(2,1)S(1)}, bf16[512,512]{1,0:T(8,128)(2,1)S(1)}, u32[]{:S(2)}, u32[]{:S(2)}) collective-permute-start(bf16[512,512]{1,0:T(8,128)(2,1)S(1)} %pad_maximum_fusion.5.refs_0_), channel_id=1, source_target_pairs={{0,16},{16,0},{1,17},{17,1},{2,18},{18,2},{3,19},{19,3},{4,20},{20... | collective-permute-start | bytes 1572872 | tf_op jit(solution)/shard_map/get_out/ppermute | solution.py:281
  145.7 25.3 %collective-permute-start.29 = (bf16[512,512]{1,0:T(8,128)(2,1)S(1)}, bf16[512,512]{1,0:T(8,128)(2,1)S(1)}, u32[]{:S(2)}, u32[]{:S(2)}) collective-permute-start(bf16[512,512]{1,0:T(8,128)(2,1)S(1)} %pad_maximum_fusion.5.refs_0_), channel_id=1, source_target_pairs={{0,1},{1,2},{2,3},{3,0},{4,5},{5,6},{6,7},{7,4},{8,9},{9,10},{10,1... | collective-permute-start | bytes 1572872 | tf_op jit(solution)/shard_map/get_out/ppermute | solution.py:284
  252.1 27.1 %collective-permute-start.37 = (bf16[1,512,1024]{2,1,0:T(8,128)(2,1)S(1)}, bf16[1,512,1024]{2,1,0:T(8,128)(2,1)}, u32[]{:S(2)}, u32[]{:S(2)}) collective-permute-start(bf16[1,512,1024]{2,1,0:T(8,128)(2,1)S(1)} %get-tuple-element.239), channel_id=1, source_target_pairs={{0,1},{1,2},{2,3},{3,0},{4,5},{5,6},{6,7},{7,4},{8,9},{9,10},{10,1... | collective-permute-start | bytes 3145736 | tf_op jit(solution)/shard_map/share_output/ppermute | solution.py:284
  289.1 58.0 %collective-permute-start.42 = (bf16[2048,1024]{1,0:T(8,128)(2,1)}, bf16[2048,1024]{1,0:T(8,128)(2,1)}, u32[]{:S(2)}, u32[]{:S(2)}) collective-permute-start(bf16[2048,1024]{1,0:T(8,128)(2,1)} %convolution_convert_fusion.2), channel_id=1, source_target_pairs={{0,4},{4,0},{8,12},{12,8},{1,5},{5,1},{9,13},{13,9},{2,6},{6,2},{1... | collective-permute-start | bytes 12582920 | tf_op jit(solution)/shard_map/sum_in/ppermute | solution.py:281
  295.1 47.8 %collective-permute-start.41 = (bf16[2048,512]{1,0:T(8,128)(2,1)}, bf16[2048,512]{1,0:T(8,128)(2,1)S(1)}, u32[]{:S(2)}, u32[]{:S(2)}) collective-permute-start(bf16[2048,512]{1,0:T(8,128)(2,1)} %slice.505), channel_id=1, source_target_pairs={{0,16},{16,0},{1,17},{17,1},{2,18},{18,2},{3,19},{19,3},{4,20},{20... | collective-permute-start | bytes 6291464 | tf_op jit(solution)/shard_map/sum_out/ppermute | solution.py:281
  297.4 57.7 %collective-permute-start.38 = (bf16[512,256]{1,0:T(8,128)(2,1)S(1)}, bf16[512,256]{1,0:T(8,128)(2,1)}, u32[]{:S(2)}, u32[]{:S(2)}) collective-permute-start(bf16[512,256]{1,0:T(8,128)(2,1)S(1)} %get-tuple-element.299), channel_id=1, source_target_pairs={{0,4},{4,0},{8,12},{12,8},{1,5},{5,1},{9,13},{13,9},{2,6},{6,2},{1... | collective-permute-start | bytes 786440 | tf_op jit(solution)/shard_map/to_sequences_grad/ppermute | solution.py:281
  297.4 57.7 %collective-permute-start.44 = (bf16[1,512,1024]{2,1,0:T(8,128)(2,1)}, bf16[1,512,1024]{2,1,0:T(8,128)(2,1)}, u32[]{:S(2)}, u32[]{:S(2)}) collective-permute-start(bf16[1,512,1024]{2,1,0:T(8,128)(2,1)} %collective-permute-done.37), channel_id=1, source_target_pairs={{0,1},{1,2},{2,3},{3,0},{4,5},{5,6},{6,7},{7,4},{8,9},{9,10},{10,1... | collective-permute-start | bytes 3145736 | tf_op jit(solution)/shard_map/share_output/ppermute | solution.py:284
  309.6 45.5 %collective-permute-start.40 = (bf16[512,256]{1,0:T(8,128)(2,1)S(1)}, bf16[512,256]{1,0:T(8,128)(2,1)S(1)}, u32[]{:S(2)}, u32[]{:S(2)}) collective-permute-start(bf16[512,256]{1,0:T(8,128)(2,1)S(1)} %get-tuple-element.298), channel_id=1, source_target_pairs={{0,12},{4,8},{8,4},{12,0},{1,13},{5,9},{9,5},{13,1},{2,14},{6,10},... | collective-permute-start | bytes 786440 | tf_op jit(solution)/shard_map/to_sequences_grad/ppermute | solution.py:281
  355.1 65.9 %collective-permute-start.56 = (bf16[2560,512]{1,0:T(8,128)(2,1)}, bf16[2560,512]{1,0:T(8,128)(2,1)}, u32[]{:S(2)}, u32[]{:S(2)}) collective-permute-start(bf16[2560,512]{1,0:T(8,128)(2,1)} %get-tuple-element.171), channel_id=1, source_target_pairs={{0,16},{16,0},{1,17},{17,1},{2,18},{18,2},{3,19},{19,3},{4,20},{20... | collective-permute-start | bytes 7864328 | tf_op jit(solution)/shard_map/sum_in/ppermute | solution.py:281
  356.4 29.1 %collective-permute-start.45 = (bf16[1024,512]{1,0:T(8,128)(2,1)S(1)}, bf16[1024,512]{1,0:T(8,128)(2,1)S(1)}, u32[]{:S(2)}, u32[]{:S(2)}) collective-permute-start(bf16[1024,512]{1,0:T(8,128)(2,1)S(1)} %slice.507), channel_id=1, source_target_pairs={{0,8},{4,12},{8,0},{12,4},{1,9},{5,13},{9,1},{13,5},{2,10},{6,14},... | collective-permute-start | bytes 3145736 | tf_op jit(solution)/shard_map/sum_out/ppermute | solution.py:281
  358.0 27.8 %collective-permute-start.46 = (bf16[1,512,1024]{2,1,0:T(8,128)(2,1)}, bf16[1,512,1024]{2,1,0:T(8,128)(2,1)S(1)}, u32[]{:S(2)}, u32[]{:S(2)}) collective-permute-start(bf16[1,512,1024]{2,1,0:T(8,128)(2,1)} %collective-permute-done.44), channel_id=1, source_target_pairs={{0,1},{1,2},{2,3},{3,0},{4,5},{5,6},{6,7},{7,4},{8,9},{9,10},{10,1... | collective-permute-start | bytes 3145736 | tf_op jit(solution)/shard_map/share_output/ppermute | solution.py:284
  385.5 35.0 %collective-permute-start.47 = (bf16[512,384]{1,0:T(8,128)(2,1)}, bf16[512,384]{1,0:T(8,128)(2,1)S(1)}, u32[]{:S(2)}, u32[]{:S(2)}) collective-permute-start(bf16[512,384]{1,0:T(8,128)(2,1)} %bitcast.303), channel_id=1, source_target_pairs={{0,4},{4,0},{8,12},{12,8},{1,5},{5,1},{9,13},{13,9},{2,6},{6,2},{1... | collective-permute-start | bytes 1179656 | tf_op jit(solution)/shard_map/to_rows_grad/ppermute | solution.py:281
  385.9 32.2 %collective-permute-start.53 = (bf16[256,512]{1,0:T(8,128)(2,1)S(1)}, bf16[256,512]{1,0:T(8,128)(2,1)S(1)}, u32[]{:S(2)}, u32[]{:S(2)}) collective-permute-start(bf16[256,512]{1,0:T(8,128)(2,1)S(1)} %get-tuple-element.269), channel_id=1, source_target_pairs={{0,3},{1,0},{2,1},{3,2},{4,7},{5,4},{6,5},{7,6},{8,11},{9,8},{10,9... | collective-permute-start | bytes 786440 | tf_op jit(solution)/shard_map/sum_out/ppermute | solution.py:571
  389.7 29.0 %collective-permute-start.54 = (bf16[256,512]{1,0:T(8,128)(2,1)S(1)}, bf16[256,512]{1,0:T(8,128)(2,1)S(1)}, u32[]{:S(2)}, u32[]{:S(2)}) collective-permute-start(bf16[256,512]{1,0:T(8,128)(2,1)S(1)} %get-tuple-element.271), channel_id=1, source_target_pairs={{0,2},{1,3},{2,0},{3,1},{4,6},{5,7},{6,4},{7,5},{8,10},{9,11},{10,... | collective-permute-start | bytes 786440 | tf_op jit(solution)/shard_map/sum_out/ppermute | solution.py:571
  389.7 29.7 %collective-permute-start.55 = (bf16[256,512]{1,0:T(8,128)(2,1)S(1)}, bf16[256,512]{1,0:T(8,128)(2,1)S(1)}, u32[]{:S(2)}, u32[]{:S(2)}) collective-permute-start(bf16[256,512]{1,0:T(8,128)(2,1)S(1)} %get-tuple-element.270), channel_id=1, source_target_pairs={{0,1},{1,2},{2,3},{3,0},{4,5},{5,6},{6,7},{7,4},{8,9},{9,10},{10,1... | collective-permute-start | bytes 786440 | tf_op jit(solution)/shard_map/sum_out/ppermute | solution.py:571
  420.4 26.7 %collective-permute-start.50 = (bf16[512,384]{1,0:T(8,128)(2,1)}, bf16[512,384]{1,0:T(8,128)(2,1)S(1)}, u32[]{:S(2)}, u32[]{:S(2)}) collective-permute-start(bf16[512,384]{1,0:T(8,128)(2,1)} %bitcast.305), channel_id=1, source_target_pairs={{0,8},{4,12},{8,0},{12,4},{1,9},{5,13},{9,1},{13,5},{2,10},{6,14},... | collective-permute-start | bytes 1179656 | tf_op jit(solution)/shard_map/to_rows_grad/ppermute | solution.py:281
  421.0 32.5 %collective-permute-start.52 = (bf16[512,384]{1,0:T(8,128)(2,1)}, bf16[512,384]{1,0:T(8,128)(2,1)S(1)}, u32[]{:S(2)}, u32[]{:S(2)}) collective-permute-start(bf16[512,384]{1,0:T(8,128)(2,1)} %bitcast.304), channel_id=1, source_target_pairs={{0,12},{4,8},{8,4},{12,0},{1,13},{5,9},{9,5},{13,1},{2,14},{6,10},... | collective-permute-start | bytes 1179656 | tf_op jit(solution)/shard_map/to_rows_grad/ppermute | solution.py:281
  459.6 45.9 %collective-permute-start.64 = (bf16[1280,512]{1,0:T(8,128)(2,1)}, bf16[1280,512]{1,0:T(8,128)(2,1)}, u32[]{:S(2)}, u32[]{:S(2)}) collective-permute-start(bf16[1280,512]{1,0:T(8,128)(2,1)} %slice.535), channel_id=1, source_target_pairs={{0,8},{4,12},{8,0},{12,4},{1,9},{5,13},{9,1},{13,5},{2,10},{6,14},... | collective-permute-start | bytes 3932168 | tf_op jit(solution)/shard_map/sum_in/ppermute | solution.py:281
  475.2 27.9 %collective-permute-start.57 = (bf16[1,512,1024]{2,1,0:T(8,128)(2,1)}, bf16[1,512,1024]{2,1,0:T(8,128)(2,1)}, u32[]{:S(2)}, u32[]{:S(2)}) collective-permute-start(bf16[1,512,1024]{2,1,0:T(8,128)(2,1)} %get-tuple-element.231), channel_id=1, source_target_pairs={{0,1},{1,2},{2,3},{3,0},{4,5},{5,6},{6,7},{7,4},{8,9},{9,10},{10,1... | collective-permute-start | bytes 3145736 | tf_op jit(solution)/shard_map/share_grad_tokens/ppermute | solution.py:284
  483.9 42.5 %collective-permute-start.62 = (bf16[768,1024]{1,0:T(8,128)(2,1)}, bf16[768,1024]{1,0:T(8,128)(2,1)}, u32[]{:S(2)}, u32[]{:S(2)}) collective-permute-start(bf16[768,1024]{1,0:T(8,128)(2,1)} %slice.533), channel_id=1, source_target_pairs={{0,8},{4,12},{8,0},{12,4},{1,9},{5,13},{9,1},{13,5},{2,10},{6,14},... | collective-permute-start | bytes 4718600 | tf_op jit(solution)/shard_map/sum_qkv/ppermute | solution.py:281
  503.1 33.7 %collective-permute-start.58 = (bf16[1,512,1024]{2,1,0:T(8,128)(2,1)}, bf16[1,512,1024]{2,1,0:T(8,128)(2,1)S(1)}, u32[]{:S(2)}, u32[]{:S(2)}) collective-permute-start(bf16[1,512,1024]{2,1,0:T(8,128)(2,1)} %collective-permute-done.57), channel_id=1, source_target_pairs={{0,1},{1,2},{2,3},{3,0},{4,5},{5,6},{6,7},{7,4},{8,9},{9,10},{10,1... | collective-permute-start | bytes 3145736 | tf_op jit(solution)/shard_map/share_grad_tokens/ppermute | solution.py:284
  503.9 22.5 %collective-permute-start.63 = (f32[12,1024]{1,0:T(8,128)S(1)}, f32[12,1024]{1,0:T(8,128)S(1)}, u32[]{:S(2)}, u32[]{:S(2)}) collective-permute-start(f32[12,1024]{1,0:T(8,128)S(1)} %add.381), channel_id=1, source_target_pairs={{0,8},{4,12},{8,0},{12,4},{1,9},{5,13},{9,1},{13,5},{2,10},{6,14},... | collective-permute-start | bytes 147464 | tf_op jit(solution)/shard_map/sum_qkv/sum_small/ppermute | solution.py:281
  532.0 52.0 %collective-permute-start.65 = (bf16[768,512]{1,0:T(8,128)(2,1)S(1)}, bf16[768,512]{1,0:T(8,128)(2,1)S(1)}, u32[]{:S(2)}, u32[]{:S(2)}) collective-permute-start(bf16[768,512]{1,0:T(8,128)(2,1)S(1)} %slice.537), channel_id=1, source_target_pairs={{0,16},{16,0},{1,17},{17,1},{2,18},{18,2},{3,19},{19,3},{4,20},{20... | collective-permute-start | bytes 2359304 | tf_op jit(solution)/shard_map/sum_qkv/ppermute | solution.py:281
  533.1 50.8 %collective-permute-start.67 = (bf16[320,512]{1,0:T(8,128)(2,1)S(1)}, bf16[320,512]{1,0:T(8,128)(2,1)S(1)}, u32[]{:S(2)}, u32[]{:S(2)}) collective-permute-start(bf16[320,512]{1,0:T(8,128)(2,1)S(1)} %pad_maximum_fusion.8), channel_id=1, source_target_pairs={{0,2},{1,3},{2,0},{3,1},{4,6},{5,7},{6,4},{7,5},{8,10},{9,11},{10,... | collective-permute-start | bytes 983048 | tf_op jit(solution)/shard_map/sum_in/ppermute | solution.py:571
  533.7 50.2 %collective-permute-start.68 = (bf16[320,512]{1,0:T(8,128)(2,1)S(1)}, bf16[320,512]{1,0:T(8,128)(2,1)S(1)}, u32[]{:S(2)}, u32[]{:S(2)}) collective-permute-start(bf16[320,512]{1,0:T(8,128)(2,1)S(1)} %pad_maximum_fusion.9), channel_id=1, source_target_pairs={{0,1},{1,2},{2,3},{3,0},{4,5},{5,6},{6,7},{7,4},{8,9},{9,10},{10,1... | collective-permute-start | bytes 983048 | tf_op jit(solution)/shard_map/sum_in/ppermute | solution.py:571
  536.8 66.0 %collective-permute-start.59 = (bf16[1,512,1024]{2,1,0:T(8,128)(2,1)S(1)}, bf16[1,512,1024]{2,1,0:T(8,128)(2,1)S(1)}, u32[]{:S(2)}, u32[]{:S(2)}) collective-permute-start(bf16[1,512,1024]{2,1,0:T(8,128)(2,1)S(1)} %collective-permute-done.58), channel_id=1, source_target_pairs={{0,1},{1,2},{2,3},{3,0},{4,5},{5,6},{6,7},{7,4},{8,9},{9,10},{10,1... | collective-permute-start | bytes 3145736 | tf_op jit(solution)/shard_map/share_grad_tokens/ppermute | solution.py:284
  591.2 23.2 %collective-permute-start.77 = (bf16[576,512]{1,0:T(8,128)(2,1)S(1)}, bf16[576,512]{1,0:T(8,128)(2,1)S(1)}, u32[]{:S(2)}, u32[]{:S(2)}) collective-permute-start(bf16[576,512]{1,0:T(8,128)(2,1)S(1)} %constant_dynamic-update-slice_fusion.15), channel_id=1, source_target_pairs={{0,4},{4,0},{8,12},{12,8},{1,5},{5,1},{9,13},{13,9},{2,6},{6,2},{1... | collective-permute-start | bytes 1769480 | tf_op jit(solution)/shard_map/join_out_in/ppermute | solution.py:281
  615.4 33.3 %collective-permute-start.78 = (bf16[1152,512]{1,0:T(8,128)(2,1)}, bf16[1152,512]{1,0:T(8,128)(2,1)}, u32[]{:S(2)}, u32[]{:S(2)}) collective-permute-start(bf16[1152,512]{1,0:T(8,128)(2,1)} %pad_maximum_fusion.1), channel_id=1, source_target_pairs={{0,8},{4,12},{8,0},{12,4},{1,9},{5,13},{9,1},{13,5},{2,10},{6,14},... | collective-permute-start | bytes 3538952 | tf_op jit(solution)/shard_map/join_out_in/ppermute | solution.py:281
  (170 other events, 2146.8 us)
